TPU v7x, 32 devices: a whole 2x2x4 slice. The times are simulated.
32 devices in a mesh: ctx: 8 (over y, x, core), exp: 4 (over z).
Axes of the slice: x: 2, y: 2, z: 4, core: 2. Of those that a mesh axis runs over, the one named last changes fastest.
Arguments:
- mixer_input: bfloat16 [8192, 4096], P('ctx', 'exp'), may hold values from -6 to 6
- scale_exponent: int32 [64, 64], P('ctx', 'exp'), may hold values from -1 to 1
- step_size: float32 [64, 8192], P('exp', 'ctx'), may hold values from 0.25 to 1
- decay_log: float32 [64, 8192], P('exp', 'ctx'), may hold values from -1.2 to 0
- state_input: bfloat16 [8192, 128], P('ctx'), may hold values from -6 to 6
- state_output: bfloat16 [8192, 128], P('ctx'), may hold values from -0.5 to 0.5
- skip_gain: float32 [64], P('exp'), may hold values from 0.5 to 1.5
- gate_input: bfloat16 [8192, 4096], P('ctx', 'exp'), may hold values from -6 to 6
- norm_gain: float32 [4096], P('exp'), may hold values from 0.25 to 1.75
- up_weight: bfloat16 [4096, 3072], P('ctx', 'exp'), may hold values from -0.09375 to 0.09375
- down_weight: bfloat16 [3072, 4096], P('exp', 'ctx'), may hold values from -0.15625 to 0.15625
- expert_slot: int32 [8192], P('ctx'), may hold values from 0 to 256, as said below
- gate_prob: float32 [8192], P('ctx'), may hold values from 0.2 to 1
Outputs:
- layer_out: bfloat16 [8192, 4096], P('ctx', 'exp')
Inputs may be any that keep to these rules, and one draw needn't show every extreme that they name: `expert_slot`: within each aligned block of 1024 tokens, the tokens routed to the expert carry the distinct slots 0 to k - 1 for some k of at most 256, and all other tokens carry 256; in some block k equals 256.
All inputs are finite; a program needn't handle non-finite values.
Results may differ from a plain program's by a relative error of at most 0.0085.
Values may be sent and summed in bfloat16 or wider, within the bound.
No kernel may reach another device: no remote copies, remote signals or barrier semaphores. Data moves between devices by JAX's collectives and lax.ppermute only.
A program may use at most 128 MiB of HBM per device.

v0:
```python
import jax
import jax.numpy as jnp
from jax import lax
from jax.sharding import PartitionSpec as P

P_SIZE = 64
BLK = 128
CAP = 256


highest = lax.Precision.HIGHEST


def local_scan(x_in, step_size, decay_log, b_rows, c_rows):
    length, head_count, head_width = x_in.shape
    blocks = length // BLK
    x_blocks = x_in.reshape(blocks, BLK, head_count, head_width)
    b_blocks = b_rows.reshape(blocks, BLK, b_rows.shape[1])
    c_blocks = c_rows.reshape(blocks, BLK, c_rows.shape[1])
    step_blocks = step_size.reshape(head_count, blocks, BLK)
    cumulative = jnp.cumsum(decay_log.reshape(head_count, blocks, BLK), axis=2)
    scores = jnp.einsum("bin,bjn->bij", c_blocks, b_blocks, precision=highest)
    causal = jnp.arange(BLK)[:, None] >= jnp.arange(BLK)[None, :]
    spread = jnp.where(causal, cumulative[:, :, :, None] - cumulative[:, :, None, :], -jnp.inf)
    mixing = jnp.exp(spread) * scores[None] * step_blocks[:, :, None, :]
    inner_part = jnp.einsum("hbij,bjhp->bihp", mixing, x_blocks, precision=highest)
    tail_decay = jnp.exp(cumulative[:, :, -1:] - cumulative) * step_blocks
    block_state = jnp.einsum(
        "hbj,bjn,bjhp->bhnp", tail_decay, b_blocks, x_blocks, precision=highest
    )
    totals = cumulative[:, :, -1]

    def carry_on(running, block_items):
        block_total, block_end = block_items
        return (jnp.exp(block_total)[:, None, None] * running + block_end, running)

    running, entering = lax.scan(
        carry_on, jnp.zeros(block_state.shape[1:], jnp.float32), (totals.T, block_state)
    )
    carried = jnp.einsum(
        "bin,hbi,bhnp->bihp", c_blocks, jnp.exp(cumulative), entering, precision=highest
    )
    offsets = jnp.cumsum(totals, axis=1) - totals
    growth = jnp.exp(offsets[:, :, None] + cumulative)
    return (inner_part + carried, running, jnp.sum(totals, axis=1), c_blocks, growth)


def body(
    mixer_input,
    scale_exponent,
    step_size,
    decay_log,
    state_input,
    state_output,
    skip_gain,
    gate_input,
    norm_gain,
    up_weight,
    down_weight,
    expert_slot,
    gate_prob,
):
    length = mixer_input.shape[0]
    head_count = skip_gain.shape[0]
    blocks = length // BLK
    factor = jnp.exp2(scale_exponent.astype(jnp.float32))
    x_in = (
        mixer_input.astype(jnp.float32).reshape(blocks, BLK, head_count, P_SIZE)
        * factor[:, None, :, None]
    ).reshape(length, head_count, P_SIZE)
    b_rows = state_input.astype(jnp.float32)
    c_rows = state_output.astype(jnp.float32)
    local_out, end_state, total_log, c_blocks, growth = local_scan(
        x_in, step_size, decay_log, b_rows, c_rows
    )
    log_totals = lax.all_gather(total_log[None, :], "ctx", axis=0, tiled=True)
    before = jnp.cumsum(log_totals, axis=0) - log_totals
    position = lax.axis_index("ctx")
    own_prior = lax.dynamic_index_in_dim(before, position, 0, keepdims=False)
    shard_piece = lax.all_gather(
        end_state[None].astype(jnp.bfloat16), "ctx", axis=0, tiled=True
    ).astype(jnp.float32)
    row_count = shard_piece.shape[0]
    row_ids = jnp.arange(row_count, dtype=jnp.int32)
    decay_gap = jnp.minimum(own_prior[None, :] - before - log_totals, 0.0)
    weight = jnp.where((row_ids < position)[:, None], jnp.exp(decay_gap), 0.0)
    start_state = jnp.zeros_like(end_state) + jnp.einsum(
        "kh,khnp->hnp", weight, shard_piece, precision=highest
    )
    handed = jnp.einsum("bin,hbi,hnp->bihp", c_blocks, growth, start_state, precision=highest)
    mixer_out = (local_out + handed).reshape(length, head_count, P_SIZE) + skip_gain[
        None, :, None
    ] * x_in
    gated_out = mixer_out * jax.nn.silu(
        gate_input.astype(jnp.float32).reshape(length, head_count, P_SIZE)
    )
    inverse_rms = lax.rsqrt(jnp.mean(gated_out * gated_out, axis=2, keepdims=True) + 1e-05)
    normed = (
        (gated_out * inverse_rms * norm_gain.reshape(head_count, P_SIZE))
        .reshape(length, head_count * P_SIZE)
        .astype(jnp.bfloat16)
    )
    places = jnp.arange(CAP, dtype=jnp.int32)[:, None] == expert_slot[None, :]
    picker = places.astype(jnp.bfloat16)
    dispatched = jnp.dot(picker, normed, preferred_element_type=jnp.float32).astype(jnp.bfloat16)
    full_features = lax.all_gather(dispatched, "exp", axis=1, tiled=True)
    up_act = jnp.dot(
        full_features,
        lax.all_gather(up_weight, "ctx", axis=0, tiled=True),
        preferred_element_type=jnp.float32,
    )
    hidden = jax.nn.silu(up_act).astype(jnp.bfloat16)
    terms = jnp.dot(
        hidden,
        lax.all_gather(down_weight, "ctx", axis=1, tiled=True),
        preferred_element_type=jnp.float32,
    )
    own_sums = lax.psum_scatter(
        terms.astype(jnp.bfloat16), "exp", scatter_dimension=1, tiled=True
    ).astype(jnp.float32)
    selector = places.astype(jnp.float32)
    expert_tok = lax.dot_general(selector, own_sums, (((0,), (0,)), ((), ())), precision=highest)
    return (normed.astype(jnp.float32) + gate_prob[:, None] * expert_tok).astype(jnp.bfloat16)


def solution(mesh):
    in_specs = (
        P("ctx", "exp"),
        P("ctx", "exp"),
        P("exp", "ctx"),
        P("exp", "ctx"),
        P("ctx", None),
        P("ctx", None),
        P("exp"),
        P("ctx", "exp"),
        P("exp"),
        P("ctx", "exp"),
        P("exp", "ctx"),
        P("ctx"),
        P("ctx"),
    )
    out_specs = P("ctx", "exp")
    return jax.shard_map(body, mesh=mesh, in_specs=in_specs, out_specs=out_specs, check_vma=False)
```

profile of v0, /device:TPU:0, one launch (start us, length us, event | category | flops | bytes accessed | tf_op | source)
XLA Modules:
  0.0 375.8 jit_solution(6003521538814983370)
XLA Ops:
  6.5 0.9 copy.117
  7.4 4.5 %reduce_window_sum.33 = f32[16,8,128]{2,1,0:T(8,128)S(1)} reduce-window(f32[16,8,128]{2,1,0:T(8,128)S(1)} %bitcast.107, f32[]{:T(128)} %constant.28.clone.1), window={size=1x1x128 pad=0_0x0_0x127_0}, to_apply=%region_0.0 | reduce-window | flops 2080768 | bytes 131076 | tf_op jit(solution)/shard_map/jit(cumsum)/reduce_window_sum | solution.py:21
  12.4 0.3 slice_reduce_fusion
  12.9 0.9 copy.118
  13.9 0.7 multiply_exponential_fusion
  14.6 6.8 %reshape.91 = f32[8,128,16,64]{3,2,1,0:T(8,128)} reshape(bf16[1024,1024]{1,0:T(8,128)(2,1)} %param.15) | data formatting | bytes 6291456 | tf_op jit(solution)/shard_map/reshape | solution.py:68
  21.4 7.2 %copy.74 = f32[8,128,16,64]{1,3,2,0:T(8,128)} copy(f32[8,128,16,64]{3,2,1,0:T(8,128)} %reshape.91) | data formatting | bytes 8388608 | tf_op jit(solution)/shard_map/reshape | solution.py:68
  28.5 6.4 %fusion.20 = f32[8,16,128,64]{2,3,1,0:T(8,128)} fusion(bf16[8,128,128,1]{2,1,3,0:T(8,128)(2,1)S(1)} %bitcast.102, f32[8,128,16,64]{1,3,2,0:T(8,128)} %copy.74, f32[8,128,16]{1,2,0:T(8,128)S(1)} %copy.81, f32[8,16]{1,0:T(8,128)S(1)} %multiply_exponential_fusion), kind=kOutput, calls=%fused_computation.31 | convolution fusion | flops 1612709888 | bytes 8716800 | tf_op jit(solution)/shard_map/hbj,bjn,bjhp->bhnp/dot_general | solution.py:28
  35.0 21.8 %while.13 = (s32[]{:T(128)}, f32[16,128,64]{2,1,0:T(8,128)S(1)}, f32[8,16,128,64]{3,2,1,0:T(8,128)}, f32[8,16]{1,0:T(8,128)S(1)}, f32[8,16,128,64]{2,3,1,0:T(8,128)}, /*index=5*/s32[]{:T(128)}, s32[]{:T(128)}) while((s32[]{:T(128)}, f32[16,128,64]{2,1,0:T(8,128)S(1)}, f32[8,16,128,64]{3,2,1,0:T(8,128)}, f32[8,16]{1,0:T(8,128)S(1)}, ...), condition=%wide.region_2.3_spmd.clone, body=%wide.region_1.2_spmd.clone.sunk | while | flops 524291 | bytes 5243680 | solution.py:37
  35.0 1.0 bitcast_dynamic-update-slice_fusion.2
  36.0 1.1 constant_dynamic-slice_fusion.3
  37.1 0.3 copy.125
  37.4 0.2 bitcast_add_fusion.2
  37.7 1.1 bitcast_dynamic-update-slice_fusion.2
  38.8 1.1 constant_dynamic-slice_fusion.3
  39.8 0.3 copy.125
  40.2 0.2 bitcast_add_fusion.2
  40.4 1.1 bitcast_dynamic-update-slice_fusion.2
  41.5 1.1 constant_dynamic-slice_fusion.3
  42.6 0.3 copy.125
  43.1 1.1 bitcast_dynamic-update-slice_fusion.2
  44.2 1.1 constant_dynamic-slice_fusion.3
  45.3 0.3 copy.125
  45.8 1.0 bitcast_dynamic-update-slice_fusion.2
  46.9 1.1 constant_dynamic-slice_fusion.3
  48.0 0.3 copy.125
  48.5 1.1 bitcast_dynamic-update-slice_fusion.2
  49.6 1.1 constant_dynamic-slice_fusion.3
  50.7 0.3 copy.125
  51.3 1.1 bitcast_dynamic-update-slice_fusion.2
  52.4 1.1 constant_dynamic-slice_fusion.3
  53.4 0.3 copy.125
  54.0 1.1 bitcast_dynamic-update-slice_fusion.2
  55.1 1.1 constant_dynamic-slice_fusion.3
  56.2 0.3 copy.125
  56.5 0.2 bitcast_add_fusion.2
  56.8 0.9 copy.87
  57.8 0.6 dynamic-slice
  59.1 0.2 dynamic-update-slice
  59.4 15.6 %all-reduce = f32[128]{0:T(128)S(1)} all-reduce(f32[128]{0:T(128)S(1)} %dynamic-update-slice), channel_id=2, replica_groups=mesh['ctx'=8,'exp'=4] {'ctx'}, use_global_device_ids=true, to_apply=%add | all-reduce | flops 128 | bytes 1024
  75.1 6.8 %reshape.93 = f32[8,128,16,64]{3,2,1,0:T(8,128)} reshape(bf16[1024,1024]{1,0:T(8,128)(2,1)} %param.22) | data formatting | bytes 6291456 | tf_op jit(solution)/shard_map/reshape | solution.py:95
  81.9 7.2 %copy.94 = f32[8,128,16,64]{1,3,2,0:T(8,128)} copy(f32[8,128,16,64]{3,2,1,0:T(8,128)} %reshape.93) | data formatting | bytes 8388608 | tf_op jit(solution)/shard_map/reshape | solution.py:95
  89.2 2.5 mul.135
  91.6 5.4 %copy.90 = f32[1024,1024]{1,0:T(8,128)} copy(f32[1024,1024]{0,1:T(8,128)} %bitcast.99) | data formatting | bytes 8388608 | tf_op jit(solution)/shard_map/mul | solution.py:68
  97.3 0.3 fusion.34
  97.6 12.1 %fusion.35 = f32[8,16,64,128]{3,2,1,0:T(8,128)} fusion(f32[8,16,128,64]{3,2,1,0:T(8,128)} %get-tuple-element.33, bf16[8,128,128,1]{2,1,3,0:T(8,128)(2,1)S(1)} %bitcast.96), kind=kOutput, calls=%fused_computation.60 | convolution fusion | flops 1610612736 | bytes 8650752 | tf_op jit(solution)/shard_map/bin,hbi,bhnp->bihp/dot_general | solution.py:40
  109.8 18.0 %fusion.2 = f32[8,16,64,128]{3,2,1,0:T(8,128)} fusion(f32[16,8,128]{2,0,1:T(8,128)S(1)} %copy_bitcast_fusion.2, f32[8,128,128]{2,1,0:T(8,128)S(1)} %fusion.34, f32[16,8,128]{2,0,1:T(8,128)S(1)} %copy.75, pred[128,128]{1,0:T(8,128)(4,1)S(1)} %iota_compare_fusion.3, f32[8,128,16,64]{1,3,2,0:T(8,128)S(1)} %copy-done.2, f32[8,16]{1,0:T(8,128)S(1)} %multiply_exponential_fusion), kind=kOutput, calls=%fused_computation.6 | convolution fusion | flops 1620049920 | bytes 9060864 | tf_op jit(solution)/shard_map/hbij,bjhp->bihp/dot_general | solution.py:26
  127.7 2.1 multiply_reduce_fusion
  129.8 9.3 %multiply_reduce_fusion.1 = (f32[8,128,16]{1,2,0:T(8,128)S(1)}, f32[8,128,16,64]{1,3,2,0:T(8,128)}) fusion(f32[8,128,16,64]{1,3,2,0:T(8,128)} %copy.94, f32[8,128,16,64]{1,3,2,0:T(8,128)} %copy.74, f32[16]{0:T(128)S(1)} %copy-done.9, f32[8,16]{1,0:T(8,128)S(1)} %multiply_exponential_fusion, bf16[8,128,128,1]{2,1,3,0:T(8,128)(2,1)S(1)} %bitcast.97, ...), kind=kOutput, calls=%fused_computation.20 | convolution fusion | flops 1625276416 | bytes 21955136 | tf_op jit(solution)/shard_map/bin,hbi,hnp->bihp/dot_general | solution.py:90
  139.1 7.1 %copy.110 = f32[8,128,16,64]{3,2,1,0:T(8,128)} copy(f32[8,128,16,64]{1,3,2,0:T(8,128)} %get-tuple-element.89) | data formatting | bytes 8388608 | tf_op jit(solution)/shard_map/reshape | solution.py:91
  146.3 7.6 %reshape.92 = f32[1024,1024]{1,0:T(8,128)} reshape(f32[8,128,16,64]{3,2,1,0:T(8,128)} %copy.110) | data formatting | bytes 8388608 | tf_op jit(solution)/shard_map/reshape | solution.py:91
  153.9 2.5 mul.146
  156.4 5.5 %copy.96 = f32[1024,1024]{1,0:T(8,128)} copy(f32[1024,1024]{0,1:T(8,128)} %bitcast.100) | data formatting | bytes 8388608 | tf_op jit(solution)/shard_map/mul | solution.py:99
  161.9 6.6 %multiply_convert_fusion = bf16[1024,1024]{1,0:T(8,128)(2,1)S(1)} fusion(f32[1024,1024]{1,0:T(8,128)} %copy.96, f32[1024,1024]{1,0:T(8,128)} %reshape.92, f32[1024,1024]{1,0:T(8,128)} %copy.90, f32[1024]{0:T(1024)S(1)} %copy-done.8, f32[1024]{0:T(1024)S(1)} %mul.131, bf16[1024,1024]{1,0:T(8,128)(2,1)S(1)} %copy-done.3, bf16[1024,1024]{1,0:T(8,128)(2,1)} %param.15), kind=kLoop, calls=%fused_computation.19 | loop fusion | flops 13631488 | bytes 18882560 | tf_op jit(solution)/shard_map/convert_element_type | solution.py:101
  168.5 1.3 copy-done.4
  169.9 1.5 convolution_convert_fusion.1
  171.5 0.7 all-gather.11.cloned.1.call-update
  172.2 0.5 all-gather.9.cloned.1.call-update
  172.8 43.8 %all-gather.7.cloned.1.call-done = bf16[256,4096]{1,0:T(8,128)(2,1)} async-done(((bf16[256,1024]{1,0:T(8,128)(2,1)}), bf16[256,4096]{1,0:T(8,128)(2,1)}) %all-gather.7.cloned.1.call-update) | async-done | bytes 2097168 | tf_op jit(solution)/shard_map/all_gather | solution.py:106
  216.6 47.3 %all-gather.11.cloned.1.call-done = bf16[768,4096]{1,0:T(8,128)(2,1)} async-done(((bf16[768,512]{1,0:T(8,128)(2,1)}), bf16[768,4096]{1,0:T(8,128)(2,1)}) %all-gather.11.cloned.1.call-update) | async-done | bytes 6291472 | tf_op jit(solution)/shard_map/all_gather | solution.py:115
  263.9 47.2 %all-gather.9.cloned.1.call-done = bf16[4096,768]{1,0:T(8,128)(2,1)} async-done(((bf16[512,768]{1,0:T(8,128)(2,1)}), bf16[4096,768]{1,0:T(8,128)(2,1)}) %all-gather.9.cloned.1.call-update) | async-done | bytes 6291472 | tf_op jit(solution)/shard_map/all_gather | solution.py:109
  311.1 11.1 %convolution_convert_fusion = bf16[256,4096]{1,0:T(8,128)(2,1)} fusion(bf16[768,4096]{1,0:T(8,128)(2,1)} %all-gather.11.cloned.1.call-done, bf16[256,4096]{1,0:T(8,128)(2,1)} %all-gather.7.cloned.1.call-done, bf16[4096,768]{1,0:T(8,128)(2,1)} %all-gather.9.cloned.1.call-done), kind=kOutput, calls=%fused_computation.12 | convolution fusion | flops 3223257088 | bytes 16777216 | tf_op jit(solution)/shard_map/dot_general | solution.py:113
  322.2 43.8 %reduce-scatter.2.cloned.1.call-done = bf16[256,1024]{1,0:T(8,128)(2,1)} async-done(((bf16[256,4096]{1,0:T(8,128)(2,1)}), bf16[256,1024]{1,0:T(8,128)(2,1)}) %reduce-scatter.2.cloned.1.call-update) | async-done | bytes 524304 | tf_op jit(solution)/shard_map/reduce_scatter | solution.py:118
  366.0 3.3 add_convert_fusion
  (74 shorter events, 2.6 us)
Async XLA Ops:
  6.5 90.8 %copy-start = (bf16[1024,128]{1,0:T(8,128)(2,1)S(1)}, bf16[1024,128]{1,0:T(8,128)(2,1)}, u32[]{:S(2)}) copy-start(bf16[1024,128]{1,0:T(8,128)(2,1)} %param.20) | copy-start | bytes 786436
  6.5 121.2 %all-gather.13.cloned.1.call-start = ((), (), s32[]{:S(2)}) async-start(), calls=%async_computation.5 | async-start | bytes 2359296 | tf_op jit(solution)/shard_map/all_gather | solution.py:80
  21.4 7.2 %copy-start.6 = (bf16[1024,128]{1,0:T(8,128)(2,1)S(1)}, bf16[1024,128]{1,0:T(8,128)(2,1)}, u32[]{:S(2)}) copy-start(bf16[1024,128]{1,0:T(8,128)(2,1)} %param.19) | copy-start | bytes 786436
  35.0 22.9 %copy-start.12 = (u32[32]{0:T(128)S(1)}, u32[32]{0:T(128)}, u32[]{:S(2)}) copy-start(u32[32]{0:T(128)} %constant.54) | copy-start | bytes 388
  57.7 158.9 %all-gather.7.cloned.1.call-start = ((), (), s32[]{:S(2)}) async-start(), calls=%async_computation.1 | async-start | bytes 2621440 | tf_op jit(solution)/shard_map/all_gather | solution.py:106
  91.6 5.4 %copy-start.9 = (f32[16]{0:T(128)S(1)}, f32[16]{0:T(128)}, u32[]{:S(2)}) copy-start(f32[16]{0:T(128)} %param.21) | copy-start | bytes 196
  91.6 5.7 %copy-start.7 = (f32[16,1024]{1,0:T(8,128)S(1)}, f32[16,1024]{1,0:T(8,128)}, u32[]{:S(2)}) copy-start(f32[16,1024]{1,0:T(8,128)} %param.17) | copy-start | bytes 196612
  97.6 12.1 %copy-start.2 = (f32[8,128,16,64]{1,3,2,0:T(8,128)S(1)}, f32[8,128,16,64]{1,3,2,0:T(8,128)}, u32[]{:S(2)}) copy-start(f32[8,128,16,64]{1,3,2,0:T(8,128)} %copy.74) | copy-start | bytes 12582916
  156.4 5.5 %copy-start.3 = (bf16[1024,1024]{1,0:T(8,128)(2,1)S(1)}, bf16[1024,1024]{1,0:T(8,128)(2,1)}, u32[]{:S(2)}) copy-start(bf16[1024,1024]{1,0:T(8,128)(2,1)} %param.22) | copy-start | bytes 6291460
  156.4 5.5 %copy-start.8 = (f32[1024]{0:T(1024)S(1)}, f32[1024]{0:T(1024)}, u32[]{:S(2)}) copy-start(f32[1024]{0:T(1024)} %param.23) | copy-start | bytes 12292
  161.9 7.9 %copy-start.10 = (s32[1024]{0:T(1024)S(1)}, s32[1024]{0:T(1024)}, u32[]{:S(2)}) copy-start(s32[1024]{0:T(1024)} %param.26) | copy-start | bytes 12292
  168.5 1.3 copy-start.4
  171.4 92.5 %all-gather.11.cloned.1.call-start = ((), (), s32[]{:S(2)}) async-start(), calls=%async_computation.3 | async-start | bytes 7077888 | tf_op jit(solution)/shard_map/all_gather | solution.py:115
  172.2 138.9 %all-gather.9.cloned.1.call-start = ((), (), s32[]{:S(2)}) async-start(), calls=%async_computation.2 | async-start | bytes 7077888 | tf_op jit(solution)/shard_map/all_gather | solution.py:109
  172.7 193.2 %copy-start.5 = (bf16[1024,1024]{1,0:T(8,128)(2,1)S(1)}, bf16[1024,1024]{1,0:T(8,128)(2,1)}, u32[]{:S(2)}) copy-start(bf16[1024,1024]{1,0:T(8,128)(2,1)} %copy-done.4) | copy-start | bytes 6291460
  172.8 193.2 %copy-start.11 = (f32[1024]{0:T(1024)S(1)}, f32[1024]{0:T(1024)}, u32[]{:S(2)}) copy-start(f32[1024]{0:T(1024)} %param.27) | copy-start | bytes 12292
  172.8 193.2 %reduce-scatter.2.cloned.1.call-start = ((), (), s32[]{:S(2)}) async-start(), calls=%async_computation.4 | async-start | bytes 2621440 | tf_op jit(solution)/shard_map/reduce_scatter | solution.py:118
  311.1 58.2 %copy-start.1 = (bf16[1024,128]{1,0:T(8,128)(2,1)S(1)}, bf16[1024,128]{1,0:T(8,128)(2,1)}, u32[]{:S(2)}) copy-start(bf16[1024,128]{1,0:T(8,128)(2,1)} %param.20) | copy-start | bytes 786436
Sparse Core Ops, SparseCore 0:
  57.8 30.5 all-gather.12
  171.5 45.0 all-gather.6
  218.5 45.3 all-gather.10
  265.6 45.3 all-gather.8
  322.3 43.6 reduce-scatter.1
where the time goes:
time: 377 us; the launch traced here: 376 us
  waiting for transfers between devices  183 us (49%)
  local copies, waits for them, and re-layouts  75.8 us (20%)
  matrix products  62 us (16%)
  other arithmetic  24.6 us (7%)
  blocking collectives  15.6 us (4%)
  between operations  14 us (4%)
    all_gather x1, waiting for transfers between devices, body(): lax.all_gather(down_weight, 'ctx', axis=1, tiled=True)  47.3 us
    all_gather x1, waiting for transfers between devices, body(): lax.all_gather(up_weight, 'ctx', axis=0, tiled=True)  47.2 us
    all_gather x1, waiting for transfers between devices, body(): full_features = lax.all_gather(dispatched, 'exp', axis=1, tiled=True)  43.8 us
    reduce_scatter x1, waiting for transfers between devices, body(): lax.psum_scatter(terms.astype(jnp.bfloat16), 'exp', scatter_dimension=1,...  43.8 us
    dot_general x1, matrix products, local_scan(): jnp.einsum('hbij,bjhp->bihp', mixing, x_blocks, precision=highest)  18 us
    unnamed x1, blocking collectives  15.6 us
    reshape x2, local copies, waits for them, and re-layouts, body(): (local_out + handed).reshape(length, head_count, P_SIZE)  14.8 us
    reshape x2, local copies, waits for them, and re-layouts, body(): gate_input.astype(jnp.float32).reshape(length, head_count, P_SIZE)  14 us
  transfers between devices with their start and end apart: 5, of which 4 were waited for; matrix products, arithmetic and copies ran while one was open for 14% of the time, Pallas kernels for 0%

commit v1 on v0

v1 whole, which is shorter than its diff:
```python
import functools

import jax
import jax.numpy as jnp
from jax import lax
from jax.experimental import pallas as pl
from jax.experimental.pallas import tpu as pltpu
from jax.sharding import PartitionSpec as P

CAP = 256
SUB = 64
F32 = jnp.float32
BF16 = jnp.bfloat16
HI = lax.Precision.HIGHEST
VMEM = 60 * 1024 * 1024


def iota(shape, dim):
    return lax.broadcasted_iota(jnp.int32, shape, dim)


def contract0(a, b):
    return lax.dot_general(a, b, (((0,), (0,)), ((), ())), preferred_element_type=F32)


def split2(v):
    high = v.astype(BF16)
    return jnp.concatenate([high, (v - high.astype(F32)).astype(BF16)], axis=0)


def spread_of(heads, chans):
    return iota((heads, chans), 1) // (chans // heads) == iota((heads, chans), 0)


def lanes_of(column, spread):
    return jnp.sum(jnp.where(spread, column, 0.0), axis=0, keepdims=True)


def scale_cols(sc_ref, start, count, blk):
    rows = sc_ref.shape[0]
    hot = iota((rows, count), 0) == (start + iota((rows, count), 1)) // blk
    return contract0(jnp.exp2(sc_ref[...].astype(F32)).astype(BF16), hot.astype(BF16))


def end_kernel(x_ref, b_ref, st_ref, dl_ref, sc_ref, msg_ref, hs, ds, *, blk):
    step = pl.program_id(0)
    span, chans = x_ref.shape
    heads = st_ref.shape[0]
    states = b_ref.shape[1]

    @pl.when(step == 0)
    def _():
        hs[...] = jnp.zeros_like(hs)
        ds[...] = jnp.ones_like(ds)

    later = (iota((span, span), 0) > iota((span, span), 1)).astype(F32)
    decay = dl_ref[...]
    tail = jnp.dot(decay, later, precision=HI, preferred_element_type=F32)
    w = jnp.exp(tail) * st_ref[...] * scale_cols(sc_ref, step * span, span, blk)
    spread = spread_of(heads, chans)
    hot = spread.astype(BF16)
    wide = contract0(split2(w), jnp.concatenate([hot, hot], axis=0))
    xw = (x_ref[...].astype(F32) * wide).astype(BF16)
    keep = lanes_of(jnp.exp(jnp.sum(decay, axis=1, keepdims=True)), spread)
    hs[...] = keep * hs[...] + contract0(b_ref[...], xw)
    ds[...] = keep * ds[...]

    @pl.when(step == pl.num_programs(0) - 1)
    def _():
        msg_ref[:states, :] = hs[...].astype(BF16)
        total = ds[...]
        high = total.astype(BF16)
        low = (total - high.astype(F32)).astype(BF16)
        msg_ref[states:, :] = jnp.concatenate([high, low], axis=0)


def local_kernel(x_ref, g_ref, b_ref, c_ref, st_ref, dl_ref, sc_ref, sk_ref, a_ref, w_ref, hs, gr, *, blk):
    step = pl.program_id(0)
    span, chans = x_ref.shape
    heads = st_ref.shape[0]

    @pl.when(step == 0)
    def _():
        hs[...] = jnp.zeros_like(hs)
        gr[...] = jnp.ones_like(gr)

    decay = dl_ref[...]
    row = iota((span, span), 0)
    col = iota((span, span), 1)
    same = row // SUB == col // SUB
    upto = jnp.where(row <= col, 1.0, 0.0) - jnp.where(row % SUB < SUB // 2, 1.0, 0.0)
    rel = jnp.dot(decay, jnp.where(same, upto, 0.0), precision=HI, preferred_element_type=F32)
    scale = scale_cols(sc_ref, step * span, span, blk)
    u = jnp.exp(rel)
    v = jnp.exp(-rel) * st_ref[...] * scale
    spread = spread_of(heads, chans)
    hot = spread.astype(BF16)
    hot2 = jnp.concatenate([hot, hot], axis=0)
    u_wide = contract0(split2(u), hot2)
    v_wide = contract0(split2(v), hot2)
    skip = lanes_of(sk_ref[...] * scale[:, :1], spread)
    x = x_ref[...].astype(F32)
    xv = (x * v_wide).astype(BF16)
    b = b_ref[...]
    c = c_ref[...]
    scores = lax.dot_general(c, b, (((1,), (1,)), ((), ())), preferred_element_type=F32)
    scores = jnp.where(same & (row >= col), scores, 0.0).astype(BF16)
    place = iota((heads, span), 1)
    g = g_ref[...].astype(F32)
    gate = g / (1.0 + jnp.exp(-g))
    for part in range(span // SUB):
        lo = part * SUB
        hi = lo + SUB
        first = (place >= lo) & (place < lo + SUB // 2)
        second = (place >= lo + SUB // 2) & (place < hi)
        head_in = lanes_of(jnp.exp(jnp.sum(jnp.where(first, decay, 0.0), axis=1, keepdims=True)), spread)
        head_out = lanes_of(jnp.exp(jnp.sum(jnp.where(second, decay, 0.0), axis=1, keepdims=True)), spread)
        mid = head_in * hs[...]
        lhs = jnp.concatenate([scores[lo:hi], c[lo:hi]], axis=1)
        rhs = jnp.concatenate([xv, mid.astype(BF16)], axis=0)
        acc = jnp.dot(lhs, rhs, preferred_element_type=F32)
        hs[...] = head_out * (mid + contract0(b[lo:hi], xv[lo:hi]))
        mid_growth = head_in * gr[0:1, :]
        gr[...] = jnp.broadcast_to(head_out * mid_growth, gr.shape)
        u_part = u_wide[lo:hi]
        a_ref[lo:hi, :] = (u_part * acc + skip * x[lo:hi]) * gate[lo:hi]
        w_ref[lo:hi, :] = (u_part * mid_growth * gate[lo:hi]).astype(BF16)


def norm_kernel(c_ref, a_ref, w_ref, h_ref, gain_ref, slot_ref, n_ref, d_ref, acc, *, width):
    step = pl.program_id(0)
    span, chans = a_ref.shape
    handed = jnp.dot(c_ref[...], h_ref[...], preferred_element_type=F32)
    t = a_ref[...] + w_ref[...].astype(F32) * handed
    square = (t * t).astype(BF16)
    group = min(256, chans)
    same = iota((group, group), 0) // width == iota((group, group), 1) // width
    mean_of = jnp.where(same, 1.0 / width, 0.0).astype(BF16)
    mean = jnp.concatenate(
        [
            jnp.dot(square[:, k : k + group], mean_of, preferred_element_type=F32)
            for k in range(0, chans, group)
        ],
        axis=1,
    )
    normed = (t * lax.rsqrt(mean + 1e-05) * gain_ref[...]).astype(BF16)
    n_ref[...] = normed
    pick = (iota((CAP, span), 0) == slot_ref[...]).astype(BF16)
    rows = jnp.dot(pick, normed, preferred_element_type=F32)

    @pl.when(step == 0)
    def _():
        acc[...] = rows

    @pl.when(step > 0)
    def _():
        acc[...] = acc[...] + rows

    @pl.when(step == pl.num_programs(0) - 1)
    def _():
        d_ref[...] = acc[...].astype(BF16)


def expert_kernel(pos_ref, *refs, ring, shards):
    own = refs[0]
    ups = refs[1:ring]
    downs = refs[ring : 2 * ring - 1]
    base = 2 * ring - 1
    u_hbm = refs[base : base + shards]
    d_hbm = refs[base + shards : base + 2 * shards]
    out = refs[base + 2 * shards]
    act, u_buf, d_buf, u_sem, d_sem = refs[base + 2 * shards + 1 :]
    z = pos_ref[0]
    c = pos_ref[1]
    chans = own.shape[1]
    u_copies = [pltpu.make_async_copy(u_hbm[k], u_buf.at[k], u_sem.at[k]) for k in range(shards)]
    d_copies = [pltpu.make_async_copy(d_hbm[k], d_buf.at[k], d_sem.at[k]) for k in range(shards)]
    for copy in u_copies + d_copies:
        copy.start()
    act[z] = own[...]
    for k in range(1, ring):
        act[lax.rem(z - k + ring, ring)] = ups[k - 1][...] + downs[ring - k - 1][...]
    feats = u_buf.shape[1]
    total = jnp.zeros((own.shape[0], u_buf.shape[2]), F32)
    for k in range(shards):
        u_copies[k].wait()
        first = jnp.bitwise_xor(c, k) * feats
        a = act[first // chans, :, pl.ds(pl.multiple_of(lax.rem(first, chans), 128), feats)]
        total = total + jnp.dot(a, u_buf[k], preferred_element_type=F32)
    hidden = (total / (1.0 + jnp.exp(-total))).astype(BF16)
    cols = d_buf.shape[2]
    for k in range(shards):
        d_copies[k].wait()
        first = jnp.bitwise_xor(c, k) * cols
        term = jnp.dot(hidden, d_buf[k], preferred_element_type=F32).astype(BF16)
        out[first // chans, :, pl.ds(pl.multiple_of(lax.rem(first, chans), 128), cols)] = term


def final_kernel(pos_ref, n_ref, slot_ref, prob_ref, own_ref, up_ref, down_ref, o_ref, sums):
    @pl.when(pl.program_id(0) == 0)
    def _():
        total = own_ref[0].astype(F32) + up_ref[...].astype(F32) + down_ref[...].astype(F32)
        sums[...] = split2(total)

    span = n_ref.shape[0]
    pick = (iota((span, 2 * CAP), 1) % CAP == slot_ref[...]).astype(BF16)
    token = jnp.dot(pick, sums[...], preferred_element_type=F32)
    o_ref[...] = (n_ref[...].astype(F32) + prob_ref[...] * token).astype(BF16)


def params():
    return pltpu.CompilerParams(vmem_limit_bytes=VMEM)


def rows_spec(span, cols):
    return pl.BlockSpec((span, cols), lambda i, *_: (i, 0))


def cols_spec(rows, span):
    return pl.BlockSpec((rows, span), lambda i, *_: (0, i))


def whole(shape):
    return pl.BlockSpec(shape, lambda i, *_: (0,) * len(shape))


def gather_pieces(value, axis, count, order):
    pieces = {0: value}
    for mask in order:
        pairs = [(i, i ^ mask) for i in range(count)]
        for key in list(pieces):
            pieces[key ^ mask] = lax.ppermute(pieces[key], axis, pairs)
    return [pieces[k] for k in range(count)]


def entering_state(message, states, axis, count):
    def parts(m):
        end = m[:states].astype(F32)
        keep = m[states : states + 1].astype(F32) + m[states + 8 : states + 9].astype(F32)
        return end, keep

    def pack(end, keep):
        high = keep.astype(BF16)
        low = (keep - high.astype(F32)).astype(BF16)
        rows = (8, keep.shape[1])
        return jnp.concatenate([end.astype(BF16), jnp.broadcast_to(high, rows), jnp.broadcast_to(low, rows)], axis=0)

    index = lax.axis_index(axis)
    end, keep = parts(message)
    prior = jnp.zeros_like(end)
    before = jnp.ones_like(keep)
    mask = 1
    while mask < count:
        got_end, got_keep = parts(lax.ppermute(message, axis, [(i, i ^ mask) for i in range(count)]))
        above = (index & mask) != 0
        prior = jnp.where(above, prior + before * got_end, prior)
        before = jnp.where(above, before * got_keep, before)
        mask *= 2
        if mask < count:
            end = jnp.where(above, keep * got_end + end, got_keep * end + got_end)
            keep = keep * got_keep
            message = pack(end, keep)
    return prior.astype(BF16)


def body(ctx, ring, mixer_input, scale_exponent, step_size, decay_log, state_input, state_output, skip_gain,
         gate_input, norm_gain, up_weight, down_weight, expert_slot, gate_prob):
    tokens, chans = mixer_input.shape
    heads = skip_gain.shape[0]
    states = state_input.shape[1]
    width = chans // heads
    blk = tokens // scale_exponent.shape[0]
    position = jnp.stack([lax.axis_index("exp"), lax.axis_index("ctx")]).astype(jnp.int32)

    span = 256
    message = pl.pallas_call(
        functools.partial(end_kernel, blk=blk),
        grid=(tokens // span,),
        in_specs=[rows_spec(span, chans), rows_spec(span, states), cols_spec(heads, span), cols_spec(heads, span),
                  whole(scale_exponent.shape)],
        out_specs=whole((states + 16, chans)),
        out_shape=jax.ShapeDtypeStruct((states + 16, chans), BF16),
        scratch_shapes=[pltpu.VMEM((states, chans), F32), pltpu.VMEM((8, chans), F32)],
        compiler_params=params(),
        name="end_state",
    )(mixer_input, state_input, step_size, decay_log, scale_exponent)

    start = entering_state(message, states, "ctx", ctx)

    local, weight = pl.pallas_call(
        functools.partial(local_kernel, blk=blk),
        grid=(tokens // blk,),
        in_specs=[rows_spec(blk, chans), rows_spec(blk, chans), rows_spec(blk, states), rows_spec(blk, states),
                  cols_spec(heads, blk), cols_spec(heads, blk), whole(scale_exponent.shape), whole((heads, 1))],
        out_specs=[rows_spec(blk, chans), rows_spec(blk, chans)],
        out_shape=[jax.ShapeDtypeStruct((tokens, chans), F32), jax.ShapeDtypeStruct((tokens, chans), BF16)],
        scratch_shapes=[pltpu.VMEM((states, chans), F32), pltpu.VMEM((8, chans), F32)],
        compiler_params=params(),
        name="local_out",
    )(mixer_input, gate_input, state_input, state_output, step_size, decay_log, scale_exponent,
      skip_gain[:, None])

    normed, dispatched = pl.pallas_call(
        functools.partial(norm_kernel, width=width),
        grid=(tokens // span,),
        in_specs=[rows_spec(span, states), rows_spec(span, chans), rows_spec(span, chans), whole((states, chans)),
                  whole((1, chans)), cols_spec(1, span)],
        out_specs=[rows_spec(span, chans), whole((CAP, chans))],
        out_shape=[jax.ShapeDtypeStruct((tokens, chans), BF16), jax.ShapeDtypeStruct((CAP, chans), BF16)],
        scratch_shapes=[pltpu.VMEM((CAP, chans), F32)],
        compiler_params=params(),
        name="norm_dispatch",
    )(state_output, local, weight, start, norm_gain[None], expert_slot[None])

    masks = []
    mask = 2
    while mask < ctx:
        masks.append(mask)
        mask *= 2
    ups = gather_pieces(up_weight, "ctx", ctx, masks + [1])
    downs = gather_pieces(down_weight, "ctx", ctx, masks[::-1] + [1])

    rise = [(i, i + 1) for i in range(ring - 1)]
    fall = [(i + 1, i) for i in range(ring - 1)]
    from_low = []
    from_high = []
    low = high = dispatched
    for _ in range(ring - 1):
        low = lax.ppermute(low, "exp", rise)
        high = lax.ppermute(high, "exp", fall)
        from_low.append(low)
        from_high.append(high)

    any_spec = pl.BlockSpec(memory_space=pl.ANY)
    terms = pl.pallas_call(
        functools.partial(expert_kernel, ring=ring, shards=ctx),
        grid_spec=pltpu.PrefetchScalarGridSpec(
            num_scalar_prefetch=1,
            grid=(1,),
            in_specs=[whole((CAP, chans))] * (2 * ring - 1) + [any_spec] * (2 * ctx),
            out_specs=whole((ring, CAP, chans)),
            scratch_shapes=[
                pltpu.VMEM((ring, CAP, chans), BF16),
                pltpu.VMEM((ctx,) + up_weight.shape, BF16),
                pltpu.VMEM((ctx,) + down_weight.shape, BF16),
                pltpu.SemaphoreType.DMA((ctx,)),
                pltpu.SemaphoreType.DMA((ctx,)),
            ],
        ),
        out_shape=jax.ShapeDtypeStruct((ring, CAP, chans), BF16),
        compiler_params=params(),
        name="expert",
    )(position, dispatched, *from_low, *from_high, *ups, *downs)

    z = position[0]
    up_sum = down_sum = None
    for turn in range(1, ring):
        far = lax.dynamic_index_in_dim(terms, (z + ring - turn) % ring, 0, keepdims=False)
        near = lax.dynamic_index_in_dim(terms, (z + turn) % ring, 0, keepdims=False)
        if turn > 1:
            far = (far.astype(F32) + up_sum.astype(F32)).astype(BF16)
            near = (near.astype(F32) + down_sum.astype(F32)).astype(BF16)
        up_sum = lax.ppermute(far, "exp", [(i, i + 1) for i in range(min(turn, ring - 1))])
        down_sum = lax.ppermute(near, "exp", [(i, i - 1) for i in range(max(ring - turn, 1), ring)])

    return pl.pallas_call(
        final_kernel,
        grid_spec=pltpu.PrefetchScalarGridSpec(
            num_scalar_prefetch=1,
            grid=(tokens // span,),
            in_specs=[rows_spec(span, chans), rows_spec(span, 1), rows_spec(span, 1),
                      pl.BlockSpec((1, CAP, chans), lambda i, pos: (pos[0], 0, 0)),
                      whole((CAP, chans)), whole((CAP, chans))],
            out_specs=rows_spec(span, chans),
            scratch_shapes=[pltpu.VMEM((2 * CAP, chans), BF16)],
        ),
        out_shape=jax.ShapeDtypeStruct((tokens, chans), BF16),
        compiler_params=params(),
        name="combine",
    )(position, normed, expert_slot[:, None], gate_prob[:, None], terms, up_sum, down_sum)


def solution(mesh):
    in_specs = (
        P("ctx", "exp"),
        P("ctx", "exp"),
        P("exp", "ctx"),
        P("exp", "ctx"),
        P("ctx", None),
        P("ctx", None),
        P("exp"),
        P("ctx", "exp"),
        P("exp"),
        P("ctx", "exp"),
        P("exp", "ctx"),
        P("ctx"),
        P("ctx"),
    )
    run = functools.partial(body, mesh.shape["ctx"], mesh.shape["exp"])
    return jax.shard_map(run, mesh=mesh, in_specs=in_specs, out_specs=P("ctx", "exp"), check_vma=False)
```

time: 377 us -> 217 us (0.58)
  waiting for transfers between devices: 183 us -> 90.8 us
  local copies, waits for them, and re-layouts: 75.8 us -> 6.27 us
  starting transfers between devices: 0.16 us -> 67.5 us
  matrix products: 62 us -> 0 us
  Pallas kernels: 0 us -> 43.3 us
  other arithmetic: 24.6 us -> 7.28 us
  blocking collectives: 15.6 us -> 0 us
  between operations: 14 us -> 0.43 us
    all_gather x4 -> x0, waiting for transfers between devices: 138 us -> none  [the longest x1 47.3 us: body(): lax.all_gather(down_weight, 'ctx', axis=1, tiled=True)]
    ppermute x0 -> x29, waiting for transfers between devices: none -> 90.8 us  [the longest x3 25 us: entering_state(): lax.ppermute(message, axis, [(i, i ^ mask) for i in range(count)])]
    ppermute x0 -> x29, starting transfers between devices: none -> 67.5 us  [the longest x3 34.7 us: body(): lax.ppermute(far, 'exp', [(i, i + 1) for i in range(min(turn, ring - 1))])]
    dot_general x8 -> x0, matrix products: 62 us -> none  [the longest x1 18 us: local_scan(): jnp.einsum('hbij,bjhp->bihp', mixing, x_blocks, precision=highest)]
    reduce_scatter x1 -> x0, waiting for transfers between devices: 43.8 us -> none  [body(): lax.psum_scatter(terms.astype(jnp.bfloat16), 'exp', scatter_dimension=1,...]
    pallas_call x0 -> x5, Pallas kernels: none -> 43.3 us  [the longest x1 12.7 us: body(): pl.pallas_call(functools.partial(expert_kernel, ring=ring, shards=ctx), g...]
    reshape x6 -> x0, local copies, waits for them, and re-layouts: 42.7 us -> none  [the longest x2 14.8 us: body(): (local_out + handed).reshape(length, head_count, P_SIZE)]
    mul x9 -> x0, local copies, waits for them, and re-layouts: 16.1 us -> none  [the longest x2 8 us: body(): gated_out * inverse_rms * norm_gain.reshape(head_count, P_SIZE)]
  transfers between devices with their start and end apart: 5 -> 29, of which waited for: 4 -> 13; matrix products, arithmetic and copies ran while one was open for 14% -> 3% of each run, Pallas kernels for 0% -> 9%
where the time goes in v1:
time: 217 us; the launch traced here: 216 us
  waiting for transfers between devices  90.8 us (42%)
  starting transfers between devices  67.5 us (31%)
  Pallas kernels  43.3 us (20%)
  other arithmetic  7.28 us (3%)
  local copies, waits for them, and re-layouts  6.27 us (3%)
    ppermute x3, starting transfers between devices, body(): lax.ppermute(far, 'exp', [(i, i + 1) for i in range(min(turn, ring - 1))])  34.7 us
    ppermute x3, waiting for transfers between devices, entering_state(): lax.ppermute(message, axis, [(i, i ^ mask) for i in range(count)])  25 us
    ppermute x3, waiting for transfers between devices, body(): low = lax.ppermute(low, 'exp', rise)  21.2 us
    ppermute x3, waiting for transfers between devices, body(): lax.ppermute(far, 'exp', [(i, i + 1) for i in range(min(turn, ring - 1))])  18.4 us
    ppermute x14, waiting for transfers between devices, gather_pieces(): pieces[key ^ mask] = lax.ppermute(pieces[key], axis, pairs)  17 us
    ppermute x3, starting transfers between devices, body(): low = lax.ppermute(low, 'exp', rise)  13.1 us
    pallas_call x1, Pallas kernels, body(): pl.pallas_call(functools.partial(expert_kernel, ring=ring, shards=ctx), g...  12.7 us
    pallas_call x1, Pallas kernels, body(): pl.pallas_call(functools.partial(local_kernel, blk=blk), grid=(tokens //...  11.5 us
  transfers between devices with their start and end apart: 29, of which 13 were waited for; matrix products, arithmetic and copies ran while one was open for 3% of the time, Pallas kernels for 9%

profile of v1, /device:TPU:0, one launch (start us, length us, event | category | flops | bytes accessed | tf_op | source)
XLA Modules:
  0.0 215.7 jit_solution(17887077106803051521)
XLA Ops:
  0.0 5.7 %end_state.1 = bf16[144,1024]{1,0:T(8,128)(2,1)} custom-call(bf16[1024,1024]{1,0:T(8,128)(2,1)} %x_ref.3, bf16[1024,128]{1,0:T(8,128)(2,1)} %b_ref.3, f32[16,1024]{1,0:T(8,128)} %st_ref.3, f32[16,1024]{1,0:T(8,128)} %dl_ref.3, s32[8,16]{1,0:T(8,128)} %sc_ref.3), custom_call_target="tpu_custom_call" | custom-call | tf_op jit(solution)/shard_map/end_state/pallas_call | solution.py:276
  5.7 0.5 collective-permute-start
  6.2 1.4 collective-permute-done
  7.7 0.8 convert_reduce_fusion.3
  8.4 1.1 fusion.7
  9.6 2.9 %collective-permute-start.1 = (bf16[144,1024]{1,0:T(8,128)(2,1)S(1)}, bf16[144,1024]{1,0:T(8,128)(2,1)S(1)}, u32[]{:S(2)}, u32[]{:S(2)}) collective-permute-start(bf16[144,1024]{1,0:T(8,128)(2,1)S(1)} %pad_maximum_fusion), channel_id=1, source_target_pairs={{0,8},{4,12},{8,0},{12,4},{16,24},{20,28},{24,16},{28,20},{1,9},{5... | collective-permute-start | bytes 884744 | tf_op jit(solution)/shard_map/ppermute | solution.py:254
  12.5 0.1 collective-permute-start.10
  12.6 2.0 collective-permute-start.12
  14.6 0.1 collective-permute-start.19
  14.6 5.7 %collective-permute-done.1 = bf16[144,1024]{1,0:T(8,128)(2,1)S(1)} collective-permute-done((bf16[144,1024]{1,0:T(8,128)(2,1)S(1)}, bf16[144,1024]{1,0:T(8,128)(2,1)S(1)}, u32[]{:S(2)}, u32[]{:S(2)}) %collective-permute-start.1) | collective-permute-done | bytes 294944 | tf_op jit(solution)/shard_map/ppermute | solution.py:254
  20.4 1.2 fusion.5
  21.6 2.1 collective-permute-start.2
  23.8 1.5 collective-permute-start.17
  25.2 12.0 %collective-permute-done.10.refs_9_ = bf16[512,768]{1,0:T(8,128)(2,1)S(1)} collective-permute-done((bf16[512,768]{1,0:T(8,128)(2,1)S(1)}, bf16[512,768]{1,0:T(8,128)(2,1)S(1)}, u32[]{:S(2)}, u32[]{:S(2)}) %collective-permute-start.10) | collective-permute-done | bytes 786464 | tf_op jit(solution)/shard_map/ppermute | solution.py:232
  37.2 17.8 %collective-permute-done.2 = bf16[144,1024]{1,0:T(8,128)(2,1)S(1)} collective-permute-done((bf16[144,1024]{1,0:T(8,128)(2,1)S(1)}, bf16[144,1024]{1,0:T(8,128)(2,1)S(1)}, u32[]{:S(2)}, u32[]{:S(2)}) %collective-permute-start.2) | collective-permute-done | bytes 294944 | tf_op jit(solution)/shard_map/ppermute | solution.py:254
  55.1 0.7 copy.15.sk_ref
  55.7 11.5 %local_out.1 = (f32[1024,1024]{1,0:T(8,128)}, bf16[1024,1024]{1,0:T(8,128)(2,1)}) custom-call(bf16[1024,1024]{1,0:T(8,128)(2,1)} %x_ref.3, bf16[1024,1024]{1,0:T(8,128)(2,1)} %g_ref.1, bf16[1024,128]{1,0:T(8,128)(2,1)} %b_ref.3, bf16[1024,128]{1,0:T(8,128)(2,1)} %c_ref.3, f32[16,1024]{1,0:T(8,128)} %st_ref.3, f32[16,1024]{1,0:T(8,128)} %dl_ref.3, ...), custom_call_target="tpu_custom_call" | custom-call | tf_op jit(solution)/shard_map/local_out/pallas_call | solution.py:290
  67.2 0.9 fusion.6.h_ref
  68.1 7.0 %norm_dispatch.1 = (bf16[1024,1024]{1,0:T(8,128)(2,1)}, bf16[256,1024]{1,0:T(8,128)(2,1)}) custom-call(bf16[1024,128]{1,0:T(8,128)(2,1)} %c_ref.3, f32[1024,1024]{1,0:T(8,128)} %get-tuple-element.9.a_ref, bf16[1024,1024]{1,0:T(8,128)(2,1)} %get-tuple-element.10.w_ref, bf16[128,1024]{1,0:T(8,128)(2,1)} %fusion.6.h_ref, f32[1,1024]{1,0:T(1,128)} %bitcast.35, ...), custom_call_target="tpu_custom_call" | custom-call | tf_op jit(solution)/shard_map/norm_dispatch/pallas_call | solution.py:303
  75.1 3.7 %collective-permute-start.3 = (bf16[256,1024]{1,0:T(8,128)(2,1)}, bf16[256,1024]{1,0:T(8,128)(2,1)S(1)}, u32[]{:S(2)}, u32[]{:S(2)}) collective-permute-start(bf16[256,1024]{1,0:T(8,128)(2,1)} %get-tuple-element.12.refs_0_), channel_id=1, source_target_pairs={{0,1},{1,2},{2,3},{4,5},{5,6},{6,7},{8,9},{9,10},{10,11},{12,13},{... | collective-permute-start | bytes 1572872 | tf_op jit(solution)/shard_map/ppermute | solution.py:329
  78.8 0.0 collective-permute-done.12.refs_11_
  78.8 1.3 collective-permute-start.6
  80.1 0.0 collective-permute-done.17.refs_17_
  80.1 1.6 collective-permute-start.14
  81.7 0.0 collective-permute-done.16.refs_16_
  81.7 1.5 collective-permute-start.21
  83.2 7.7 %collective-permute-done.3.refs_1_ = bf16[256,1024]{1,0:T(8,128)(2,1)S(1)} collective-permute-done((bf16[256,1024]{1,0:T(8,128)(2,1)}, bf16[256,1024]{1,0:T(8,128)(2,1)S(1)}, u32[]{:S(2)}, u32[]{:S(2)}) %collective-permute-start.3) | collective-permute-done | bytes 524320 | tf_op jit(solution)/shard_map/ppermute | solution.py:329
  90.9 4.0 %collective-permute-done.6.refs_4_ = bf16[256,1024]{1,0:T(8,128)(2,1)S(1)} collective-permute-done((bf16[256,1024]{1,0:T(8,128)(2,1)}, bf16[256,1024]{1,0:T(8,128)(2,1)S(1)}, u32[]{:S(2)}, u32[]{:S(2)}) %collective-permute-start.6) | collective-permute-done | bytes 524320 | tf_op jit(solution)/shard_map/ppermute | solution.py:330
  94.9 5.0 %collective-permute-done.14.refs_13_ = bf16[512,768]{1,0:T(8,128)(2,1)} collective-permute-done((bf16[512,768]{1,0:T(8,128)(2,1)S(1)}, bf16[512,768]{1,0:T(8,128)(2,1)}, u32[]{:S(2)}, u32[]{:S(2)}) %collective-permute-start.14) | collective-permute-done | bytes 786464 | tf_op jit(solution)/shard_map/ppermute | solution.py:232
  99.9 4.3 %collective-permute-start.4 = (bf16[256,1024]{1,0:T(8,128)(2,1)S(1)}, bf16[256,1024]{1,0:T(8,128)(2,1)S(1)}, u32[]{:S(2)}, u32[]{:S(2)}) collective-permute-start(bf16[256,1024]{1,0:T(8,128)(2,1)S(1)} %collective-permute-done.3.refs_1_), channel_id=1, source_target_pairs={{0,1},{1,2},{2,3},{4,5},{5,6},{6,7},{8,9},{9,10},{10,11},{12,13},{... | collective-permute-start | bytes 1572872 | tf_op jit(solution)/shard_map/ppermute | solution.py:329
  104.2 1.3 collective-permute-start.7
  105.5 0.0 copy-start.5
  105.6 0.1 collective-permute-start.18
  105.7 0.5 collective-permute-start.15
  106.1 0.5 copy-done.6
  106.7 0.9 copy-done.7
  107.6 0.4 collective-permute-start.22
  108.0 6.6 %collective-permute-done.4.refs_2_ = bf16[256,1024]{1,0:T(8,128)(2,1)S(1)} collective-permute-done((bf16[256,1024]{1,0:T(8,128)(2,1)S(1)}, bf16[256,1024]{1,0:T(8,128)(2,1)S(1)}, u32[]{:S(2)}, u32[]{:S(2)}) %collective-permute-start.4) | collective-permute-done | bytes 524320 | tf_op jit(solution)/shard_map/ppermute | solution.py:329
  114.6 5.2 %collective-permute-start.5 = (bf16[256,1024]{1,0:T(8,128)(2,1)S(1)}, bf16[256,1024]{1,0:T(8,128)(2,1)}, u32[]{:S(2)}, u32[]{:S(2)}) collective-permute-start(bf16[256,1024]{1,0:T(8,128)(2,1)S(1)} %collective-permute-done.4.refs_2_), channel_id=1, source_target_pairs={{0,1},{1,2},{2,3},{4,5},{5,6},{6,7},{8,9},{9,10},{10,11},{12,13},{... | collective-permute-start | bytes 1572872 | tf_op jit(solution)/shard_map/ppermute | solution.py:329
  119.8 1.3 collective-permute-start.8
  121.1 0.6 pad_add_fusion.pos_ref
  121.7 6.9 %collective-permute-done.5.refs_3_ = bf16[256,1024]{1,0:T(8,128)(2,1)} collective-permute-done((bf16[256,1024]{1,0:T(8,128)(2,1)S(1)}, bf16[256,1024]{1,0:T(8,128)(2,1)}, u32[]{:S(2)}, u32[]{:S(2)}) %collective-permute-start.5) | collective-permute-done | bytes 524320 | tf_op jit(solution)/shard_map/ppermute | solution.py:329
  128.6 5.2 %collective-permute-done.8.refs_6_ = bf16[256,1024]{1,0:T(8,128)(2,1)} collective-permute-done((bf16[256,1024]{1,0:T(8,128)(2,1)}, bf16[256,1024]{1,0:T(8,128)(2,1)}, u32[]{:S(2)}, u32[]{:S(2)}) %collective-permute-start.8) | collective-permute-done | bytes 524320 | tf_op jit(solution)/shard_map/ppermute | solution.py:330
  133.9 12.7 %expert.1.own_ref = bf16[4,256,1024]{2,1,0:T(8,128)(2,1)} custom-call(s32[2]{0:T(128)} %pad_add_fusion.pos_ref, bf16[256,1024]{1,0:T(8,128)(2,1)} %get-tuple-element.12.refs_0_, bf16[256,1024]{1,0:T(8,128)(2,1)} %copy-done.11, bf16[256,1024]{1,0:T(8,128)(2,1)} %copy-done.13, bf16[256,1024]{1,0:T(8,128)(2,1)} %collective-permute-done.5.refs_3_, ...), custom_call_target="tpu_custom_call" | custom-call | tf_op jit(solution)/shard_map/expert/pallas_call | solution.py:335
  146.6 1.2 dynamic-slice_bitcast_fusion.1
  147.8 0.7 collective-permute-start.26
  148.6 1.2 fusion.1
  149.8 0.7 collective-permute-start.27
  150.6 0.2 add_convert_fusion
  150.8 0.0 copy-start.14
  150.8 0.0 copy-start.15
  150.8 25.9 %collective-permute-start.23 = (bf16[256,1024]{1,0:T(8,128)(2,1)S(1)}, bf16[256,1024]{1,0:T(8,128)(2,1)S(1)}, u32[]{:S(2)}, u32[]{:S(2)}) collective-permute-start(bf16[256,1024]{1,0:T(8,128)(2,1)S(1)} %get-tuple-element.18), channel_id=1, source_target_pairs={{0,1},{4,5},{8,9},{12,13},{16,17},{20,21},{24,25},{28,29}} | collective-permute-start | bytes 1572872 | tf_op jit(solution)/shard_map/ppermute | solution.py:363
  176.7 7.5 %collective-permute-done.23 = bf16[256,1024]{1,0:T(8,128)(2,1)S(1)} collective-permute-done((bf16[256,1024]{1,0:T(8,128)(2,1)S(1)}, bf16[256,1024]{1,0:T(8,128)(2,1)S(1)}, u32[]{:S(2)}, u32[]{:S(2)}) %collective-permute-start.23) | collective-permute-done | bytes 524320 | tf_op jit(solution)/shard_map/ppermute | solution.py:363
  184.1 0.2 fusion
  184.3 4.4 %collective-permute-start.24 = (bf16[256,1024]{1,0:T(8,128)(2,1)S(1)}, bf16[256,1024]{1,0:T(8,128)(2,1)S(1)}, u32[]{:S(2)}, u32[]{:S(2)}) collective-permute-start(bf16[256,1024]{1,0:T(8,128)(2,1)S(1)} %fusion), channel_id=1, source_target_pairs={{0,1},{1,2},{4,5},{5,6},{8,9},{9,10},{12,13},{13,14},{16,17},{17,1... | collective-permute-start | bytes 1572872 | tf_op jit(solution)/shard_map/ppermute | solution.py:363
  188.8 1.3 collective-permute-start.28
  190.1 6.0 %collective-permute-done.24 = bf16[256,1024]{1,0:T(8,128)(2,1)S(1)} collective-permute-done((bf16[256,1024]{1,0:T(8,128)(2,1)S(1)}, bf16[256,1024]{1,0:T(8,128)(2,1)S(1)}, u32[]{:S(2)}, u32[]{:S(2)}) %collective-permute-start.24) | collective-permute-done | bytes 524320 | tf_op jit(solution)/shard_map/ppermute | solution.py:363
  196.1 1.0 add_convert_fusion.1
  197.1 4.4 %collective-permute-start.25 = (bf16[256,1024]{1,0:T(8,128)(2,1)}, bf16[256,1024]{1,0:T(8,128)(2,1)S(1)}, u32[]{:S(2)}, u32[]{:S(2)}) collective-permute-start(bf16[256,1024]{1,0:T(8,128)(2,1)} %add_convert_fusion.1), channel_id=1, source_target_pairs={{0,1},{1,2},{2,3},{4,5},{5,6},{6,7},{8,9},{9,10},{10,11},{12,13},{... | collective-permute-start | bytes 1572872 | tf_op jit(solution)/shard_map/ppermute | solution.py:363
  201.5 1.0 copy.16.slot_ref
  202.6 1.0 copy.17.prob_ref
  203.6 4.9 %collective-permute-done.25.up_ref = bf16[256,1024]{1,0:T(8,128)(2,1)S(1)} collective-permute-done((bf16[256,1024]{1,0:T(8,128)(2,1)}, bf16[256,1024]{1,0:T(8,128)(2,1)S(1)}, u32[]{:S(2)}, u32[]{:S(2)}) %collective-permute-start.25) | collective-permute-done | bytes 524320 | tf_op jit(solution)/shard_map/ppermute | solution.py:363
  208.5 0.8 copy-done.10
  209.3 6.4 %combine.1 = bf16[1024,1024]{1,0:T(8,128)(2,1)} custom-call(s32[2]{0:T(128)} %pad_add_fusion.pos_ref, bf16[1024,1024]{1,0:T(8,128)(2,1)} %get-tuple-element.11.n_ref, s32[1024,1]{1,0:T(8,128)} %copy.16.slot_ref, f32[1024,1]{1,0:T(8,128)} %copy.17.prob_ref, bf16[4,256,1024]{2,1,0:T(8,128)(2,1)} %expert.1.own_ref, bf16[256,1024]{1,0:T(8,128)(2,1)} %copy-done.10, ...), custom_call_target="tpu_custom_call" | custom-call | tf_op jit(solution)/shard_map/combine/pallas_call | solution.py:366
  (54 shorter events, 0.2 us)
Async XLA Ops:
  0.0 12.5 %copy-start.1 = (bf16[512,768]{1,0:T(8,128)(2,1)S(1)}, bf16[512,768]{1,0:T(8,128)(2,1)}, u32[]{:S(2)}) copy-start(bf16[512,768]{1,0:T(8,128)(2,1)} %refs_7_.1) | copy-start | bytes 2359300
  0.0 14.5 %copy-start.2 = (bf16[768,512]{1,0:T(8,128)(2,1)S(1)}, bf16[768,512]{1,0:T(8,128)(2,1)}, u32[]{:S(2)}) copy-start(bf16[768,512]{1,0:T(8,128)(2,1)} %refs_15_.1) | copy-start | bytes 2359300
  5.7 49.3 %copy-start.16 = (f32[16]{0:T(128)S(1)}, f32[16]{0:T(128)}, u32[]{:S(2)}) copy-start(f32[16]{0:T(128)} %param.19) | copy-start | bytes 196
  5.7 1.9 collective-permute-start
  9.6 10.8 %collective-permute-start.1 = (bf16[144,1024]{1,0:T(8,128)(2,1)S(1)}, bf16[144,1024]{1,0:T(8,128)(2,1)S(1)}, u32[]{:S(2)}, u32[]{:S(2)}) collective-permute-start(bf16[144,1024]{1,0:T(8,128)(2,1)S(1)} %pad_maximum_fusion), channel_id=1, source_target_pairs={{0,8},{4,12},{8,0},{12,4},{16,24},{20,28},{24,16},{28,20},{1,9},{5... | collective-permute-start | bytes 884744 | tf_op jit(solution)/shard_map/ppermute | solution.py:254
  12.5 24.7 %collective-permute-start.10 = (bf16[512,768]{1,0:T(8,128)(2,1)S(1)}, bf16[512,768]{1,0:T(8,128)(2,1)S(1)}, u32[]{:S(2)}, u32[]{:S(2)}) collective-permute-start(bf16[512,768]{1,0:T(8,128)(2,1)S(1)} %copy-done.1), channel_id=1, source_target_pairs={{0,8},{4,12},{8,0},{12,4},{16,24},{20,28},{24,16},{28,20},{1,9},{5... | collective-permute-start | bytes 2359304 | tf_op jit(solution)/shard_map/ppermute | solution.py:232
  12.6 66.2 %collective-permute-start.12 = (bf16[512,768]{1,0:T(8,128)(2,1)S(1)}, bf16[512,768]{1,0:T(8,128)(2,1)}, u32[]{:S(2)}, u32[]{:S(2)}) collective-permute-start(bf16[512,768]{1,0:T(8,128)(2,1)S(1)} %copy-done.1), channel_id=1, source_target_pairs={{0,16},{4,20},{8,24},{12,28},{16,0},{20,4},{24,8},{28,12},{1,17},{... | collective-permute-start | bytes 2359304 | tf_op jit(solution)/shard_map/ppermute | solution.py:232
  14.6 60.5 %collective-permute-start.19 = (bf16[768,512]{1,0:T(8,128)(2,1)S(1)}, bf16[768,512]{1,0:T(8,128)(2,1)}, u32[]{:S(2)}, u32[]{:S(2)}) collective-permute-start(bf16[768,512]{1,0:T(8,128)(2,1)S(1)} %copy-done.2), channel_id=1, source_target_pairs={{0,16},{4,20},{8,24},{12,28},{16,0},{20,4},{24,8},{28,12},{1,17},{... | collective-permute-start | bytes 2359304 | tf_op jit(solution)/shard_map/ppermute | solution.py:232
  21.6 33.4 %collective-permute-start.2 = (bf16[144,1024]{1,0:T(8,128)(2,1)S(1)}, bf16[144,1024]{1,0:T(8,128)(2,1)S(1)}, u32[]{:S(2)}, u32[]{:S(2)}) collective-permute-start(bf16[144,1024]{1,0:T(8,128)(2,1)S(1)} %pad_maximum_fusion.1), channel_id=1, source_target_pairs={{0,16},{4,20},{8,24},{12,28},{16,0},{20,4},{24,8},{28,12},{1,17},{... | collective-permute-start | bytes 884744 | tf_op jit(solution)/shard_map/ppermute | solution.py:254
  23.8 56.3 %collective-permute-start.17 = (bf16[768,512]{1,0:T(8,128)(2,1)S(1)}, bf16[768,512]{1,0:T(8,128)(2,1)}, u32[]{:S(2)}, u32[]{:S(2)}) collective-permute-start(bf16[768,512]{1,0:T(8,128)(2,1)S(1)} %copy-done.2), channel_id=1, source_target_pairs={{0,8},{4,12},{8,0},{12,4},{16,24},{20,28},{24,16},{28,20},{1,9},{5... | collective-permute-start | bytes 2359304 | tf_op jit(solution)/shard_map/ppermute | solution.py:232
  37.2 46.0 %copy-start.3 = (bf16[512,768]{1,0:T(8,128)(2,1)}, bf16[512,768]{1,0:T(8,128)(2,1)S(1)}, u32[]{:S(2)}) copy-start(bf16[512,768]{1,0:T(8,128)(2,1)S(1)} %collective-permute-done.10.refs_9_) | copy-start | bytes 2359300
  37.2 44.5 %collective-permute-start.16 = (bf16[768,512]{1,0:T(8,128)(2,1)S(1)}, bf16[768,512]{1,0:T(8,128)(2,1)}, u32[]{:S(2)}, u32[]{:S(2)}) collective-permute-start(bf16[768,512]{1,0:T(8,128)(2,1)S(1)} %copy-done.2), channel_id=1, source_target_pairs={{0,4},{4,0},{8,12},{12,8},{16,20},{20,16},{24,28},{28,24},{1,5},{5... | collective-permute-start | bytes 2359304 | tf_op jit(solution)/shard_map/ppermute | solution.py:232
  55.1 28.1 %collective-permute-start.9 = (bf16[512,768]{1,0:T(8,128)(2,1)S(1)}, bf16[512,768]{1,0:T(8,128)(2,1)}, u32[]{:S(2)}, u32[]{:S(2)}) collective-permute-start(bf16[512,768]{1,0:T(8,128)(2,1)S(1)} %copy-done.1), channel_id=1, source_target_pairs={{0,4},{4,0},{8,12},{12,8},{16,20},{20,16},{24,28},{28,24},{1,5},{5... | collective-permute-start | bytes 2359304 | tf_op jit(solution)/shard_map/ppermute | solution.py:232
  75.1 15.8 %collective-permute-start.3 = (bf16[256,1024]{1,0:T(8,128)(2,1)}, bf16[256,1024]{1,0:T(8,128)(2,1)S(1)}, u32[]{:S(2)}, u32[]{:S(2)}) collective-permute-start(bf16[256,1024]{1,0:T(8,128)(2,1)} %get-tuple-element.12.refs_0_), channel_id=1, source_target_pairs={{0,1},{1,2},{2,3},{4,5},{5,6},{6,7},{8,9},{9,10},{10,11},{12,13},{... | collective-permute-start | bytes 1572872 | tf_op jit(solution)/shard_map/ppermute | solution.py:329
  78.8 16.1 %collective-permute-start.6 = (bf16[256,1024]{1,0:T(8,128)(2,1)}, bf16[256,1024]{1,0:T(8,128)(2,1)S(1)}, u32[]{:S(2)}, u32[]{:S(2)}) collective-permute-start(bf16[256,1024]{1,0:T(8,128)(2,1)} %get-tuple-element.12.refs_0_), channel_id=1, source_target_pairs={{1,0},{2,1},{3,2},{5,4},{6,5},{7,6},{9,8},{10,9},{11,10},{13,12},{... | collective-permute-start | bytes 1572872 | tf_op jit(solution)/shard_map/ppermute | solution.py:330
  80.1 19.8 %collective-permute-start.14 = (bf16[512,768]{1,0:T(8,128)(2,1)S(1)}, bf16[512,768]{1,0:T(8,128)(2,1)}, u32[]{:S(2)}, u32[]{:S(2)}) collective-permute-start(bf16[512,768]{1,0:T(8,128)(2,1)S(1)} %collective-permute-done.10.refs_9_), channel_id=1, source_target_pairs={{0,16},{4,20},{8,24},{12,28},{16,0},{20,4},{24,8},{28,12},{1,17},{... | collective-permute-start | bytes 2359304 | tf_op jit(solution)/shard_map/ppermute | solution.py:232
  81.7 22.5 %collective-permute-start.21 = (bf16[768,512]{1,0:T(8,128)(2,1)}, bf16[768,512]{1,0:T(8,128)(2,1)S(1)}, u32[]{:S(2)}, u32[]{:S(2)}) collective-permute-start(bf16[768,512]{1,0:T(8,128)(2,1)} %collective-permute-done.19.refs_19_), channel_id=1, source_target_pairs={{0,8},{4,12},{8,0},{12,4},{16,24},{20,28},{24,16},{28,20},{1,9},{5... | collective-permute-start | bytes 2359304 | tf_op jit(solution)/shard_map/ppermute | solution.py:232
  83.2 22.4 %collective-permute-start.11 = (bf16[512,768]{1,0:T(8,128)(2,1)S(1)}, bf16[512,768]{1,0:T(8,128)(2,1)S(1)}, u32[]{:S(2)}, u32[]{:S(2)}) collective-permute-start(bf16[512,768]{1,0:T(8,128)(2,1)S(1)} %collective-permute-done.10.refs_9_), channel_id=1, source_target_pairs={{0,4},{4,0},{8,12},{12,8},{16,20},{20,16},{24,28},{28,24},{1,5},{5... | collective-permute-start | bytes 2359304 | tf_op jit(solution)/shard_map/ppermute | solution.py:232
  90.9 42.9 %copy-start.11 = (bf16[256,1024]{1,0:T(8,128)(2,1)}, bf16[256,1024]{1,0:T(8,128)(2,1)S(1)}, u32[]{:S(2)}) copy-start(bf16[256,1024]{1,0:T(8,128)(2,1)S(1)} %collective-permute-done.3.refs_1_) | copy-start | bytes 1572868
  90.9 14.8 %collective-permute-start.20 = (bf16[768,512]{1,0:T(8,128)(2,1)}, bf16[768,512]{1,0:T(8,128)(2,1)S(1)}, u32[]{:S(2)}, u32[]{:S(2)}) collective-permute-start(bf16[768,512]{1,0:T(8,128)(2,1)} %collective-permute-done.19.refs_19_), channel_id=1, source_target_pairs={{0,4},{4,0},{8,12},{12,8},{16,20},{20,16},{24,28},{28,24},{1,5},{5... | collective-permute-start | bytes 2359304 | tf_op jit(solution)/shard_map/ppermute | solution.py:232
  94.9 19.7 %copy-start.12 = (bf16[256,1024]{1,0:T(8,128)(2,1)}, bf16[256,1024]{1,0:T(8,128)(2,1)S(1)}, u32[]{:S(2)}) copy-start(bf16[256,1024]{1,0:T(8,128)(2,1)S(1)} %collective-permute-done.6.refs_4_) | copy-start | bytes 1572868
  94.9 11.7 %collective-permute-start.13 = (bf16[512,768]{1,0:T(8,128)(2,1)}, bf16[512,768]{1,0:T(8,128)(2,1)S(1)}, u32[]{:S(2)}, u32[]{:S(2)}) collective-permute-start(bf16[512,768]{1,0:T(8,128)(2,1)} %collective-permute-done.12.refs_11_), channel_id=1, source_target_pairs={{0,4},{4,0},{8,12},{12,8},{16,20},{20,16},{24,28},{28,24},{1,5},{5... | collective-permute-start | bytes 2359304 | tf_op jit(solution)/shard_map/ppermute | solution.py:232
  99.9 14.7 %collective-permute-start.4 = (bf16[256,1024]{1,0:T(8,128)(2,1)S(1)}, bf16[256,1024]{1,0:T(8,128)(2,1)S(1)}, u32[]{:S(2)}, u32[]{:S(2)}) collective-permute-start(bf16[256,1024]{1,0:T(8,128)(2,1)S(1)} %collective-permute-done.3.refs_1_), channel_id=1, source_target_pairs={{0,1},{1,2},{2,3},{4,5},{5,6},{6,7},{8,9},{9,10},{10,11},{12,13},{... | collective-permute-start | bytes 1572872 | tf_op jit(solution)/shard_map/ppermute | solution.py:329
  104.2 29.6 %copy-start.4 = (bf16[768,512]{1,0:T(8,128)(2,1)}, bf16[768,512]{1,0:T(8,128)(2,1)S(1)}, u32[]{:S(2)}) copy-start(bf16[768,512]{1,0:T(8,128)(2,1)S(1)} %collective-permute-done.21.refs_21_) | copy-start | bytes 2359300
  104.2 15.5 %collective-permute-start.7 = (bf16[256,1024]{1,0:T(8,128)(2,1)S(1)}, bf16[256,1024]{1,0:T(8,128)(2,1)}, u32[]{:S(2)}, u32[]{:S(2)}) collective-permute-start(bf16[256,1024]{1,0:T(8,128)(2,1)S(1)} %collective-permute-done.6.refs_4_), channel_id=1, source_target_pairs={{1,0},{2,1},{3,2},{5,4},{6,5},{7,6},{9,8},{10,9},{11,10},{13,12},{... | collective-permute-start | bytes 1572872 | tf_op jit(solution)/shard_map/ppermute | solution.py:330
  105.5 28.3 %copy-start.5 = (bf16[512,768]{1,0:T(8,128)(2,1)}, bf16[512,768]{1,0:T(8,128)(2,1)S(1)}, u32[]{:S(2)}) copy-start(bf16[512,768]{1,0:T(8,128)(2,1)S(1)} %collective-permute-done.11.refs_10_) | copy-start | bytes 2359300
  105.6 16.1 %collective-permute-start.18 = (bf16[768,512]{1,0:T(8,128)(2,1)}, bf16[768,512]{1,0:T(8,128)(2,1)S(1)}, u32[]{:S(2)}, u32[]{:S(2)}) collective-permute-start(bf16[768,512]{1,0:T(8,128)(2,1)} %collective-permute-done.17.refs_17_), channel_id=1, source_target_pairs={{0,4},{4,0},{8,12},{12,8},{16,20},{20,16},{24,28},{28,24},{1,5},{5... | collective-permute-start | bytes 2359304 | tf_op jit(solution)/shard_map/ppermute | solution.py:232
  105.6 1.0 copy-start.6
  105.7 16.0 %collective-permute-start.15 = (bf16[512,768]{1,0:T(8,128)(2,1)}, bf16[512,768]{1,0:T(8,128)(2,1)}, u32[]{:S(2)}, u32[]{:S(2)}) collective-permute-start(bf16[512,768]{1,0:T(8,128)(2,1)} %collective-permute-done.14.refs_13_), channel_id=1, source_target_pairs={{0,4},{4,0},{8,12},{12,8},{16,20},{20,16},{24,28},{28,24},{1,5},{5... | collective-permute-start | bytes 2359304 | tf_op jit(solution)/shard_map/ppermute | solution.py:232
  106.7 0.9 copy-start.7
  107.6 14.1 %collective-permute-start.22 = (bf16[768,512]{1,0:T(8,128)(2,1)S(1)}, bf16[768,512]{1,0:T(8,128)(2,1)}, u32[]{:S(2)}, u32[]{:S(2)}) collective-permute-start(bf16[768,512]{1,0:T(8,128)(2,1)S(1)} %collective-permute-done.21.refs_21_), channel_id=1, source_target_pairs={{0,4},{4,0},{8,12},{12,8},{16,20},{20,16},{24,28},{28,24},{1,5},{5... | collective-permute-start | bytes 2359304 | tf_op jit(solution)/shard_map/ppermute | solution.py:232
  114.6 19.3 %copy-start.13 = (bf16[256,1024]{1,0:T(8,128)(2,1)}, bf16[256,1024]{1,0:T(8,128)(2,1)S(1)}, u32[]{:S(2)}) copy-start(bf16[256,1024]{1,0:T(8,128)(2,1)S(1)} %collective-permute-done.4.refs_2_) | copy-start | bytes 1572868
  114.6 14.0 %collective-permute-start.5 = (bf16[256,1024]{1,0:T(8,128)(2,1)S(1)}, bf16[256,1024]{1,0:T(8,128)(2,1)}, u32[]{:S(2)}, u32[]{:S(2)}) collective-permute-start(bf16[256,1024]{1,0:T(8,128)(2,1)S(1)} %collective-permute-done.4.refs_2_), channel_id=1, source_target_pairs={{0,1},{1,2},{2,3},{4,5},{5,6},{6,7},{8,9},{9,10},{10,11},{12,13},{... | collective-permute-start | bytes 1572872 | tf_op jit(solution)/shard_map/ppermute | solution.py:329
  119.8 14.1 %collective-permute-start.8 = (bf16[256,1024]{1,0:T(8,128)(2,1)}, bf16[256,1024]{1,0:T(8,128)(2,1)}, u32[]{:S(2)}, u32[]{:S(2)}) collective-permute-start(bf16[256,1024]{1,0:T(8,128)(2,1)} %collective-permute-done.7.refs_5_), channel_id=1, source_target_pairs={{1,0},{2,1},{3,2},{5,4},{6,5},{7,6},{9,8},{10,9},{11,10},{13,12},{... | collective-permute-start | bytes 1572872 | tf_op jit(solution)/shard_map/ppermute | solution.py:330
  121.7 12.2 %copy-start.8 = (bf16[768,512]{1,0:T(8,128)(2,1)}, bf16[768,512]{1,0:T(8,128)(2,1)S(1)}, u32[]{:S(2)}) copy-start(bf16[768,512]{1,0:T(8,128)(2,1)S(1)} %collective-permute-done.18.refs_18_) | copy-start | bytes 2359300
  146.6 3.9 %copy-start = (bf16[4,256,1024]{2,1,0:T(8,128)(2,1)S(1)}, bf16[4,256,1024]{2,1,0:T(8,128)(2,1)}, u32[]{:S(2)}) copy-start(bf16[4,256,1024]{2,1,0:T(8,128)(2,1)} %expert.1.own_ref) | copy-start | bytes 6291460
  147.8 0.7 collective-permute-start.26
  149.8 0.7 collective-permute-start.27
  150.8 50.7 %copy-start.14 = (s32[1024]{0:T(1024)S(1)}, s32[1024]{0:T(1024)}, u32[]{:S(2)}) copy-start(s32[1024]{0:T(1024)} %param.24) | copy-start | bytes 12292
  150.8 51.8 %copy-start.15 = (f32[1024]{0:T(1024)S(1)}, f32[1024]{0:T(1024)}, u32[]{:S(2)}) copy-start(f32[1024]{0:T(1024)} %param.25) | copy-start | bytes 12292
  150.8 33.3 %collective-permute-start.23 = (bf16[256,1024]{1,0:T(8,128)(2,1)S(1)}, bf16[256,1024]{1,0:T(8,128)(2,1)S(1)}, u32[]{:S(2)}, u32[]{:S(2)}) collective-permute-start(bf16[256,1024]{1,0:T(8,128)(2,1)S(1)} %get-tuple-element.18), channel_id=1, source_target_pairs={{0,1},{4,5},{8,9},{12,13},{16,17},{20,21},{24,25},{28,29}} | collective-permute-start | bytes 1572872 | tf_op jit(solution)/shard_map/ppermute | solution.py:363
  184.3 11.8 %collective-permute-start.24 = (bf16[256,1024]{1,0:T(8,128)(2,1)S(1)}, bf16[256,1024]{1,0:T(8,128)(2,1)S(1)}, u32[]{:S(2)}, u32[]{:S(2)}) collective-permute-start(bf16[256,1024]{1,0:T(8,128)(2,1)S(1)} %fusion), channel_id=1, source_target_pairs={{0,1},{1,2},{4,5},{5,6},{8,9},{9,10},{12,13},{13,14},{16,17},{17,1... | collective-permute-start | bytes 1572872 | tf_op jit(solution)/shard_map/ppermute | solution.py:363
  188.8 14.8 %collective-permute-start.28 = (bf16[256,1024]{1,0:T(8,128)(2,1)S(1)}, bf16[256,1024]{1,0:T(8,128)(2,1)S(1)}, u32[]{:S(2)}, u32[]{:S(2)}) collective-permute-start(bf16[256,1024]{1,0:T(8,128)(2,1)S(1)} %get-tuple-element.17), channel_id=1, source_target_pairs={{1,0},{2,1},{3,2},{5,4},{6,5},{7,6},{9,8},{10,9},{11,10},{13,12},{... | collective-permute-start | bytes 1572872 | tf_op jit(solution)/shard_map/ppermute | solution.py:364
  197.1 11.4 %collective-permute-start.25 = (bf16[256,1024]{1,0:T(8,128)(2,1)}, bf16[256,1024]{1,0:T(8,128)(2,1)S(1)}, u32[]{:S(2)}, u32[]{:S(2)}) collective-permute-start(bf16[256,1024]{1,0:T(8,128)(2,1)} %add_convert_fusion.1), channel_id=1, source_target_pairs={{0,1},{1,2},{2,3},{4,5},{5,6},{6,7},{8,9},{9,10},{10,11},{12,13},{... | collective-permute-start | bytes 1572872 | tf_op jit(solution)/shard_map/ppermute | solution.py:363
  203.6 4.9 %copy-start.9 = (bf16[256,1024]{1,0:T(8,128)(2,1)}, bf16[256,1024]{1,0:T(8,128)(2,1)S(1)}, u32[]{:S(2)}) copy-start(bf16[256,1024]{1,0:T(8,128)(2,1)S(1)} %collective-permute-done.28.down_ref) | copy-start | bytes 1572868
  208.5 0.8 copy-start.10

commit v2 on v1

--- a/solution.py
+++ b/solution.py
@@ -6,6 +6,7 @@
 from jax.experimental import pallas as pl
 from jax.experimental.pallas import tpu as pltpu
 from jax.sharding import PartitionSpec as P
+
 
 CAP = 256
 SUB = 64
@@ -98,7 +99,7 @@
     hot2 = jnp.concatenate([hot, hot], axis=0)
     u_wide = contract0(split2(u), hot2)
     v_wide = contract0(split2(v), hot2)
-    skip = lanes_of(sk_ref[...] * scale[:, :1], spread)
+    skip = lanes_of(turned(sk_ref[...]) * scale[:, :1], spread)
     x = x_ref[...].astype(F32)
     xv = (x * v_wide).astype(BF16)
     b = b_ref[...]
@@ -127,7 +128,8 @@
         w_ref[lo:hi, :] = (u_part * mid_growth * gate[lo:hi]).astype(BF16)
 
 
-def norm_kernel(c_ref, a_ref, w_ref, h_ref, gain_ref, slot_ref, n_ref, d_ref, acc, *, width):
+def norm_kernel(c_ref, a_ref, w_ref, h_ref, gain_ref, slot_ref, n_ref, *outs, width):
+    d_refs, acc = outs[:-1], outs[-1]
     step = pl.program_id(0)
     span, chans = a_ref.shape
     handed = jnp.dot(c_ref[...], h_ref[...], preferred_element_type=F32)
@@ -158,34 +160,41 @@
 
     @pl.when(step == pl.num_programs(0) - 1)
     def _():
-        d_ref[...] = acc[...].astype(BF16)
-
-
-def expert_kernel(pos_ref, *refs, ring, shards):
-    own = refs[0]
-    ups = refs[1:ring]
-    downs = refs[ring : 2 * ring - 1]
-    base = 2 * ring - 1
-    u_hbm = refs[base : base + shards]
-    d_hbm = refs[base + shards : base + 2 * shards]
-    out = refs[base + 2 * shards]
-    act, u_buf, d_buf, u_sem, d_sem = refs[base + 2 * shards + 1 :]
-    z = pos_ref[0]
-    c = pos_ref[1]
-    chans = own.shape[1]
+        rows = CAP // len(d_refs)
+        for k, d_ref in enumerate(d_refs):
+            d_ref[...] = acc[k * rows : (k + 1) * rows, :].astype(BF16)
+
+
+def turned(row):
+    return jnp.broadcast_to(row, (8, row.shape[1])).T[:, :1]
+
+
+def expert_kernel(*refs, ring, shards, groups):
+    inputs = refs[: sum(groups)]
+    u_hbm = refs[sum(groups) : sum(groups) + shards]
+    d_hbm = refs[sum(groups) + shards : sum(groups) + 2 * shards]
+    outs = refs[sum(groups) + 2 * shards : sum(groups) + 2 * shards + ring]
+    act, terms, u_buf, d_buf, u_sem, d_sem = refs[sum(groups) + 2 * shards + ring :]
+    z = lax.axis_index("exp")
+    c = lax.axis_index("ctx")
+    rows, chans = inputs[0].shape
     u_copies = [pltpu.make_async_copy(u_hbm[k], u_buf.at[k], u_sem.at[k]) for k in range(shards)]
     d_copies = [pltpu.make_async_copy(d_hbm[k], d_buf.at[k], d_sem.at[k]) for k in range(shards)]
     for copy in u_copies + d_copies:
         copy.start()
-    act[z] = own[...]
-    for k in range(1, ring):
-        act[lax.rem(z - k + ring, ring)] = ups[k - 1][...] + downs[ring - k - 1][...]
+    at = 0
+    for k in range(ring):
+        piece = inputs[at][...]
+        for other in range(at + 1, at + groups[k]):
+            piece = piece + inputs[other][...]
+        act[k] = piece
+        at += groups[k]
     feats = u_buf.shape[1]
-    total = jnp.zeros((own.shape[0], u_buf.shape[2]), F32)
+    total = jnp.zeros((rows, u_buf.shape[2]), F32)
     for k in range(shards):
         u_copies[k].wait()
         first = jnp.bitwise_xor(c, k) * feats
-        a = act[first // chans, :, pl.ds(pl.multiple_of(lax.rem(first, chans), 128), feats)]
+        a = act[jnp.bitwise_xor(z, first // chans), :, pl.ds(pl.multiple_of(lax.rem(first, chans), 128), feats)]
         total = total + jnp.dot(a, u_buf[k], preferred_element_type=F32)
     hidden = (total / (1.0 + jnp.exp(-total))).astype(BF16)
     cols = d_buf.shape[2]
@@ -193,19 +202,33 @@
         d_copies[k].wait()
         first = jnp.bitwise_xor(c, k) * cols
         term = jnp.dot(hidden, d_buf[k], preferred_element_type=F32).astype(BF16)
-        out[first // chans, :, pl.ds(pl.multiple_of(lax.rem(first, chans), 128), cols)] = term
-
-
-def final_kernel(pos_ref, n_ref, slot_ref, prob_ref, own_ref, up_ref, down_ref, o_ref, sums):
+        terms[jnp.bitwise_xor(z, first // chans), :, pl.ds(pl.multiple_of(lax.rem(first, chans), 128), cols)] = term
+    for k in range(ring):
+        outs[k][...] = terms[k]
+
+
+def final_kernel(*refs, parts):
+    n_ref, slot_ref, prob_ref = refs[:3]
+    terms = refs[3:-2]
+    o_ref, sums = refs[-2:]
+
     @pl.when(pl.program_id(0) == 0)
     def _():
-        total = own_ref[0].astype(F32) + up_ref[...].astype(F32) + down_ref[...].astype(F32)
-        sums[...] = split2(total)
+        each = len(terms) // parts
+        rows = CAP // parts
+        for k in range(parts):
+            total = terms[k * each][...].astype(F32)
+            for other in range(k * each + 1, (k + 1) * each):
+                total = total + terms[other][...].astype(F32)
+            high = total.astype(BF16)
+            sums[k * rows : (k + 1) * rows, :] = high
+            sums[CAP + k * rows : CAP + (k + 1) * rows, :] = (total - high.astype(F32)).astype(BF16)
 
     span = n_ref.shape[0]
-    pick = (iota((span, 2 * CAP), 1) % CAP == slot_ref[...]).astype(BF16)
+    slot = turned(slot_ref[...].astype(F32)).astype(jnp.int32)
+    pick = (iota((span, 2 * CAP), 1) % CAP == slot).astype(BF16)
     token = jnp.dot(pick, sums[...], preferred_element_type=F32)
-    o_ref[...] = (n_ref[...].astype(F32) + prob_ref[...] * token).astype(BF16)
+    o_ref[...] = (n_ref[...].astype(F32) + turned(prob_ref[...]) * token).astype(BF16)
 
 
 def params():
@@ -224,13 +247,57 @@
     return pl.BlockSpec(shape, lambda i, *_: (0,) * len(shape))
 
 
+def swap(value, axis, count, mask):
+    return lax.ppermute(value, axis, [(i, i ^ mask) for i in range(count)])
+
+
 def gather_pieces(value, axis, count, order):
     pieces = {0: value}
-    for mask in order:
-        pairs = [(i, i ^ mask) for i in range(count)]
-        for key in list(pieces):
-            pieces[key ^ mask] = lax.ppermute(pieces[key], axis, pairs)
+    if count == 8:
+        far, near = order
+        pieces[far] = swap(value, axis, count, far)
+        pieces[near] = swap(value, axis, count, near)
+        pieces[6] = swap(pieces[far], axis, count, near)
+        for key in (0, far, near, 6):
+            pieces[key ^ 1] = swap(pieces[key], axis, count, 1)
+    else:
+        mask = 1
+        while mask < count:
+            for key in list(pieces):
+                pieces[key ^ mask] = swap(pieces[key], axis, count, mask)
+            mask *= 2
     return [pieces[k] for k in range(count)]
+
+
+ENDS = [(0, 1), (3, 2)]
+MIDDLE = [(1, 2), (2, 1)]
+OUTWARD = [(1, 0), (2, 3)]
+
+
+def gather_line(own, ring):
+    if ring != 4:
+        return [own] + [swap(own, "exp", ring, k) for k in range(1, ring)], [1] * ring
+    beside = swap(own, "exp", ring, 1)
+    cross = lax.ppermute(own, "exp", MIDDLE)
+    cross_far = lax.ppermute(beside, "exp", MIDDLE)
+    out_near = lax.ppermute(cross, "exp", OUTWARD)
+    out_far = lax.ppermute(cross_far, "exp", OUTWARD)
+    return [own, beside, cross_far, out_near, cross, out_far], [1, 1, 2, 2]
+
+
+def added(a, b):
+    return (a.astype(F32) + b.astype(F32)).astype(BF16)
+
+
+def sum_line(terms, ring):
+    if ring != 4:
+        return [terms[0]] + [swap(terms[k], "exp", ring, k) for k in range(1, ring)]
+    far = lax.ppermute(terms[3], "exp", ENDS)
+    near = lax.ppermute(terms[2], "exp", ENDS)
+    far = lax.ppermute(added(terms[2], far), "exp", MIDDLE)
+    near = lax.ppermute(added(terms[3], near), "exp", MIDDLE)
+    beside = swap(added(terms[1], far), "exp", ring, 1)
+    return [terms[0], near, beside]
 
 
 def entering_state(message, states, axis, count):
@@ -251,7 +318,7 @@
     before = jnp.ones_like(keep)
     mask = 1
     while mask < count:
-        got_end, got_keep = parts(lax.ppermute(message, axis, [(i, i ^ mask) for i in range(count)]))
+        got_end, got_keep = parts(swap(message, axis, count, mask))
         above = (index & mask) != 0
         prior = jnp.where(above, prior + before * got_end, prior)
         before = jnp.where(above, before * got_keep, before)
@@ -270,7 +337,8 @@
     states = state_input.shape[1]
     width = chans // heads
     blk = tokens // scale_exponent.shape[0]
-    position = jnp.stack([lax.axis_index("exp"), lax.axis_index("ctx")]).astype(jnp.int32)
+    parts = 2
+    rows = CAP // parts
 
     span = 256
     message = pl.pallas_call(
@@ -291,93 +359,63 @@
         functools.partial(local_kernel, blk=blk),
         grid=(tokens // blk,),
         in_specs=[rows_spec(blk, chans), rows_spec(blk, chans), rows_spec(blk, states), rows_spec(blk, states),
-                  cols_spec(heads, blk), cols_spec(heads, blk), whole(scale_exponent.shape), whole((heads, 1))],
+                  cols_spec(heads, blk), cols_spec(heads, blk), whole(scale_exponent.shape), whole((1, heads))],
         out_specs=[rows_spec(blk, chans), rows_spec(blk, chans)],
         out_shape=[jax.ShapeDtypeStruct((tokens, chans), F32), jax.ShapeDtypeStruct((tokens, chans), BF16)],
         scratch_shapes=[pltpu.VMEM((states, chans), F32), pltpu.VMEM((8, chans), F32)],
         compiler_params=params(),
         name="local_out",
     )(mixer_input, gate_input, state_input, state_output, step_size, decay_log, scale_exponent,
-      skip_gain[:, None])
-
-    normed, dispatched = pl.pallas_call(
+      skip_gain[None])
+
+    normed, *dispatched = pl.pallas_call(
         functools.partial(norm_kernel, width=width),
         grid=(tokens // span,),
         in_specs=[rows_spec(span, states), rows_spec(span, chans), rows_spec(span, chans), whole((states, chans)),
                   whole((1, chans)), cols_spec(1, span)],
-        out_specs=[rows_spec(span, chans), whole((CAP, chans))],
-        out_shape=[jax.ShapeDtypeStruct((tokens, chans), BF16), jax.ShapeDtypeStruct((CAP, chans), BF16)],
+        out_specs=[rows_spec(span, chans)] + [whole((rows, chans))] * parts,
+        out_shape=[jax.ShapeDtypeStruct((tokens, chans), BF16)] + [jax.ShapeDtypeStruct((rows, chans), BF16)] * parts,
         scratch_shapes=[pltpu.VMEM((CAP, chans), F32)],
         compiler_params=params(),
         name="norm_dispatch",
     )(state_output, local, weight, start, norm_gain[None], expert_slot[None])
 
-    masks = []
-    mask = 2
-    while mask < ctx:
-        masks.append(mask)
-        mask *= 2
-    ups = gather_pieces(up_weight, "ctx", ctx, masks + [1])
-    downs = gather_pieces(down_weight, "ctx", ctx, masks[::-1] + [1])
-
-    rise = [(i, i + 1) for i in range(ring - 1)]
-    fall = [(i + 1, i) for i in range(ring - 1)]
-    from_low = []
-    from_high = []
-    low = high = dispatched
-    for _ in range(ring - 1):
-        low = lax.ppermute(low, "exp", rise)
-        high = lax.ppermute(high, "exp", fall)
-        from_low.append(low)
-        from_high.append(high)
+    ups = gather_pieces(up_weight, "ctx", ctx, (2, 4))
+    downs = gather_pieces(down_weight, "ctx", ctx, (4, 2))
 
     any_spec = pl.BlockSpec(memory_space=pl.ANY)
-    terms = pl.pallas_call(
-        functools.partial(expert_kernel, ring=ring, shards=ctx),
-        grid_spec=pltpu.PrefetchScalarGridSpec(
-            num_scalar_prefetch=1,
+    summed = []
+    for part in range(parts):
+        pieces, groups = gather_line(dispatched[part], ring)
+        terms = pl.pallas_call(
+            functools.partial(expert_kernel, ring=ring, shards=ctx, groups=groups),
+            in_specs=[whole((rows, chans))] * len(pieces) + [any_spec] * (2 * ctx),
+            out_specs=[whole((rows, chans))] * ring,
             grid=(1,),
-            in_specs=[whole((CAP, chans))] * (2 * ring - 1) + [any_spec] * (2 * ctx),
-            out_specs=whole((ring, CAP, chans)),
             scratch_shapes=[
-                pltpu.VMEM((ring, CAP, chans), BF16),
+                pltpu.VMEM((ring, rows, chans), BF16),
+                pltpu.VMEM((ring, rows, chans), BF16),
                 pltpu.VMEM((ctx,) + up_weight.shape, BF16),
                 pltpu.VMEM((ctx,) + down_weight.shape, BF16),
                 pltpu.SemaphoreType.DMA((ctx,)),
                 pltpu.SemaphoreType.DMA((ctx,)),
             ],
-        ),
-        out_shape=jax.ShapeDtypeStruct((ring, CAP, chans), BF16),
-        compiler_params=params(),
-        name="expert",
-    )(position, dispatched, *from_low, *from_high, *ups, *downs)
-
-    z = position[0]
-    up_sum = down_sum = None
-    for turn in range(1, ring):
-        far = lax.dynamic_index_in_dim(terms, (z + ring - turn) % ring, 0, keepdims=False)
-        near = lax.dynamic_index_in_dim(terms, (z + turn) % ring, 0, keepdims=False)
-        if turn > 1:
-            far = (far.astype(F32) + up_sum.astype(F32)).astype(BF16)
-            near = (near.astype(F32) + down_sum.astype(F32)).astype(BF16)
-        up_sum = lax.ppermute(far, "exp", [(i, i + 1) for i in range(min(turn, ring - 1))])
-        down_sum = lax.ppermute(near, "exp", [(i, i - 1) for i in range(max(ring - turn, 1), ring)])
+            out_shape=[jax.ShapeDtypeStruct((rows, chans), BF16)] * ring,
+            compiler_params=params(),
+        )(*pieces, *ups, *downs)
+        summed += sum_line(terms, ring)
 
     return pl.pallas_call(
-        final_kernel,
-        grid_spec=pltpu.PrefetchScalarGridSpec(
-            num_scalar_prefetch=1,
-            grid=(tokens // span,),
-            in_specs=[rows_spec(span, chans), rows_spec(span, 1), rows_spec(span, 1),
-                      pl.BlockSpec((1, CAP, chans), lambda i, pos: (pos[0], 0, 0)),
-                      whole((CAP, chans)), whole((CAP, chans))],
-            out_specs=rows_spec(span, chans),
-            scratch_shapes=[pltpu.VMEM((2 * CAP, chans), BF16)],
-        ),
+        functools.partial(final_kernel, parts=parts),
+        grid=(tokens // span,),
+        in_specs=[rows_spec(span, chans), cols_spec(1, span), cols_spec(1, span)]
+        + [whole((rows, chans))] * len(summed),
+        out_specs=rows_spec(span, chans),
+        scratch_shapes=[pltpu.VMEM((2 * CAP, chans), BF16)],
         out_shape=jax.ShapeDtypeStruct((tokens, chans), BF16),
         compiler_params=params(),
         name="combine",
-    )(position, normed, expert_slot[:, None], gate_prob[:, None], terms, up_sum, down_sum)
+    )(normed, expert_slot[None], gate_prob[None], *summed)
 
 
 def solution(mesh):
@@ -396,5 +434,9 @@
         P("ctx"),
         P("ctx"),
     )
-    run = functools.partial(body, mesh.shape["ctx"], mesh.shape["exp"])
+    ctx, ring = mesh.shape["ctx"], mesh.shape["exp"]
+
+    def run(*arrays):
+        return body(ctx, ring, *arrays)
+
     return jax.shard_map(run, mesh=mesh, in_specs=in_specs, out_specs=P("ctx", "exp"), check_vma=False)

time: 217 us -> 161 us (0.74)
  waiting for transfers between devices: 90.8 us -> 52.7 us
  starting transfers between devices: 67.5 us -> 47.2 us
  Pallas kernels: 43.3 us -> 49.6 us
  local copies, waits for them, and re-layouts: 6.27 us -> 3.21 us
    ppermute x29 -> x37, waiting for transfers between devices: 90.8 us -> 52.7 us  [the longest x21 24.9 us: swap(): return lax.ppermute(value, axis, [(i, i ^ mask) for i in range(count)])]
    ppermute x29 -> x37, starting transfers between devices: 67.5 us -> 47.2 us  [the longest x21 31 us: swap(): return lax.ppermute(value, axis, [(i, i ^ mask) for i in range(count)])]
    pallas_call x2 -> x3, Pallas kernels: 19.1 us -> 25.2 us  [the longest x2 19.3 us: body(): pl.pallas_call(functools.partial(expert_kernel, ring=ring, shards=ctx, gr...]
    broadcast_in_dim x3 -> x0, local copies, waits for them, and re-layouts: 2.74 us -> none  [the longest x1 1.03 us: body(): expert_slot[:, None]]
  transfers between devices with their start and end apart: 29 -> 37, of which waited for: 13 -> 11; matrix products, arithmetic and copies ran while one was open for 3% -> 3% of each run, Pallas kernels for 9% -> 24%
where the time goes in v2:
time: 161 us; the launch traced here: 160 us
  waiting for transfers between devices  52.7 us (33%)
  Pallas kernels  49.6 us (31%)
  starting transfers between devices  47.2 us (29%)
  other arithmetic  7.12 us (4%)
  local copies, waits for them, and re-layouts  3.21 us (2%)
    ppermute x21, starting transfers between devices, swap(): return lax.ppermute(value, axis, [(i, i ^ mask) for i in range(count)])  31 us
    ppermute x21, waiting for transfers between devices, swap(): return lax.ppermute(value, axis, [(i, i ^ mask) for i in range(count)])  24.9 us
    pallas_call x2, Pallas kernels, body(): pl.pallas_call(functools.partial(expert_kernel, ring=ring, shards=ctx, gr...  19.3 us
    pallas_call x1, Pallas kernels, body(): pl.pallas_call(functools.partial(local_kernel, blk=blk), grid=(tokens //...  11.7 us
    ppermute x2, waiting for transfers between devices, gather_line(): out_far = lax.ppermute(cross_far, 'exp', OUTWARD)  10.1 us
    ppermute x2, waiting for transfers between devices, gather_line(): out_near = lax.ppermute(cross, 'exp', OUTWARD)  9.95 us
    ppermute x2, waiting for transfers between devices, sum_line(): far = lax.ppermute(terms[3], 'exp', ENDS)  7.77 us
    pallas_call x1, Pallas kernels, body(): pl.pallas_call(functools.partial(norm_kernel, width=width), grid=(tokens...  6.99 us
  transfers between devices with their start and end apart: 37, of which 11 were waited for; matrix products, arithmetic and copies ran while one was open for 3% of the time, Pallas kernels for 24%

profile of v2, /device:TPU:0, one launch (start us, length us, event | category | flops | bytes accessed | tf_op | source)
XLA Modules:
  0.0 160.4 jit_solution(2665420433215804517)
XLA Ops:
  0.0 5.7 %end_state.1 = bf16[144,1024]{1,0:T(8,128)(2,1)} custom-call(bf16[1024,1024]{1,0:T(8,128)(2,1)} %x_ref.3, bf16[1024,128]{1,0:T(8,128)(2,1)} %b_ref.3, f32[16,1024]{1,0:T(8,128)} %st_ref.3, f32[16,1024]{1,0:T(8,128)} %dl_ref.3, s32[8,16]{1,0:T(8,128)} %sc_ref.3), custom_call_target="tpu_custom_call" | custom-call | tf_op jit(solution)/shard_map/end_state/pallas_call | solution.py:344
  5.7 0.5 collective-permute-start
  6.2 1.4 collective-permute-done
  7.6 0.8 convert_reduce_fusion.3
  8.4 1.1 fusion.5
  9.5 0.7 pad_maximum_fusion
  10.2 2.8 %collective-permute-start.1 = (bf16[144,1024]{1,0:T(8,128)(2,1)}, bf16[144,1024]{1,0:T(8,128)(2,1)S(1)}, u32[]{:S(2)}, u32[]{:S(2)}) collective-permute-start(bf16[144,1024]{1,0:T(8,128)(2,1)} %pad_maximum_fusion), channel_id=1, source_target_pairs={{0,8},{4,12},{8,0},{12,4},{16,24},{20,28},{24,16},{28,20},{1,9},{5... | collective-permute-start | bytes 884744 | tf_op jit(solution)/shard_map/ppermute | solution.py:251
  13.1 7.5 %collective-permute-done.1 = bf16[144,1024]{1,0:T(8,128)(2,1)S(1)} collective-permute-done((bf16[144,1024]{1,0:T(8,128)(2,1)}, bf16[144,1024]{1,0:T(8,128)(2,1)S(1)}, u32[]{:S(2)}, u32[]{:S(2)}) %collective-permute-start.1) | collective-permute-done | bytes 294944 | tf_op jit(solution)/shard_map/ppermute | solution.py:251
  20.7 1.3 fusion.3
  22.0 1.8 %collective-permute-start.2 = (bf16[144,1024]{1,0:T(8,128)(2,1)S(1)}, bf16[144,1024]{1,0:T(8,128)(2,1)S(1)}, u32[]{:S(2)}, u32[]{:S(2)}) collective-permute-start(bf16[144,1024]{1,0:T(8,128)(2,1)S(1)} %pad_maximum_fusion.1), channel_id=1, source_target_pairs={{0,16},{4,20},{8,24},{12,28},{16,0},{20,4},{24,8},{28,12},{1,17},{... | collective-permute-start | bytes 884744 | tf_op jit(solution)/shard_map/ppermute | solution.py:251
  23.8 1.5 collective-permute-start.9
  25.3 0.5 collective-permute-start.11
  25.8 0.3 collective-permute-start.16
  26.2 5.7 %collective-permute-done.2 = bf16[144,1024]{1,0:T(8,128)(2,1)S(1)} collective-permute-done((bf16[144,1024]{1,0:T(8,128)(2,1)S(1)}, bf16[144,1024]{1,0:T(8,128)(2,1)S(1)}, u32[]{:S(2)}, u32[]{:S(2)}) %collective-permute-start.2) | collective-permute-done | bytes 294944 | tf_op jit(solution)/shard_map/ppermute | solution.py:251
  31.9 0.7 copy-done.29
  32.7 1.8 %collective-permute-start.18 = (bf16[768,512]{1,0:T(8,128)(2,1)S(1)}, bf16[768,512]{1,0:T(8,128)(2,1)}, u32[]{:S(2)}, u32[]{:S(2)}) collective-permute-start(bf16[768,512]{1,0:T(8,128)(2,1)S(1)} %copy-done.1), channel_id=1, source_target_pairs={{0,16},{4,20},{8,24},{12,28},{16,0},{20,4},{24,8},{28,12},{1,17},{... | collective-permute-start | bytes 2359304 | tf_op jit(solution)/shard_map/ppermute | solution.py:251
  34.5 11.7 %local_out.1 = (f32[1024,1024]{1,0:T(8,128)}, bf16[1024,1024]{1,0:T(8,128)(2,1)}) custom-call(bf16[1024,1024]{1,0:T(8,128)(2,1)} %x_ref.3, bf16[1024,1024]{1,0:T(8,128)(2,1)} %g_ref.1, bf16[1024,128]{1,0:T(8,128)(2,1)} %b_ref.3, bf16[1024,128]{1,0:T(8,128)(2,1)} %c_ref.3, f32[16,1024]{1,0:T(8,128)} %st_ref.3, f32[16,1024]{1,0:T(8,128)} %dl_ref.3, ...), custom_call_target="tpu_custom_call" | custom-call | tf_op jit(solution)/shard_map/local_out/pallas_call | solution.py:358
  46.2 1.8 %fusion.4.h_ref = bf16[128,1024]{1,0:T(8,128)(2,1)} fusion(bf16[144,1024]{1,0:T(8,128)(2,1)} %copy-done.29, f32[1024]{0:T(1024)S(1)} %bitcast.16, f32[1024]{0:T(1024)S(1)} %bitcast.17, pred[]{:T(512)S(6)} %ne.11, pred[]{:T(512)S(6)} %ne.10, pred[]{:T(512)S(6)} %ne.9, bf16[144,1024]{1,0:T(8,128)(2,1)S(1)} %copy-done.12, ...), kind=kLoop, calls=%fused_computation.14 | loop fusion | flops 1441792 | bytes 1056771 | tf_op jit(solution)/shard_map/convert_element_type | solution.py:330
  48.0 7.0 %norm_dispatch.1 = (bf16[1024,1024]{1,0:T(8,128)(2,1)}, bf16[128,1024]{1,0:T(8,128)(2,1)}, bf16[128,1024]{1,0:T(8,128)(2,1)}) custom-call(bf16[1024,128]{1,0:T(8,128)(2,1)} %c_ref.3, f32[1024,1024]{1,0:T(8,128)} %get-tuple-element.18.a_ref, bf16[1024,1024]{1,0:T(8,128)(2,1)} %get-tuple-element.19.w_ref, bf16[128,1024]{1,0:T(8,128)(2,1)} %fusion.4.h_ref, ...), custom_call_target="tpu_custom_call" | custom-call | tf_op jit(solution)/shard_map/norm_dispatch/pallas_call | solution.py:371
  55.0 0.0 copy-start.3
  55.0 1.6 %collective-permute-start.3 = (bf16[128,1024]{1,0:T(8,128)(2,1)}, bf16[128,1024]{1,0:T(8,128)(2,1)S(1)}, u32[]{:S(2)}, u32[]{:S(2)}) collective-permute-start(bf16[128,1024]{1,0:T(8,128)(2,1)} %get-tuple-element.21.refs_0_), channel_id=1, source_target_pairs={{0,1},{1,0},{2,3},{3,2},{4,5},{5,4},{6,7},{7,6},{8,9},{9,8},{10,11... | collective-permute-start | bytes 786440 | tf_op jit(solution)/shard_map/ppermute | solution.py:251
  56.7 0.7 collective-permute-start.5
  57.4 4.5 %collective-permute-start.27 = (bf16[128,1024]{1,0:T(8,128)(2,1)}, bf16[128,1024]{1,0:T(8,128)(2,1)S(1)}, u32[]{:S(2)}, u32[]{:S(2)}) collective-permute-start(bf16[128,1024]{1,0:T(8,128)(2,1)} %get-tuple-element.26.refs_0_), channel_id=1, source_target_pairs={{0,1},{1,0},{2,3},{3,2},{4,5},{5,4},{6,7},{7,6},{8,9},{9,8},{10,11... | collective-permute-start | bytes 786440 | tf_op jit(solution)/shard_map/ppermute | solution.py:251
  61.8 2.5 %collective-permute-done.18.refs_18_ = bf16[768,512]{1,0:T(8,128)(2,1)} collective-permute-done((bf16[768,512]{1,0:T(8,128)(2,1)S(1)}, bf16[768,512]{1,0:T(8,128)(2,1)}, u32[]{:S(2)}, u32[]{:S(2)}) %collective-permute-start.18) | collective-permute-done | bytes 786464 | tf_op jit(solution)/shard_map/ppermute | solution.py:251
  64.3 0.7 collective-permute-start.29
  65.0 1.6 collective-permute-start.13
  66.6 1.5 collective-permute-start.20
  68.1 0.7 collective-permute-start.4
  68.8 1.3 collective-permute-start.6
  70.1 0.7 collective-permute-start.28
  70.8 9.9 %collective-permute-done.6.refs_3_ = bf16[128,1024]{1,0:T(8,128)(2,1)} collective-permute-done((bf16[128,1024]{1,0:T(8,128)(2,1)S(1)}, bf16[128,1024]{1,0:T(8,128)(2,1)}, u32[]{:S(2)}, u32[]{:S(2)}) %collective-permute-start.6) | collective-permute-done | bytes 262176 | tf_op jit(solution)/shard_map/ppermute | solution.py:283
  80.8 0.5 collective-permute-start.17
  81.3 0.1 collective-permute-start.19
  81.4 1.9 %collective-permute-done.13.refs_12_ = bf16[512,768]{1,0:T(8,128)(2,1)S(1)} collective-permute-done((bf16[512,768]{1,0:T(8,128)(2,1)S(1)}, bf16[512,768]{1,0:T(8,128)(2,1)S(1)}, u32[]{:S(2)}, u32[]{:S(2)}) %collective-permute-start.13) | collective-permute-done | bytes 786464 | tf_op jit(solution)/shard_map/ppermute | solution.py:251
  83.3 1.1 collective-permute-done.20.refs_20_
  84.4 1.3 collective-permute-start.7
  85.7 1.3 collective-permute-start.30
  87.1 1.3 collective-permute-start.31
  88.4 10.1 %collective-permute-done.7.refs_5_ = bf16[128,1024]{1,0:T(8,128)(2,1)S(1)} collective-permute-done((bf16[128,1024]{1,0:T(8,128)(2,1)S(1)}, bf16[128,1024]{1,0:T(8,128)(2,1)S(1)}, u32[]{:S(2)}, u32[]{:S(2)}) %collective-permute-start.7) | collective-permute-done | bytes 262176 | tf_op jit(solution)/shard_map/ppermute | solution.py:284
  98.5 0.7 copy-done.19
  99.2 1.0 copy-done.10
  100.2 9.7 %shard_map.127 = (bf16[128,1024]{1,0:T(8,128)(2,1)}, bf16[128,1024]{1,0:T(8,128)(2,1)}, bf16[128,1024]{1,0:T(8,128)(2,1)}, bf16[128,1024]{1,0:T(8,128)(2,1)}) custom-call(bf16[128,1024]{1,0:T(8,128)(2,1)} %get-tuple-element.21.refs_0_, bf16[128,1024]{1,0:T(8,128)(2,1)} %copy-done.15, bf16[128,1024]{1,0:T(8,128)(2,1)} %copy-done.18, ...), custom_call_target="tpu_custom_call" | custom-call | tf_op jit(solution)/shard_map/pallas_call | solution.py:390
  109.9 1.5 collective-permute-start.22
  111.4 1.4 collective-permute-start.24
  112.8 9.6 %shard_map.128 = (bf16[128,1024]{1,0:T(8,128)(2,1)}, bf16[128,1024]{1,0:T(8,128)(2,1)}, bf16[128,1024]{1,0:T(8,128)(2,1)}, bf16[128,1024]{1,0:T(8,128)(2,1)}) custom-call(bf16[128,1024]{1,0:T(8,128)(2,1)} %get-tuple-element.26.refs_0_, bf16[128,1024]{1,0:T(8,128)(2,1)} %copy-done.13, bf16[128,1024]{1,0:T(8,128)(2,1)} %copy-done.17, ...), custom_call_target="tpu_custom_call" | custom-call | tf_op jit(solution)/shard_map/pallas_call | solution.py:390
  122.5 1.4 collective-permute-start.32
  123.9 1.3 collective-permute-start.34
  125.3 0.1 add_convert_fusion.5
  125.3 0.7 collective-permute-start.23
  126.1 0.1 add_convert_fusion.4
  126.1 0.7 collective-permute-start.25
  126.8 7.8 %collective-permute-done.34 = bf16[128,1024]{1,0:T(8,128)(2,1)S(1)} collective-permute-done((bf16[128,1024]{1,0:T(8,128)(2,1)}, bf16[128,1024]{1,0:T(8,128)(2,1)S(1)}, u32[]{:S(2)}, u32[]{:S(2)}) %collective-permute-start.34) | collective-permute-done | bytes 262176 | tf_op jit(solution)/shard_map/ppermute | solution.py:295
  134.6 1.0 add_convert_fusion.1
  135.6 0.7 collective-permute-start.35
  136.3 0.1 add_convert_fusion.2
  136.4 0.7 collective-permute-start.33
  137.1 0.1 add_convert_fusion.3
  137.2 6.9 %collective-permute-start.26 = (bf16[128,1024]{1,0:T(8,128)(2,1)S(1)}, bf16[128,1024]{1,0:T(8,128)(2,1)S(1)}, u32[]{:S(2)}, u32[]{:S(2)}) collective-permute-start(bf16[128,1024]{1,0:T(8,128)(2,1)S(1)} %add_convert_fusion.3), channel_id=1, source_target_pairs={{0,1},{1,0},{2,3},{3,2},{4,5},{5,4},{6,7},{7,6},{8,9},{9,8},{10,11... | collective-permute-start | bytes 786440 | tf_op jit(solution)/shard_map/ppermute | solution.py:251
  144.1 0.1 add_convert_fusion
  144.2 5.0 %collective-permute-start.36 = (bf16[128,1024]{1,0:T(8,128)(2,1)S(1)}, bf16[128,1024]{1,0:T(8,128)(2,1)S(1)}, u32[]{:S(2)}, u32[]{:S(2)}) collective-permute-start(bf16[128,1024]{1,0:T(8,128)(2,1)S(1)} %add_convert_fusion), channel_id=1, source_target_pairs={{0,1},{1,0},{2,3},{3,2},{4,5},{5,4},{6,7},{7,6},{8,9},{9,8},{10,11... | collective-permute-start | bytes 786440 | tf_op jit(solution)/shard_map/ppermute | solution.py:251
  149.2 1.8 %collective-permute-done.26.refs_5_ = bf16[128,1024]{1,0:T(8,128)(2,1)S(1)} collective-permute-done((bf16[128,1024]{1,0:T(8,128)(2,1)S(1)}, bf16[128,1024]{1,0:T(8,128)(2,1)S(1)}, u32[]{:S(2)}, u32[]{:S(2)}) %collective-permute-start.26) | collective-permute-done | bytes 262176 | tf_op jit(solution)/shard_map/ppermute | solution.py:251
  151.0 2.8 %collective-permute-done.36.refs_8_ = bf16[128,1024]{1,0:T(8,128)(2,1)S(1)} collective-permute-done((bf16[128,1024]{1,0:T(8,128)(2,1)S(1)}, bf16[128,1024]{1,0:T(8,128)(2,1)S(1)}, u32[]{:S(2)}, u32[]{:S(2)}) %collective-permute-start.36) | collective-permute-done | bytes 262176 | tf_op jit(solution)/shard_map/ppermute | solution.py:251
  153.8 0.7 copy-done.28
  154.5 5.9 %combine.1 = bf16[1024,1024]{1,0:T(8,128)(2,1)} custom-call(bf16[1024,1024]{1,0:T(8,128)(2,1)} %get-tuple-element.20.refs_0_, s32[1,1024]{1,0:T(1,128)} %bitcast.19, f32[1,1024]{1,0:T(1,128)} %bitcast.21, bf16[128,1024]{1,0:T(8,128)(2,1)} %get-tuple-element.22.refs_3_, bf16[128,1024]{1,0:T(8,128)(2,1)} %copy-done.22, bf16[128,1024]{1,0:T(8,128)(2,1)} %copy-done.27, ...), custom_call_target="tpu_custom_call" | custom-call | tf_op jit(solution)/shard_map/combine/pallas_call | solution.py:408
  (94 shorter events, 0.3 us)
Async XLA Ops:
  0.0 13.1 %copy-start = (bf16[512,768]{1,0:T(8,128)(2,1)S(1)}, bf16[512,768]{1,0:T(8,128)(2,1)}, u32[]{:S(2)}) copy-start(bf16[512,768]{1,0:T(8,128)(2,1)} %refs_6_.3) | copy-start | bytes 2359300
  5.7 20.1 %copy-start.1 = (bf16[768,512]{1,0:T(8,128)(2,1)S(1)}, bf16[768,512]{1,0:T(8,128)(2,1)}, u32[]{:S(2)}) copy-start(bf16[768,512]{1,0:T(8,128)(2,1)} %refs_14_.3) | copy-start | bytes 2359300
  5.7 1.9 %collective-permute-start = (bf16[144,1024]{1,0:T(8,128)(2,1)}, bf16[144,1024]{1,0:T(8,128)(2,1)S(1)}, u32[]{:S(2)}, u32[]{:S(2)}) collective-permute-start(bf16[144,1024]{1,0:T(8,128)(2,1)} %end_state.1), channel_id=1, source_target_pairs={{0,4},{4,0},{8,12},{12,8},{16,20},{20,16},{24,28},{28,24},{1,5},{5... | collective-permute-start | bytes 884744 | tf_op jit(solution)/shard_map/ppermute | solution.py:251
  10.2 10.4 %collective-permute-start.1 = (bf16[144,1024]{1,0:T(8,128)(2,1)}, bf16[144,1024]{1,0:T(8,128)(2,1)S(1)}, u32[]{:S(2)}, u32[]{:S(2)}) collective-permute-start(bf16[144,1024]{1,0:T(8,128)(2,1)} %pad_maximum_fusion), channel_id=1, source_target_pairs={{0,8},{4,12},{8,0},{12,4},{16,24},{20,28},{24,16},{28,20},{1,9},{5... | collective-permute-start | bytes 884744 | tf_op jit(solution)/shard_map/ppermute | solution.py:251
  13.1 12.7 %collective-permute-start.8 = (bf16[512,768]{1,0:T(8,128)(2,1)S(1)}, bf16[512,768]{1,0:T(8,128)(2,1)S(1)}, u32[]{:S(2)}, u32[]{:S(2)}) collective-permute-start(bf16[512,768]{1,0:T(8,128)(2,1)S(1)} %copy-done), channel_id=1, source_target_pairs={{0,4},{4,0},{8,12},{12,8},{16,20},{20,16},{24,28},{28,24},{1,5},{5... | collective-permute-start | bytes 2359304 | tf_op jit(solution)/shard_map/ppermute | solution.py:251
  20.6 1.4 copy-start.11
  22.0 9.9 %collective-permute-start.2 = (bf16[144,1024]{1,0:T(8,128)(2,1)S(1)}, bf16[144,1024]{1,0:T(8,128)(2,1)S(1)}, u32[]{:S(2)}, u32[]{:S(2)}) collective-permute-start(bf16[144,1024]{1,0:T(8,128)(2,1)S(1)} %pad_maximum_fusion.1), channel_id=1, source_target_pairs={{0,16},{4,20},{8,24},{12,28},{16,0},{20,4},{24,8},{28,12},{1,17},{... | collective-permute-start | bytes 884744 | tf_op jit(solution)/shard_map/ppermute | solution.py:251
  23.8 31.2 %collective-permute-start.9 = (bf16[512,768]{1,0:T(8,128)(2,1)S(1)}, bf16[512,768]{1,0:T(8,128)(2,1)S(1)}, u32[]{:S(2)}, u32[]{:S(2)}) collective-permute-start(bf16[512,768]{1,0:T(8,128)(2,1)S(1)} %copy-done), channel_id=1, source_target_pairs={{0,8},{4,12},{8,0},{12,4},{16,24},{20,28},{24,16},{28,20},{1,9},{5... | collective-permute-start | bytes 2359304 | tf_op jit(solution)/shard_map/ppermute | solution.py:251
  25.3 31.4 %collective-permute-start.11 = (bf16[512,768]{1,0:T(8,128)(2,1)S(1)}, bf16[512,768]{1,0:T(8,128)(2,1)}, u32[]{:S(2)}, u32[]{:S(2)}) collective-permute-start(bf16[512,768]{1,0:T(8,128)(2,1)S(1)} %copy-done), channel_id=1, source_target_pairs={{0,16},{4,20},{8,24},{12,28},{16,0},{20,4},{24,8},{28,12},{1,17},{... | collective-permute-start | bytes 2359304 | tf_op jit(solution)/shard_map/ppermute | solution.py:251
  25.8 31.5 %collective-permute-start.15 = (bf16[768,512]{1,0:T(8,128)(2,1)S(1)}, bf16[768,512]{1,0:T(8,128)(2,1)}, u32[]{:S(2)}, u32[]{:S(2)}) collective-permute-start(bf16[768,512]{1,0:T(8,128)(2,1)S(1)} %copy-done.1), channel_id=1, source_target_pairs={{0,4},{4,0},{8,12},{12,8},{16,20},{20,16},{24,28},{28,24},{1,5},{5... | collective-permute-start | bytes 2359304 | tf_op jit(solution)/shard_map/ppermute | solution.py:251
  25.8 20.3 %copy-start.2 = (bf16[512,768]{1,0:T(8,128)(2,1)}, bf16[512,768]{1,0:T(8,128)(2,1)S(1)}, u32[]{:S(2)}) copy-start(bf16[512,768]{1,0:T(8,128)(2,1)S(1)} %collective-permute-done.8.refs_7_) | copy-start | bytes 2359300
  25.8 36.0 %collective-permute-start.16 = (bf16[768,512]{1,0:T(8,128)(2,1)S(1)}, bf16[768,512]{1,0:T(8,128)(2,1)}, u32[]{:S(2)}, u32[]{:S(2)}) collective-permute-start(bf16[768,512]{1,0:T(8,128)(2,1)S(1)} %copy-done.1), channel_id=1, source_target_pairs={{0,8},{4,12},{8,0},{12,4},{16,24},{20,28},{24,16},{28,20},{1,9},{5... | collective-permute-start | bytes 2359304 | tf_op jit(solution)/shard_map/ppermute | solution.py:251
  32.7 31.7 %collective-permute-start.18 = (bf16[768,512]{1,0:T(8,128)(2,1)S(1)}, bf16[768,512]{1,0:T(8,128)(2,1)}, u32[]{:S(2)}, u32[]{:S(2)}) collective-permute-start(bf16[768,512]{1,0:T(8,128)(2,1)S(1)} %copy-done.1), channel_id=1, source_target_pairs={{0,16},{4,20},{8,24},{12,28},{16,0},{20,4},{24,8},{28,12},{1,17},{... | collective-permute-start | bytes 2359304 | tf_op jit(solution)/shard_map/ppermute | solution.py:251
  34.4 11.7 %copy-start.12 = (bf16[144,1024]{1,0:T(8,128)(2,1)S(1)}, bf16[144,1024]{1,0:T(8,128)(2,1)}, u32[]{:S(2)}) copy-start(bf16[144,1024]{1,0:T(8,128)(2,1)} %copy-done.11) | copy-start | bytes 884740
  55.0 45.1 %copy-start.3 = (bf16[512,768]{1,0:T(8,128)(2,1)}, bf16[512,768]{1,0:T(8,128)(2,1)S(1)}, u32[]{:S(2)}) copy-start(bf16[512,768]{1,0:T(8,128)(2,1)S(1)} %collective-permute-done.9.refs_8_) | copy-start | bytes 2359300
  55.0 10.0 %collective-permute-start.3 = (bf16[128,1024]{1,0:T(8,128)(2,1)}, bf16[128,1024]{1,0:T(8,128)(2,1)S(1)}, u32[]{:S(2)}, u32[]{:S(2)}) collective-permute-start(bf16[128,1024]{1,0:T(8,128)(2,1)} %get-tuple-element.21.refs_0_), channel_id=1, source_target_pairs={{0,1},{1,0},{2,3},{3,2},{4,5},{5,4},{6,7},{7,6},{8,9},{9,8},{10,11... | collective-permute-start | bytes 786440 | tf_op jit(solution)/shard_map/ppermute | solution.py:251
  56.7 9.9 %collective-permute-start.5 = (bf16[128,1024]{1,0:T(8,128)(2,1)}, bf16[128,1024]{1,0:T(8,128)(2,1)S(1)}, u32[]{:S(2)}, u32[]{:S(2)}) collective-permute-start(bf16[128,1024]{1,0:T(8,128)(2,1)} %get-tuple-element.21.refs_0_), channel_id=1, source_target_pairs={{1,2},{2,1},{5,6},{6,5},{9,10},{10,9},{13,14},{14,13},{17,18},{18,... | collective-permute-start | bytes 786440 | tf_op jit(solution)/shard_map/ppermute | solution.py:281
  57.4 10.7 %collective-permute-start.27 = (bf16[128,1024]{1,0:T(8,128)(2,1)}, bf16[128,1024]{1,0:T(8,128)(2,1)S(1)}, u32[]{:S(2)}, u32[]{:S(2)}) collective-permute-start(bf16[128,1024]{1,0:T(8,128)(2,1)} %get-tuple-element.26.refs_0_), channel_id=1, source_target_pairs={{0,1},{1,0},{2,3},{3,2},{4,5},{5,4},{6,7},{7,6},{8,9},{9,8},{10,11... | collective-permute-start | bytes 786440 | tf_op jit(solution)/shard_map/ppermute | solution.py:251
  61.8 19.5 %collective-permute-start.10 = (bf16[512,768]{1,0:T(8,128)(2,1)S(1)}, bf16[512,768]{1,0:T(8,128)(2,1)S(1)}, u32[]{:S(2)}, u32[]{:S(2)}) collective-permute-start(bf16[512,768]{1,0:T(8,128)(2,1)S(1)} %collective-permute-done.9.refs_8_), channel_id=1, source_target_pairs={{0,4},{4,0},{8,12},{12,8},{16,20},{20,16},{24,28},{28,24},{1,5},{5... | collective-permute-start | bytes 2359304 | tf_op jit(solution)/shard_map/ppermute | solution.py:251
  64.3 4.4 %collective-permute-start.29 = (bf16[128,1024]{1,0:T(8,128)(2,1)}, bf16[128,1024]{1,0:T(8,128)(2,1)S(1)}, u32[]{:S(2)}, u32[]{:S(2)}) collective-permute-start(bf16[128,1024]{1,0:T(8,128)(2,1)} %get-tuple-element.26.refs_0_), channel_id=1, source_target_pairs={{1,2},{2,1},{5,6},{6,5},{9,10},{10,9},{13,14},{14,13},{17,18},{18,... | collective-permute-start | bytes 786440 | tf_op jit(solution)/shard_map/ppermute | solution.py:281
  65.0 5.8 %copy-start.15 = (bf16[128,1024]{1,0:T(8,128)(2,1)}, bf16[128,1024]{1,0:T(8,128)(2,1)S(1)}, u32[]{:S(2)}) copy-start(bf16[128,1024]{1,0:T(8,128)(2,1)S(1)} %collective-permute-done.3.refs_1_) | copy-start | bytes 786436
  65.0 18.2 %collective-permute-start.13 = (bf16[512,768]{1,0:T(8,128)(2,1)S(1)}, bf16[512,768]{1,0:T(8,128)(2,1)S(1)}, u32[]{:S(2)}, u32[]{:S(2)}) collective-permute-start(bf16[512,768]{1,0:T(8,128)(2,1)S(1)} %collective-permute-done.9.refs_8_), channel_id=1, source_target_pairs={{0,16},{4,20},{8,24},{12,28},{16,0},{20,4},{24,8},{28,12},{1,17},{... | collective-permute-start | bytes 2359304 | tf_op jit(solution)/shard_map/ppermute | solution.py:251
  66.6 4.2 %copy-start.16 = (bf16[128,1024]{1,0:T(8,128)(2,1)}, bf16[128,1024]{1,0:T(8,128)(2,1)S(1)}, u32[]{:S(2)}) copy-start(bf16[128,1024]{1,0:T(8,128)(2,1)S(1)} %collective-permute-done.5.refs_4_) | copy-start | bytes 786436
  66.6 17.8 %collective-permute-start.20 = (bf16[768,512]{1,0:T(8,128)(2,1)}, bf16[768,512]{1,0:T(8,128)(2,1)S(1)}, u32[]{:S(2)}, u32[]{:S(2)}) collective-permute-start(bf16[768,512]{1,0:T(8,128)(2,1)} %collective-permute-done.18.refs_18_), channel_id=1, source_target_pairs={{0,8},{4,12},{8,0},{12,4},{16,24},{20,28},{24,16},{28,20},{1,9},{5... | collective-permute-start | bytes 2359304 | tf_op jit(solution)/shard_map/ppermute | solution.py:251
  68.1 41.8 %copy-start.13 = (bf16[128,1024]{1,0:T(8,128)(2,1)}, bf16[128,1024]{1,0:T(8,128)(2,1)S(1)}, u32[]{:S(2)}) copy-start(bf16[128,1024]{1,0:T(8,128)(2,1)S(1)} %collective-permute-done.27.refs_1_) | copy-start | bytes 786436
  68.1 2.0 %collective-permute-start.4 = (bf16[128,1024]{1,0:T(8,128)(2,1)S(1)}, bf16[128,1024]{1,0:T(8,128)(2,1)S(1)}, u32[]{:S(2)}, u32[]{:S(2)}) collective-permute-start(bf16[128,1024]{1,0:T(8,128)(2,1)S(1)} %collective-permute-done.3.refs_1_), channel_id=1, source_target_pairs={{1,2},{2,1},{5,6},{6,5},{9,10},{10,9},{13,14},{14,13},{17,18},{18,... | collective-permute-start | bytes 786440 | tf_op jit(solution)/shard_map/ppermute | solution.py:282
  68.8 41.1 %copy-start.14 = (bf16[128,1024]{1,0:T(8,128)(2,1)}, bf16[128,1024]{1,0:T(8,128)(2,1)S(1)}, u32[]{:S(2)}) copy-start(bf16[128,1024]{1,0:T(8,128)(2,1)S(1)} %collective-permute-done.29.refs_4_) | copy-start | bytes 786436
  68.8 12.0 %collective-permute-start.6 = (bf16[128,1024]{1,0:T(8,128)(2,1)S(1)}, bf16[128,1024]{1,0:T(8,128)(2,1)}, u32[]{:S(2)}, u32[]{:S(2)}) collective-permute-start(bf16[128,1024]{1,0:T(8,128)(2,1)S(1)} %collective-permute-done.5.refs_4_), channel_id=1, source_target_pairs={{1,0},{2,3},{5,4},{6,7},{9,8},{10,11},{13,12},{14,15},{17,16},{18,... | collective-permute-start | bytes 786440 | tf_op jit(solution)/shard_map/ppermute | solution.py:283
  70.1 28.4 %copy-start.18 = (bf16[128,1024]{1,0:T(8,128)(2,1)}, bf16[128,1024]{1,0:T(8,128)(2,1)S(1)}, u32[]{:S(2)}) copy-start(bf16[128,1024]{1,0:T(8,128)(2,1)S(1)} %collective-permute-done.4.refs_2_) | copy-start | bytes 786436
  70.1 10.7 %collective-permute-start.28 = (bf16[128,1024]{1,0:T(8,128)(2,1)S(1)}, bf16[128,1024]{1,0:T(8,128)(2,1)S(1)}, u32[]{:S(2)}, u32[]{:S(2)}) collective-permute-start(bf16[128,1024]{1,0:T(8,128)(2,1)S(1)} %collective-permute-done.27.refs_1_), channel_id=1, source_target_pairs={{1,2},{2,1},{5,6},{6,5},{9,10},{10,9},{13,14},{14,13},{17,18},{18,... | collective-permute-start | bytes 786440 | tf_op jit(solution)/shard_map/ppermute | solution.py:282
  80.7 3.7 %collective-permute-start.12 = (bf16[512,768]{1,0:T(8,128)(2,1)}, bf16[512,768]{1,0:T(8,128)(2,1)S(1)}, u32[]{:S(2)}, u32[]{:S(2)}) collective-permute-start(bf16[512,768]{1,0:T(8,128)(2,1)} %collective-permute-done.11.refs_10_), channel_id=1, source_target_pairs={{0,4},{4,0},{8,12},{12,8},{16,20},{20,16},{24,28},{28,24},{1,5},{5... | collective-permute-start | bytes 2359304 | tf_op jit(solution)/shard_map/ppermute | solution.py:251
  80.8 29.1 %copy-start.17 = (bf16[128,1024]{1,0:T(8,128)(2,1)}, bf16[128,1024]{1,0:T(8,128)(2,1)S(1)}, u32[]{:S(2)}) copy-start(bf16[128,1024]{1,0:T(8,128)(2,1)S(1)} %collective-permute-done.28.refs_2_) | copy-start | bytes 786436
  80.8 5.0 %collective-permute-start.17 = (bf16[768,512]{1,0:T(8,128)(2,1)}, bf16[768,512]{1,0:T(8,128)(2,1)S(1)}, u32[]{:S(2)}, u32[]{:S(2)}) collective-permute-start(bf16[768,512]{1,0:T(8,128)(2,1)} %collective-permute-done.16.refs_16_), channel_id=1, source_target_pairs={{0,4},{4,0},{8,12},{12,8},{16,20},{20,16},{24,28},{28,24},{1,5},{5... | collective-permute-start | bytes 2359304 | tf_op jit(solution)/shard_map/ppermute | solution.py:251
  81.3 18.9 %copy-start.4 = (bf16[512,768]{1,0:T(8,128)(2,1)}, bf16[512,768]{1,0:T(8,128)(2,1)S(1)}, u32[]{:S(2)}) copy-start(bf16[512,768]{1,0:T(8,128)(2,1)S(1)} %collective-permute-done.10.refs_9_) | copy-start | bytes 2359300
  81.3 5.8 %collective-permute-start.19 = (bf16[768,512]{1,0:T(8,128)(2,1)}, bf16[768,512]{1,0:T(8,128)(2,1)S(1)}, u32[]{:S(2)}, u32[]{:S(2)}) collective-permute-start(bf16[768,512]{1,0:T(8,128)(2,1)} %collective-permute-done.18.refs_18_), channel_id=1, source_target_pairs={{0,4},{4,0},{8,12},{12,8},{16,20},{20,16},{24,28},{28,24},{1,5},{5... | collective-permute-start | bytes 2359304 | tf_op jit(solution)/shard_map/ppermute | solution.py:251
  83.2 16.9 %copy-start.5 = (bf16[512,768]{1,0:T(8,128)(2,1)}, bf16[512,768]{1,0:T(8,128)(2,1)S(1)}, u32[]{:S(2)}) copy-start(bf16[512,768]{1,0:T(8,128)(2,1)S(1)} %collective-permute-done.13.refs_12_) | copy-start | bytes 2359300
  83.2 15.2 %collective-permute-start.14 = (bf16[512,768]{1,0:T(8,128)(2,1)S(1)}, bf16[512,768]{1,0:T(8,128)(2,1)S(1)}, u32[]{:S(2)}, u32[]{:S(2)}) collective-permute-start(bf16[512,768]{1,0:T(8,128)(2,1)S(1)} %collective-permute-done.13.refs_12_), channel_id=1, source_target_pairs={{0,4},{4,0},{8,12},{12,8},{16,20},{20,16},{24,28},{28,24},{1,5},{5... | collective-permute-start | bytes 2359304 | tf_op jit(solution)/shard_map/ppermute | solution.py:251
  84.4 15.8 %copy-start.6 = (bf16[768,512]{1,0:T(8,128)(2,1)}, bf16[768,512]{1,0:T(8,128)(2,1)S(1)}, u32[]{:S(2)}) copy-start(bf16[768,512]{1,0:T(8,128)(2,1)S(1)} %collective-permute-done.20.refs_20_) | copy-start | bytes 2359300
  84.4 15.7 %collective-permute-start.21 = (bf16[768,512]{1,0:T(8,128)(2,1)S(1)}, bf16[768,512]{1,0:T(8,128)(2,1)}, u32[]{:S(2)}, u32[]{:S(2)}) collective-permute-start(bf16[768,512]{1,0:T(8,128)(2,1)S(1)} %collective-permute-done.20.refs_20_), channel_id=1, source_target_pairs={{0,4},{4,0},{8,12},{12,8},{16,20},{20,16},{24,28},{28,24},{1,5},{5... | collective-permute-start | bytes 2359304 | tf_op jit(solution)/shard_map/ppermute | solution.py:251
  84.4 14.1 %copy-start.7 = (bf16[512,768]{1,0:T(8,128)(2,1)}, bf16[512,768]{1,0:T(8,128)(2,1)S(1)}, u32[]{:S(2)}) copy-start(bf16[512,768]{1,0:T(8,128)(2,1)S(1)} %collective-permute-done.12.refs_11_) | copy-start | bytes 2359300
  84.4 14.0 %collective-permute-start.7 = (bf16[128,1024]{1,0:T(8,128)(2,1)S(1)}, bf16[128,1024]{1,0:T(8,128)(2,1)S(1)}, u32[]{:S(2)}, u32[]{:S(2)}) collective-permute-start(bf16[128,1024]{1,0:T(8,128)(2,1)S(1)} %collective-permute-done.4.refs_2_), channel_id=1, source_target_pairs={{1,0},{2,3},{5,4},{6,7},{9,8},{10,11},{13,12},{14,15},{17,16},{18,... | collective-permute-start | bytes 786440 | tf_op jit(solution)/shard_map/ppermute | solution.py:284
  85.7 12.7 %copy-start.8 = (bf16[768,512]{1,0:T(8,128)(2,1)}, bf16[768,512]{1,0:T(8,128)(2,1)S(1)}, u32[]{:S(2)}) copy-start(bf16[768,512]{1,0:T(8,128)(2,1)S(1)} %collective-permute-done.17.refs_17_) | copy-start | bytes 2359300
  85.7 27.1 %collective-permute-start.30 = (bf16[128,1024]{1,0:T(8,128)(2,1)S(1)}, bf16[128,1024]{1,0:T(8,128)(2,1)}, u32[]{:S(2)}, u32[]{:S(2)}) collective-permute-start(bf16[128,1024]{1,0:T(8,128)(2,1)S(1)} %collective-permute-done.29.refs_4_), channel_id=1, source_target_pairs={{1,0},{2,3},{5,4},{6,7},{9,8},{10,11},{13,12},{14,15},{17,16},{18,... | collective-permute-start | bytes 786440 | tf_op jit(solution)/shard_map/ppermute | solution.py:283
  87.0 11.4 %copy-start.9 = (bf16[768,512]{1,0:T(8,128)(2,1)}, bf16[768,512]{1,0:T(8,128)(2,1)S(1)}, u32[]{:S(2)}) copy-start(bf16[768,512]{1,0:T(8,128)(2,1)S(1)} %collective-permute-done.19.refs_19_) | copy-start | bytes 2359300
  87.1 25.8 %collective-permute-start.31 = (bf16[128,1024]{1,0:T(8,128)(2,1)S(1)}, bf16[128,1024]{1,0:T(8,128)(2,1)}, u32[]{:S(2)}, u32[]{:S(2)}) collective-permute-start(bf16[128,1024]{1,0:T(8,128)(2,1)S(1)} %collective-permute-done.28.refs_2_), channel_id=1, source_target_pairs={{1,0},{2,3},{5,4},{6,7},{9,8},{10,11},{13,12},{14,15},{17,16},{18,... | collective-permute-start | bytes 786440 | tf_op jit(solution)/shard_map/ppermute | solution.py:284
  99.2 1.0 copy-start.10
  109.9 15.4 %collective-permute-start.22 = (bf16[128,1024]{1,0:T(8,128)(2,1)}, bf16[128,1024]{1,0:T(8,128)(2,1)S(1)}, u32[]{:S(2)}, u32[]{:S(2)}) collective-permute-start(bf16[128,1024]{1,0:T(8,128)(2,1)} %get-tuple-element.24), channel_id=1, source_target_pairs={{0,1},{3,2},{4,5},{7,6},{8,9},{11,10},{12,13},{15,14},{16,17},{19,... | collective-permute-start | bytes 786440 | tf_op jit(solution)/shard_map/ppermute | solution.py:296
  111.4 13.9 %copy-start.24 = (bf16[128,1024]{1,0:T(8,128)(2,1)S(1)}, bf16[128,1024]{1,0:T(8,128)(2,1)}, u32[]{:S(2)}) copy-start(bf16[128,1024]{1,0:T(8,128)(2,1)} %get-tuple-element.23) | copy-start | bytes 786436
  111.4 14.7 %copy-start.23 = (bf16[128,1024]{1,0:T(8,128)(2,1)S(1)}, bf16[128,1024]{1,0:T(8,128)(2,1)}, u32[]{:S(2)}) copy-start(bf16[128,1024]{1,0:T(8,128)(2,1)} %get-tuple-element.24) | copy-start | bytes 786436
  111.4 14.7 %collective-permute-start.24 = (bf16[128,1024]{1,0:T(8,128)(2,1)}, bf16[128,1024]{1,0:T(8,128)(2,1)S(1)}, u32[]{:S(2)}, u32[]{:S(2)}) collective-permute-start(bf16[128,1024]{1,0:T(8,128)(2,1)} %get-tuple-element.23), channel_id=1, source_target_pairs={{0,1},{3,2},{4,5},{7,6},{8,9},{11,10},{12,13},{15,14},{16,17},{19,... | collective-permute-start | bytes 786440 | tf_op jit(solution)/shard_map/ppermute | solution.py:295
  122.5 13.8 %copy-start.25 = (bf16[128,1024]{1,0:T(8,128)(2,1)S(1)}, bf16[128,1024]{1,0:T(8,128)(2,1)}, u32[]{:S(2)}) copy-start(bf16[128,1024]{1,0:T(8,128)(2,1)} %get-tuple-element.28) | copy-start | bytes 786436
  122.5 14.6 %copy-start.20 = (bf16[128,1024]{1,0:T(8,128)(2,1)S(1)}, bf16[128,1024]{1,0:T(8,128)(2,1)}, u32[]{:S(2)}) copy-start(bf16[128,1024]{1,0:T(8,128)(2,1)} %get-tuple-element.25) | copy-start | bytes 786436
  122.5 21.6 %copy-start.21 = (bf16[128,1024]{1,0:T(8,128)(2,1)S(1)}, bf16[128,1024]{1,0:T(8,128)(2,1)}, u32[]{:S(2)}) copy-start(bf16[128,1024]{1,0:T(8,128)(2,1)} %get-tuple-element.30) | copy-start | bytes 786436
  122.5 13.8 %collective-permute-start.32 = (bf16[128,1024]{1,0:T(8,128)(2,1)}, bf16[128,1024]{1,0:T(8,128)(2,1)S(1)}, u32[]{:S(2)}, u32[]{:S(2)}) collective-permute-start(bf16[128,1024]{1,0:T(8,128)(2,1)} %get-tuple-element.29), channel_id=1, source_target_pairs={{0,1},{3,2},{4,5},{7,6},{8,9},{11,10},{12,13},{15,14},{16,17},{19,... | collective-permute-start | bytes 786440 | tf_op jit(solution)/shard_map/ppermute | solution.py:296
  123.9 10.6 %collective-permute-start.34 = (bf16[128,1024]{1,0:T(8,128)(2,1)}, bf16[128,1024]{1,0:T(8,128)(2,1)S(1)}, u32[]{:S(2)}, u32[]{:S(2)}) collective-permute-start(bf16[128,1024]{1,0:T(8,128)(2,1)} %get-tuple-element.28), channel_id=1, source_target_pairs={{0,1},{3,2},{4,5},{7,6},{8,9},{11,10},{12,13},{15,14},{16,17},{19,... | collective-permute-start | bytes 786440 | tf_op jit(solution)/shard_map/ppermute | solution.py:295
  125.3 23.8 %collective-permute-start.23 = (bf16[128,1024]{1,0:T(8,128)(2,1)S(1)}, bf16[128,1024]{1,0:T(8,128)(2,1)S(1)}, u32[]{:S(2)}, u32[]{:S(2)}) collective-permute-start(bf16[128,1024]{1,0:T(8,128)(2,1)S(1)} %add_convert_fusion.5), channel_id=1, source_target_pairs={{1,2},{2,1},{5,6},{6,5},{9,10},{10,9},{13,14},{14,13},{17,18},{18,... | collective-permute-start | bytes 786440 | tf_op jit(solution)/shard_map/ppermute | solution.py:298
  126.1 10.9 %collective-permute-start.25 = (bf16[128,1024]{1,0:T(8,128)(2,1)S(1)}, bf16[128,1024]{1,0:T(8,128)(2,1)S(1)}, u32[]{:S(2)}, u32[]{:S(2)}) collective-permute-start(bf16[128,1024]{1,0:T(8,128)(2,1)S(1)} %add_convert_fusion.4), channel_id=1, source_target_pairs={{1,2},{2,1},{5,6},{6,5},{9,10},{10,9},{13,14},{14,13},{17,18},{18,... | collective-permute-start | bytes 786440 | tf_op jit(solution)/shard_map/ppermute | solution.py:297
  135.6 8.5 %collective-permute-start.35 = (bf16[128,1024]{1,0:T(8,128)(2,1)S(1)}, bf16[128,1024]{1,0:T(8,128)(2,1)S(1)}, u32[]{:S(2)}, u32[]{:S(2)}) collective-permute-start(bf16[128,1024]{1,0:T(8,128)(2,1)S(1)} %add_convert_fusion.1), channel_id=1, source_target_pairs={{1,2},{2,1},{5,6},{6,5},{9,10},{10,9},{13,14},{14,13},{17,18},{18,... | collective-permute-start | bytes 786440 | tf_op jit(solution)/shard_map/ppermute | solution.py:297
  136.4 12.8 %collective-permute-start.33 = (bf16[128,1024]{1,0:T(8,128)(2,1)S(1)}, bf16[128,1024]{1,0:T(8,128)(2,1)S(1)}, u32[]{:S(2)}, u32[]{:S(2)}) collective-permute-start(bf16[128,1024]{1,0:T(8,128)(2,1)S(1)} %add_convert_fusion.2), channel_id=1, source_target_pairs={{1,2},{2,1},{5,6},{6,5},{9,10},{10,9},{13,14},{14,13},{17,18},{18,... | collective-permute-start | bytes 786440 | tf_op jit(solution)/shard_map/ppermute | solution.py:298
  137.2 13.8 %collective-permute-start.26 = (bf16[128,1024]{1,0:T(8,128)(2,1)S(1)}, bf16[128,1024]{1,0:T(8,128)(2,1)S(1)}, u32[]{:S(2)}, u32[]{:S(2)}) collective-permute-start(bf16[128,1024]{1,0:T(8,128)(2,1)S(1)} %add_convert_fusion.3), channel_id=1, source_target_pairs={{0,1},{1,0},{2,3},{3,2},{4,5},{5,4},{6,7},{7,6},{8,9},{9,8},{10,11... | collective-permute-start | bytes 786440 | tf_op jit(solution)/shard_map/ppermute | solution.py:251
  144.2 9.6 %collective-permute-start.36 = (bf16[128,1024]{1,0:T(8,128)(2,1)S(1)}, bf16[128,1024]{1,0:T(8,128)(2,1)S(1)}, u32[]{:S(2)}, u32[]{:S(2)}) collective-permute-start(bf16[128,1024]{1,0:T(8,128)(2,1)S(1)} %add_convert_fusion), channel_id=1, source_target_pairs={{0,1},{1,0},{2,3},{3,2},{4,5},{5,4},{6,7},{7,6},{8,9},{9,8},{10,11... | collective-permute-start | bytes 786440 | tf_op jit(solution)/shard_map/ppermute | solution.py:251
  149.2 4.6 %copy-start.22 = (bf16[128,1024]{1,0:T(8,128)(2,1)}, bf16[128,1024]{1,0:T(8,128)(2,1)S(1)}, u32[]{:S(2)}) copy-start(bf16[128,1024]{1,0:T(8,128)(2,1)S(1)} %collective-permute-done.23.refs_4_) | copy-start | bytes 786436
  149.2 4.6 %copy-start.26 = (bf16[128,1024]{1,0:T(8,128)(2,1)}, bf16[128,1024]{1,0:T(8,128)(2,1)S(1)}, u32[]{:S(2)}) copy-start(bf16[128,1024]{1,0:T(8,128)(2,1)S(1)} %collective-permute-done.33.refs_7_) | copy-start | bytes 786436
  151.0 2.8 %copy-start.27 = (bf16[128,1024]{1,0:T(8,128)(2,1)}, bf16[128,1024]{1,0:T(8,128)(2,1)S(1)}, u32[]{:S(2)}) copy-start(bf16[128,1024]{1,0:T(8,128)(2,1)S(1)} %collective-permute-done.26.refs_5_) | copy-start | bytes 786436
  (3 other events, 2.2 us)

commit v3 on v2

--- a/solution.py
+++ b/solution.py
@@ -13,7 +13,7 @@
 F32 = jnp.float32
 BF16 = jnp.bfloat16
 HI = lax.Precision.HIGHEST
-VMEM = 60 * 1024 * 1024
+MIB = 1024 * 1024
 
 
 def iota(shape, dim):
@@ -128,78 +128,125 @@
         w_ref[lo:hi, :] = (u_part * mid_growth * gate[lo:hi]).astype(BF16)
 
 
-def norm_kernel(c_ref, a_ref, w_ref, h_ref, gain_ref, slot_ref, n_ref, *outs, width):
-    d_refs, acc = outs[:-1], outs[-1]
+def turned(row):
+    return jnp.broadcast_to(row, (8, row.shape[1])).T[:, :1]
+
+
+def keep_of(ref, lanes=slice(None)):
+    rows = ref.shape[0]
+    return ref[rows - 16 : rows - 15, lanes].astype(F32) + ref[rows - 8 : rows - 7, lanes].astype(F32)
+
+
+def chip_kernel(own_ref, other_ref, o_ref):
+    core = lax.rem(lax.axis_index("ctx"), 2)
+    states = own_ref.shape[0] - 16
+    half = o_ref.shape[1]
+    lanes = pl.ds(pl.multiple_of(core * half, 128), half)
+    own = own_ref[:states, lanes].astype(F32)
+    other = other_ref[:states, lanes].astype(F32)
+    own_keep = keep_of(own_ref, lanes)
+    other_keep = keep_of(other_ref, lanes)
+    total = jnp.where(core == 0, other_keep * own + other, own_keep * other + own)
+    keep = own_keep * other_keep
+    o_ref[:states, :] = total.astype(BF16)
+    high = keep.astype(BF16)
+    low = (keep - high.astype(F32)).astype(BF16)
+    o_ref[states : states + 8, :] = jnp.broadcast_to(high, (8, half))
+    o_ref[states + 8 :, :] = jnp.broadcast_to(low, (8, half))
+
+
+def prior_kernel(*refs):
+    o_ref = refs[-1]
+    chip = lax.axis_index("ctx") // 2
+    states = o_ref.shape[0]
+    chips = [jnp.bitwise_xor(chip, k + 1) for k in range(len(refs) - 1)]
+    keeps = [keep_of(ref) for ref in refs[:-1]]
+    total = jnp.zeros(o_ref.shape, F32)
+    for k, ref in enumerate(refs[:-1]):
+        weight = jnp.ones_like(keeps[k])
+        for other, keep in zip(chips, keeps):
+            weight = jnp.where((other > chips[k]) & (other < chip), weight * keep, weight)
+        weight = jnp.where(chips[k] < chip, weight, jnp.zeros_like(weight))
+        total = total + weight * ref[:states, :].astype(F32)
+    o_ref[...] = total.astype(BF16)
+
+
+def norm_kernel(flip_ref, c_ref, a_ref, w_ref, gain_ref, slot_ref, h_ref, *refs, width):
+    n_ref, d_ref, acc, start = refs[-4:]
     step = pl.program_id(0)
-    span, chans = a_ref.shape
-    handed = jnp.dot(c_ref[...], h_ref[...], preferred_element_type=F32)
-    t = a_ref[...] + w_ref[...].astype(F32) * handed
-    square = (t * t).astype(BF16)
-    group = min(256, chans)
+    span, half = a_ref.shape
+
+    @pl.when(step == 0)
+    def _():
+        acc[...] = jnp.zeros_like(acc)
+        if len(refs) > 4:
+            prior = h_ref[...].astype(F32)
+            states = prior.shape[0]
+            before = keep_of(refs[0]) * prior + refs[0][:states, :].astype(F32)
+            start[...] = jnp.where(flip_ref[0] == 1, before, prior).astype(BF16)
+        else:
+            start[...] = h_ref[...]
+
+    group = min(256, half)
     same = iota((group, group), 0) // width == iota((group, group), 1) // width
     mean_of = jnp.where(same, 1.0 / width, 0.0).astype(BF16)
-    mean = jnp.concatenate(
-        [
-            jnp.dot(square[:, k : k + group], mean_of, preferred_element_type=F32)
-            for k in range(0, chans, group)
-        ],
-        axis=1,
-    )
-    normed = (t * lax.rsqrt(mean + 1e-05) * gain_ref[...]).astype(BF16)
-    n_ref[...] = normed
+    for k in range(0, half, group):
+        for r in range(0, span, 128):
+            handed = jnp.dot(c_ref[r : r + 128, :], start[:, k : k + group], preferred_element_type=F32)
+            t = a_ref[r : r + 128, k : k + group] + w_ref[r : r + 128, k : k + group].astype(F32) * handed
+            mean = jnp.dot((t * t).astype(BF16), mean_of, preferred_element_type=F32)
+            normed = t * lax.rsqrt(mean + 1e-05) * gain_ref[:, k : k + group]
+            n_ref[r : r + 128, k : k + group] = normed.astype(BF16)
     pick = (iota((CAP, span), 0) == slot_ref[...]).astype(BF16)
-    rows = jnp.dot(pick, normed, preferred_element_type=F32)
-
-    @pl.when(step == 0)
-    def _():
-        acc[...] = rows
-
-    @pl.when(step > 0)
-    def _():
-        acc[...] = acc[...] + rows
+    acc[...] = acc[...] + jnp.dot(pick, n_ref[...], preferred_element_type=F32)
 
     @pl.when(step == pl.num_programs(0) - 1)
     def _():
-        rows = CAP // len(d_refs)
-        for k, d_ref in enumerate(d_refs):
-            d_ref[...] = acc[k * rows : (k + 1) * rows, :].astype(BF16)
-
-
-def turned(row):
-    return jnp.broadcast_to(row, (8, row.shape[1])).T[:, :1]
-
-
-def expert_kernel(*refs, ring, shards, groups):
-    inputs = refs[: sum(groups)]
-    u_hbm = refs[sum(groups) : sum(groups) + shards]
-    d_hbm = refs[sum(groups) + shards : sum(groups) + 2 * shards]
-    outs = refs[sum(groups) + 2 * shards : sum(groups) + 2 * shards + ring]
-    act, terms, u_buf, d_buf, u_sem, d_sem = refs[sum(groups) + 2 * shards + ring :]
+        d_ref[...] = acc[...].astype(BF16)
+
+
+def expert_kernel(flip_ref, *refs, ring, shards, groups, half):
+    halves = len(groups)
+    count = sum(map(sum, groups))
+    inputs = refs[:count]
+    hbm = refs[count : count + 2 * shards]
+    outs = refs[count + 2 * shards : count + 2 * shards + ring]
+    act, terms, u_buf, d_buf, sem = refs[count + 2 * shards + ring :]
     z = lax.axis_index("exp")
     c = lax.axis_index("ctx")
-    rows, chans = inputs[0].shape
-    u_copies = [pltpu.make_async_copy(u_hbm[k], u_buf.at[k], u_sem.at[k]) for k in range(shards)]
-    d_copies = [pltpu.make_async_copy(d_hbm[k], d_buf.at[k], d_sem.at[k]) for k in range(shards)]
-    for copy in u_copies + d_copies:
+    rows = inputs[0].shape[0]
+    chans = half * halves
+    copies = [pltpu.make_async_copy(hbm[k], u_buf.at[k], sem.at[k]) for k in range(shards)]
+    copies += [pltpu.make_async_copy(hbm[shards + k], d_buf.at[k], sem.at[shards + k]) for k in range(shards)]
+    ahead = min(3, len(copies))
+    for copy in copies[:ahead]:
         copy.start()
+
+    def ready(index):
+        if index + ahead < len(copies):
+            copies[index + ahead].start()
+        copies[index].wait()
+
     at = 0
-    for k in range(ring):
-        piece = inputs[at][...]
-        for other in range(at + 1, at + groups[k]):
-            piece = piece + inputs[other][...]
-        act[k] = piece
-        at += groups[k]
+    for q in range(halves):
+        lanes = pl.ds(pl.multiple_of(jnp.bitwise_xor(flip_ref[0], q) * half, 128), half)
+        for k in range(ring):
+            piece = inputs[at][...]
+            for other in range(at + 1, at + groups[q][k]):
+                piece = piece + inputs[other][...]
+            act[k, :, lanes] = piece
+            at += groups[q][k]
     feats = u_buf.shape[1]
     total = jnp.zeros((rows, u_buf.shape[2]), F32)
     for k in range(shards):
-        u_copies[k].wait()
+        ready(k)
         first = jnp.bitwise_xor(c, k) * feats
         a = act[jnp.bitwise_xor(z, first // chans), :, pl.ds(pl.multiple_of(lax.rem(first, chans), 128), feats)]
         total = total + jnp.dot(a, u_buf[k], preferred_element_type=F32)
     hidden = (total / (1.0 + jnp.exp(-total))).astype(BF16)
     cols = d_buf.shape[2]
     for k in range(shards):
-        d_copies[k].wait()
+        ready(shards + k)
         first = jnp.bitwise_xor(c, k) * cols
         term = jnp.dot(hidden, d_buf[k], preferred_element_type=F32).astype(BF16)
         terms[jnp.bitwise_xor(z, first // chans), :, pl.ds(pl.multiple_of(lax.rem(first, chans), 128), cols)] = term
@@ -207,32 +254,34 @@
         outs[k][...] = terms[k]
 
 
-def final_kernel(*refs, parts):
-    n_ref, slot_ref, prob_ref = refs[:3]
-    terms = refs[3:-2]
+def final_kernel(flip_ref, slot_ref, prob_ref, *refs, base, count):
+    rests = refs[:count]
+    terms = refs[count:-2]
     o_ref, sums = refs[-2:]
+    rows = sums.shape[0]
 
     @pl.when(pl.program_id(0) == 0)
     def _():
-        each = len(terms) // parts
-        rows = CAP // parts
-        for k in range(parts):
-            total = terms[k * each][...].astype(F32)
-            for other in range(k * each + 1, (k + 1) * each):
-                total = total + terms[other][...].astype(F32)
-            high = total.astype(BF16)
-            sums[k * rows : (k + 1) * rows, :] = high
-            sums[CAP + k * rows : CAP + (k + 1) * rows, :] = (total - high.astype(F32)).astype(BF16)
-
-    span = n_ref.shape[0]
+        total = terms[0][...].astype(F32)
+        for other in terms[1:]:
+            total = total + other[...].astype(F32)
+        sums[...] = total.astype(BF16)
+
+    span = o_ref.shape[0]
     slot = turned(slot_ref[...].astype(F32)).astype(jnp.int32)
-    pick = (iota((span, 2 * CAP), 1) % CAP == slot).astype(BF16)
-    token = jnp.dot(pick, sums[...], preferred_element_type=F32)
-    o_ref[...] = (n_ref[...].astype(F32) + turned(prob_ref[...]) * token).astype(BF16)
-
-
-def params():
-    return pltpu.CompilerParams(vmem_limit_bytes=VMEM)
+    prob = turned(prob_ref[...])
+    pick = (iota((span, rows), 1) + base == slot).astype(BF16)
+    part = o_ref.shape[1] // count
+    for q in range(count):
+        lanes = slice(None)
+        if count > 1:
+            lanes = pl.ds(pl.multiple_of(jnp.bitwise_xor(flip_ref[0], q) * part, 128), part)
+        token = jnp.dot(pick, sums[:, lanes], preferred_element_type=F32)
+        o_ref[:, lanes] = (rests[q][...].astype(F32) + prob * token).astype(BF16)
+
+
+def params(size=16):
+    return pltpu.CompilerParams(vmem_limit_bytes=size * MIB)
 
 
 def rows_spec(span, cols):
@@ -337,8 +386,11 @@
     states = state_input.shape[1]
     width = chans // heads
     blk = tokens // scale_exponent.shape[0]
-    parts = 2
+    halves = parts = 2
+    half = chans // halves
     rows = CAP // parts
+    paired = ctx == 8
+    flip = lax.rem(lax.axis_index("ctx"), 2)[None] if paired else jnp.zeros((1,), jnp.int32)
 
     span = 256
     message = pl.pallas_call(
@@ -353,7 +405,22 @@
         name="end_state",
     )(mixer_input, state_input, step_size, decay_log, scale_exponent)
 
-    start = entering_state(message, states, "ctx", ctx)
+    if paired:
+        beside = swap(message, "ctx", ctx, 1)
+        chip_shape = jax.ShapeDtypeStruct((states + 16, half), BF16)
+        chip = pl.pallas_call(
+            chip_kernel, out_shape=chip_shape, compiler_params=params(), name="chip_state"
+        )(message, beside)
+        chips = [swap(chip, "ctx", ctx, mask) for mask in (2, 4, 6)]
+        prior = pl.pallas_call(
+            prior_kernel,
+            out_shape=jax.ShapeDtypeStruct((states, half), BF16),
+            compiler_params=params(),
+            name="prior",
+        )(*chips)
+        priors = [prior, swap(prior, "ctx", ctx, 1)]
+    else:
+        start = entering_state(message, states, "ctx", ctx)
 
     local, weight = pl.pallas_call(
         functools.partial(local_kernel, blk=blk),
@@ -368,54 +435,89 @@
     )(mixer_input, gate_input, state_input, state_output, step_size, decay_log, scale_exponent,
       skip_gain[None])
 
-    normed, *dispatched = pl.pallas_call(
-        functools.partial(norm_kernel, width=width),
-        grid=(tokens // span,),
-        in_specs=[rows_spec(span, states), rows_spec(span, chans), rows_spec(span, chans), whole((states, chans)),
-                  whole((1, chans)), cols_spec(1, span)],
-        out_specs=[rows_spec(span, chans)] + [whole((rows, chans))] * parts,
-        out_shape=[jax.ShapeDtypeStruct((tokens, chans), BF16)] + [jax.ShapeDtypeStruct((rows, chans), BF16)] * parts,
-        scratch_shapes=[pltpu.VMEM((CAP, chans), F32)],
-        compiler_params=params(),
-        name="norm_dispatch",
-    )(state_output, local, weight, start, norm_gain[None], expert_slot[None])
+    normed = []
+    dispatched = []
+    for q in range(halves):
+
+        def col(i, flip, q=q):
+            return (0, jnp.bitwise_xor(flip[0], q))
+
+        def block(i, flip, q=q):
+            return (i, jnp.bitwise_xor(flip[0], q))
+
+        if paired:
+            entry = [whole((states, half)), pl.BlockSpec((states + 16, half), col)]
+            values = [priors[q], beside]
+        else:
+            entry = [pl.BlockSpec((states, half), col)]
+            values = [start]
+        outs = pl.pallas_call(
+            functools.partial(norm_kernel, width=width),
+            grid_spec=pltpu.PrefetchScalarGridSpec(
+                num_scalar_prefetch=1,
+                grid=(tokens // span,),
+                in_specs=[rows_spec(span, states), pl.BlockSpec((span, half), block), pl.BlockSpec((span, half), block),
+                          pl.BlockSpec((1, half), col), cols_spec(1, span)] + entry,
+                out_specs=[rows_spec(span, half), whole((CAP, half))],
+                scratch_shapes=[pltpu.VMEM((CAP, half), F32), pltpu.VMEM((states, half), BF16)],
+            ),
+            out_shape=[jax.ShapeDtypeStruct((tokens, half), BF16), jax.ShapeDtypeStruct((CAP, half), BF16)],
+            compiler_params=params(),
+        )(flip, state_output, local, weight, norm_gain[None], expert_slot[None], *values)
+        normed.append(outs[0])
+        dispatched.append(outs[1])
 
     ups = gather_pieces(up_weight, "ctx", ctx, (2, 4))
     downs = gather_pieces(down_weight, "ctx", ctx, (4, 2))
 
+    pieces = []
+    groups = []
+    for q in range(halves):
+        got, group = gather_line(dispatched[q], ring)
+        pieces += got
+        groups.append(group)
+
     any_spec = pl.BlockSpec(memory_space=pl.ANY)
+    rests = normed
     summed = []
     for part in range(parts):
-        pieces, groups = gather_line(dispatched[part], ring)
         terms = pl.pallas_call(
-            functools.partial(expert_kernel, ring=ring, shards=ctx, groups=groups),
-            in_specs=[whole((rows, chans))] * len(pieces) + [any_spec] * (2 * ctx),
-            out_specs=[whole((rows, chans))] * ring,
-            grid=(1,),
-            scratch_shapes=[
-                pltpu.VMEM((ring, rows, chans), BF16),
-                pltpu.VMEM((ring, rows, chans), BF16),
-                pltpu.VMEM((ctx,) + up_weight.shape, BF16),
-                pltpu.VMEM((ctx,) + down_weight.shape, BF16),
-                pltpu.SemaphoreType.DMA((ctx,)),
-                pltpu.SemaphoreType.DMA((ctx,)),
-            ],
+            functools.partial(expert_kernel, ring=ring, shards=ctx, groups=groups, half=half),
+            grid_spec=pltpu.PrefetchScalarGridSpec(
+                num_scalar_prefetch=1,
+                grid=(1,),
+                in_specs=[pl.BlockSpec((rows, half), lambda i, flip, part=part: (part, 0))] * len(pieces)
+                + [any_spec] * (2 * ctx),
+                out_specs=[whole((rows, chans))] * ring,
+                scratch_shapes=[
+                    pltpu.VMEM((ring, rows, chans), BF16),
+                    pltpu.VMEM((ring, rows, chans), BF16),
+                    pltpu.VMEM((ctx,) + up_weight.shape, BF16),
+                    pltpu.VMEM((ctx,) + down_weight.shape, BF16),
+                    pltpu.SemaphoreType.DMA((2 * ctx,)),
+                ],
+            ),
             out_shape=[jax.ShapeDtypeStruct((rows, chans), BF16)] * ring,
+            compiler_params=params(26),
+        )(flip, *pieces, *ups, *downs)
+        summed.append(sum_line(terms, ring))
+
+    for part in range(parts):
+        rests = [pl.pallas_call(
+            functools.partial(final_kernel, base=part * rows, count=len(rests)),
+            grid_spec=pltpu.PrefetchScalarGridSpec(
+                num_scalar_prefetch=1,
+                grid=(tokens // span,),
+                in_specs=[cols_spec(1, span), cols_spec(1, span)]
+                + [rows_spec(span, chans // len(rests))] * len(rests)
+                + [whole((rows, chans))] * len(summed[part]),
+                out_specs=rows_spec(span, chans),
+                scratch_shapes=[pltpu.VMEM((rows, chans), BF16)],
+            ),
+            out_shape=jax.ShapeDtypeStruct((tokens, chans), BF16),
             compiler_params=params(),
-        )(*pieces, *ups, *downs)
-        summed += sum_line(terms, ring)
-
-    return pl.pallas_call(
-        functools.partial(final_kernel, parts=parts),
-        grid=(tokens // span,),
-        in_specs=[rows_spec(span, chans), cols_spec(1, span), cols_spec(1, span)]
-        + [whole((rows, chans))] * len(summed),
-        out_specs=rows_spec(span, chans),
-        scratch_shapes=[pltpu.VMEM((2 * CAP, chans), BF16)],
-        out_shape=jax.ShapeDtypeStruct((tokens, chans), BF16),
-        compiler_params=params(),
-        name="combine",
-    )(normed, expert_slot[None], gate_prob[None], *summed)
+        )(flip, expert_slot[None], gate_prob[None], *rests, *summed[part])]
+    return rests[0]
 
 
 def solution(mesh):

time: 161 us -> 190 us (1.18)
  waiting for transfers between devices: 52.7 us -> 102 us
  Pallas kernels: 49.6 us -> 37.5 us
  other arithmetic: 7.12 us -> 0.4 us
  starting transfers between devices: 47.2 us -> 40.8 us
  local copies, waits for them, and re-layouts: 3.21 us -> 8.32 us
    ppermute x21 -> x23, waiting for transfers between devices: 24.9 us -> 60.1 us  [swap(): return lax.ppermute(value, axis, [(i, i ^ mask) for i in range(count)])]
    ppermute x2, waiting for transfers between devices: 9.95 us -> 20 us  [gather_line(): out_near = lax.ppermute(cross, 'exp', OUTWARD)]
    ppermute x2, waiting for transfers between devices: 0.01 us -> 9 us  [sum_line(): near = lax.ppermute(terms[2], 'exp', ENDS)]
    pallas_call x2, Pallas kernels: 19.3 us -> 10.5 us  [body(): pl.pallas_call(functools.partial(expert_kernel, ring=ring, shards=ctx, gr...]
    ppermute x21 -> x23, starting transfers between devices: 31 us -> 24.9 us  [swap(): return lax.ppermute(value, axis, [(i, i ^ mask) for i in range(count)])]
    unnamed x60 -> x36, local copies, waits for them, and re-layouts: 3.19 us -> 8.32 us
    convert_element_type x5 -> x0, other arithmetic: 4.99 us -> none  [the longest x2 2.35 us: pack(): end.astype(BF16)]
    ppermute x2, waiting for transfers between devices: 7.77 us -> 3.25 us  [sum_line(): far = lax.ppermute(terms[3], 'exp', ENDS)]
  transfers between devices with their start and end apart: 37 -> 39, of which waited for: 11 -> 18; matrix products, arithmetic and copies ran while one was open for 3% -> 0% of each run, Pallas kernels for 24% -> 13%
where the time goes in v3:
time: 190 us; the launch traced here: 189 us
  waiting for transfers between devices  102 us (54%)
  starting transfers between devices  40.8 us (21%)
  Pallas kernels  37.5 us (20%)
  local copies, waits for them, and re-layouts  8.32 us (4%)
    ppermute x23, waiting for transfers between devices, swap(): return lax.ppermute(value, axis, [(i, i ^ mask) for i in range(count)])  60.1 us
    ppermute x23, starting transfers between devices, swap(): return lax.ppermute(value, axis, [(i, i ^ mask) for i in range(count)])  24.9 us
    ppermute x2, waiting for transfers between devices, gather_line(): out_near = lax.ppermute(cross, 'exp', OUTWARD)  20 us
    pallas_call x2, Pallas kernels, body(): pl.pallas_call(functools.partial(expert_kernel, ring=ring, shards=ctx, gr...  10.5 us
    pallas_call x1, Pallas kernels, body(): pl.pallas_call(functools.partial(local_kernel, blk=blk), grid=(tokens //...  9.64 us
    ppermute x2, waiting for transfers between devices, gather_line(): out_far = lax.ppermute(cross_far, 'exp', OUTWARD)  9.29 us
    ppermute x2, waiting for transfers between devices, sum_line(): near = lax.ppermute(terms[2], 'exp', ENDS)  9 us
    unnamed x36, local copies, waits for them, and re-layouts  8.32 us
  transfers between devices with their start and end apart: 39, of which 18 were waited for; matrix products, arithmetic and copies ran while one was open for 0% of the time, Pallas kernels for 13%

profile of v3, /device:TPU:0, one launch (start us, length us, event | category | flops | bytes accessed | tf_op | source)
XLA Modules:
  0.0 189.1 jit_solution(9533299065751892288)
XLA Ops:
  0.0 1.6 copy-done
  1.6 0.9 copy-done.6
  2.5 0.8 copy-done.8
  3.4 0.8 copy-done.10
  4.2 0.7 copy-done.14
  4.9 3.6 %end_state.1.own_ref = bf16[144,1024]{1,0:T(8,128)(2,1)S(1)} custom-call(bf16[1024,1024]{1,0:T(8,128)(2,1)S(1)} %copy-done, bf16[1024,128]{1,0:T(8,128)(2,1)S(1)} %copy-done.6, f32[16,1024]{1,0:T(8,128)S(1)} %copy-done.8, f32[16,1024]{1,0:T(8,128)S(1)} %copy-done.10, s32[8,16]{1,0:T(8,128)S(1)} %copy-done.14), custom_call_target="tpu_custom_call" | custom-call | tf_op jit(solution)/shard_map/end_state/pallas_call | solution.py:396
  8.6 0.5 collective-permute-start
  9.1 2.6 %collective-permute-start.16 = (bf16[512,768]{1,0:T(8,128)(2,1)}, bf16[512,768]{1,0:T(8,128)(2,1)S(1)}, u32[]{:S(2)}, u32[]{:S(2)}) collective-permute-start(bf16[512,768]{1,0:T(8,128)(2,1)} %refs_12_.3), channel_id=1, source_target_pairs={{0,8},{4,12},{8,0},{12,4},{16,24},{20,28},{24,16},{28,20},{1,9},{5... | collective-permute-start | bytes 2359304 | tf_op jit(solution)/shard_map/ppermute | solution.py:300
  11.8 1.6 collective-permute-start.1
  13.3 1.5 collective-permute-start.2
  15.3 18.1 %collective-permute-done.1.refs_0_ = bf16[144,512]{1,0:T(8,128)(2,1)S(1)} collective-permute-done((bf16[144,512]{1,0:T(8,128)(2,1)S(1)}, bf16[144,512]{1,0:T(8,128)(2,1)S(1)}, u32[]{:S(2)}, u32[]{:S(2)}) %collective-permute-start.1) | collective-permute-done | bytes 147488 | tf_op jit(solution)/shard_map/ppermute | solution.py:300
  33.5 4.1 %collective-permute-done.3.refs_2_ = bf16[144,512]{1,0:T(8,128)(2,1)S(1)} collective-permute-done((bf16[144,512]{1,0:T(8,128)(2,1)S(1)}, bf16[144,512]{1,0:T(8,128)(2,1)S(1)}, u32[]{:S(2)}, u32[]{:S(2)}) %collective-permute-start.3) | collective-permute-done | bytes 147488 | tf_op jit(solution)/shard_map/ppermute | solution.py:300
  37.6 0.8 prior.1.h_ref
  38.4 1.6 copy-done.5
  40.0 0.9 copy-done.7
  40.9 0.8 copy-done.11
  41.8 9.6 %local_out.1 = (f32[1024,1024]{1,0:T(8,128)S(1)}, bf16[1024,1024]{1,0:T(8,128)(2,1)S(1)}) custom-call(bf16[1024,1024]{1,0:T(8,128)(2,1)S(1)} %copy-done.1, bf16[1024,1024]{1,0:T(8,128)(2,1)S(1)} %copy-done.5, bf16[1024,128]{1,0:T(8,128)(2,1)S(1)} %copy-done.7, bf16[1024,128]{1,0:T(8,128)(2,1)S(1)} %copy-done.4, f32[16,1024]{1,0:T(8,128)S(1)} %copy-done.9, ...), custom_call_target="tpu_custom_call" | custom-call | tf_op jit(solution)/shard_map/local_out/pallas_call | solution.py:425
  51.4 3.8 %shard_map.127 = (bf16[1024,512]{1,0:T(8,128)(2,1)S(1)}, bf16[256,512]{1,0:T(8,128)(2,1)S(1)}) custom-call(s32[1]{0:T(128)} %bitcast.flip_ref, bf16[1024,128]{1,0:T(8,128)(2,1)S(1)} %copy-done.4, f32[1024,1024]{1,0:T(8,128)S(1)} %get-tuple-element.19.a_ref, bf16[1024,1024]{1,0:T(8,128)(2,1)S(1)} %get-tuple-element.20.w_ref, f32[1,1024]{1,0:T(1,128)S(1)} %bitcast.11, ...), custom_call_target="tpu_custom_call" | custom-call | tf_op jit(solution)/shard_map/pallas_call | solution.py:454
  55.2 1.7 collective-permute-start.5
  56.9 0.7 collective-permute-start.7
  57.6 0.6 collective-permute-start.25
  58.1 1.5 collective-permute-start.18
  59.7 4.3 %collective-permute-done.5.refs_1_ = bf16[256,512]{1,0:T(8,128)(2,1)S(1)} collective-permute-done((bf16[256,512]{1,0:T(8,128)(2,1)S(1)}, bf16[256,512]{1,0:T(8,128)(2,1)S(1)}, u32[]{:S(2)}, u32[]{:S(2)}) %collective-permute-start.5) | collective-permute-done | bytes 262176 | tf_op jit(solution)/shard_map/ppermute | solution.py:300
  64.0 1.5 collective-permute-start.23
  66.0 3.6 %shard_map.128 = (bf16[1024,512]{1,0:T(8,128)(2,1)S(1)}, bf16[256,512]{1,0:T(8,128)(2,1)S(1)}) custom-call(s32[1]{0:T(128)} %bitcast.flip_ref, bf16[1024,128]{1,0:T(8,128)(2,1)S(1)} %copy-done.4, f32[1024,1024]{1,0:T(8,128)S(1)} %get-tuple-element.19.a_ref, bf16[1024,1024]{1,0:T(8,128)(2,1)S(1)} %get-tuple-element.20.w_ref, f32[1,1024]{1,0:T(1,128)S(1)} %bitcast.12, ...), custom_call_target="tpu_custom_call" | custom-call | tf_op jit(solution)/shard_map/pallas_call | solution.py:454
  69.7 8.4 %collective-permute-done.25.refs_24_ = bf16[768,512]{1,0:T(8,128)(2,1)S(1)} collective-permute-done((bf16[768,512]{1,0:T(8,128)(2,1)S(1)}, bf16[768,512]{1,0:T(8,128)(2,1)S(1)}, u32[]{:S(2)}, u32[]{:S(2)}) %collective-permute-start.25) | collective-permute-done | bytes 786464 | tf_op jit(solution)/shard_map/ppermute | solution.py:300
  78.0 4.4 %collective-permute-start.10 = (bf16[256,512]{1,0:T(8,128)(2,1)S(1)}, bf16[256,512]{1,0:T(8,128)(2,1)S(1)}, u32[]{:S(2)}, u32[]{:S(2)}) collective-permute-start(bf16[256,512]{1,0:T(8,128)(2,1)S(1)} %get-tuple-element.24.refs_6_), channel_id=1, source_target_pairs={{0,1},{1,0},{2,3},{3,2},{4,5},{5,4},{6,7},{7,6},{8,9},{9,8},{10,11... | collective-permute-start | bytes 786440 | tf_op jit(solution)/shard_map/ppermute | solution.py:300
  82.4 11.7 %collective-permute-done.18.refs_16_ = bf16[512,768]{1,0:T(8,128)(2,1)S(1)} collective-permute-done((bf16[512,768]{1,0:T(8,128)(2,1)S(1)}, bf16[512,768]{1,0:T(8,128)(2,1)S(1)}, u32[]{:S(2)}, u32[]{:S(2)}) %collective-permute-start.18) | collective-permute-done | bytes 786464 | tf_op jit(solution)/shard_map/ppermute | solution.py:300
  94.1 0.7 collective-permute-start.12
  94.8 0.7 collective-permute-start.6
  95.5 1.3 collective-permute-start.8
  96.8 0.6 collective-permute-start.20
  97.4 1.5 collective-permute-start.27
  98.9 0.7 collective-permute-start.11
  99.6 10.8 %collective-permute-done.8.refs_3_ = bf16[256,512]{1,0:T(8,128)(2,1)S(1)} collective-permute-done((bf16[256,512]{1,0:T(8,128)(2,1)S(1)}, bf16[256,512]{1,0:T(8,128)(2,1)S(1)}, u32[]{:S(2)}, u32[]{:S(2)}) %collective-permute-start.8) | collective-permute-done | bytes 262176 | tf_op jit(solution)/shard_map/ppermute | solution.py:332
  110.4 1.3 collective-permute-start.13
  111.7 1.3 collective-permute-start.9
  113.0 9.2 %collective-permute-done.13.refs_9_ = bf16[256,512]{1,0:T(8,128)(2,1)S(1)} collective-permute-done((bf16[256,512]{1,0:T(8,128)(2,1)S(1)}, bf16[256,512]{1,0:T(8,128)(2,1)S(1)}, u32[]{:S(2)}, u32[]{:S(2)}) %collective-permute-start.13) | collective-permute-done | bytes 262176 | tf_op jit(solution)/shard_map/ppermute | solution.py:332
  122.1 1.3 collective-permute-start.14
  123.4 6.3 %collective-permute-done.9.refs_5_ = bf16[256,512]{1,0:T(8,128)(2,1)S(1)} collective-permute-done((bf16[256,512]{1,0:T(8,128)(2,1)S(1)}, bf16[256,512]{1,0:T(8,128)(2,1)S(1)}, u32[]{:S(2)}, u32[]{:S(2)}) %collective-permute-start.9) | collective-permute-done | bytes 262176 | tf_op jit(solution)/shard_map/ppermute | solution.py:333
  129.8 2.9 %collective-permute-done.14.refs_11_ = bf16[256,512]{1,0:T(8,128)(2,1)S(1)} collective-permute-done((bf16[256,512]{1,0:T(8,128)(2,1)S(1)}, bf16[256,512]{1,0:T(8,128)(2,1)S(1)}, u32[]{:S(2)}, u32[]{:S(2)}) %collective-permute-start.14) | collective-permute-done | bytes 262176 | tf_op jit(solution)/shard_map/ppermute | solution.py:333
  132.7 0.5 collective-permute-start.24
  133.8 1.2 collective-permute-done.19.refs_17_
  135.0 1.1 collective-permute-done.24.refs_23_
  136.1 1.1 collective-permute-done.21.refs_19_
  137.3 1.1 collective-permute-done.28.refs_27_
  138.4 5.2 %shard_map.131 = (bf16[128,1024]{1,0:T(8,128)(2,1)S(1)}, bf16[128,1024]{1,0:T(8,128)(2,1)S(1)}, bf16[128,1024]{1,0:T(8,128)(2,1)S(1)}, bf16[128,1024]{1,0:T(8,128)(2,1)S(1)}) custom-call(s32[1]{0:T(128)} %bitcast.flip_ref, bf16[256,512]{1,0:T(8,128)(2,1)S(1)} %get-tuple-element.23.refs_0_, bf16[256,512]{1,0:T(8,128)(2,1)S(1)} %collective-permute-done.5.refs_1_, ...), custom_call_target="tpu_custom_call" | custom-call | tf_op jit(solution)/shard_map/pallas_call | solution.py:484
  143.6 1.5 collective-permute-start.36
  145.1 5.3 %shard_map.129 = (bf16[128,1024]{1,0:T(8,128)(2,1)S(1)}, bf16[128,1024]{1,0:T(8,128)(2,1)S(1)}, bf16[128,1024]{1,0:T(8,128)(2,1)S(1)}, bf16[128,1024]{1,0:T(8,128)(2,1)S(1)}) custom-call(s32[1]{0:T(128)} %bitcast.flip_ref, bf16[256,512]{1,0:T(8,128)(2,1)S(1)} %get-tuple-element.23.refs_0_, bf16[256,512]{1,0:T(8,128)(2,1)S(1)} %collective-permute-done.5.refs_1_, ...), custom_call_target="tpu_custom_call" | custom-call | tf_op jit(solution)/shard_map/pallas_call | solution.py:484
  150.4 1.3 collective-permute-start.31
  151.7 1.3 collective-permute-start.34
  153.0 1.3 collective-permute-start.29
  154.4 0.7 collective-permute-start.37
  155.1 3.3 %collective-permute-done.31 = bf16[128,1024]{1,0:T(8,128)(2,1)S(1)} collective-permute-done((bf16[128,1024]{1,0:T(8,128)(2,1)S(1)}, bf16[128,1024]{1,0:T(8,128)(2,1)S(1)}, u32[]{:S(2)}, u32[]{:S(2)}) %collective-permute-start.31) | collective-permute-done | bytes 262176 | tf_op jit(solution)/shard_map/ppermute | solution.py:344
  158.4 0.7 collective-permute-start.32
  159.1 4.9 %collective-permute-done.34 = bf16[128,1024]{1,0:T(8,128)(2,1)S(1)} collective-permute-done((bf16[128,1024]{1,0:T(8,128)(2,1)S(1)}, bf16[128,1024]{1,0:T(8,128)(2,1)S(1)}, u32[]{:S(2)}, u32[]{:S(2)}) %collective-permute-start.34) | collective-permute-done | bytes 262176 | tf_op jit(solution)/shard_map/ppermute | solution.py:345
  164.1 0.7 collective-permute-start.35
  164.7 4.1 %collective-permute-done.29 = bf16[128,1024]{1,0:T(8,128)(2,1)S(1)} collective-permute-done((bf16[128,1024]{1,0:T(8,128)(2,1)S(1)}, bf16[128,1024]{1,0:T(8,128)(2,1)S(1)}, u32[]{:S(2)}, u32[]{:S(2)}) %collective-permute-start.29) | collective-permute-done | bytes 262176 | tf_op jit(solution)/shard_map/ppermute | solution.py:345
  169.0 0.7 collective-permute-start.30
  169.7 5.0 %collective-permute-start.33 = (bf16[128,1024]{1,0:T(8,128)(2,1)S(1)}, bf16[128,1024]{1,0:T(8,128)(2,1)S(1)}, u32[]{:S(2)}, u32[]{:S(2)}) collective-permute-start(bf16[128,1024]{1,0:T(8,128)(2,1)S(1)} %add_convert_fusion.3), channel_id=1, source_target_pairs={{0,1},{1,0},{2,3},{3,2},{4,5},{5,4},{6,7},{7,6},{8,9},{9,8},{10,11... | collective-permute-start | bytes 786440 | tf_op jit(solution)/shard_map/ppermute | solution.py:300
  174.8 7.0 %collective-permute-done.33.refs_4_ = bf16[128,1024]{1,0:T(8,128)(2,1)S(1)} collective-permute-done((bf16[128,1024]{1,0:T(8,128)(2,1)S(1)}, bf16[128,1024]{1,0:T(8,128)(2,1)S(1)}, u32[]{:S(2)}, u32[]{:S(2)}) %collective-permute-start.33) | collective-permute-done | bytes 262176 | tf_op jit(solution)/shard_map/ppermute | solution.py:300
  181.8 2.2 %shard_map.130.refs_0_ = bf16[1024,1024]{1,0:T(8,128)(2,1)S(1)} custom-call(s32[1]{0:T(128)} %bitcast.flip_ref, s32[1,1024]{1,0:T(1,128)S(1)} %bitcast.7, f32[1,1024]{1,0:T(1,128)S(1)} %bitcast.9, bf16[1024,512]{1,0:T(8,128)(2,1)S(1)} %get-tuple-element.21.refs_0_, bf16[1024,512]{1,0:T(8,128)(2,1)S(1)} %get-tuple-element.22.refs_1_, ...), custom_call_target="tpu_custom_call" | custom-call | tf_op jit(solution)/shard_map/pallas_call | solution.py:506
  184.0 1.8 collective-permute-done.38.refs_3_
  185.9 3.2 %shard_map.132 = bf16[1024,1024]{1,0:T(8,128)(2,1)} custom-call(s32[1]{0:T(128)} %bitcast.flip_ref, s32[1,1024]{1,0:T(1,128)S(1)} %bitcast.8, f32[1,1024]{1,0:T(1,128)S(1)} %bitcast.10, bf16[1024,1024]{1,0:T(8,128)(2,1)S(1)} %shard_map.130.refs_0_, bf16[128,1024]{1,0:T(8,128)(2,1)S(1)} %get-tuple-element.29.refs_1_, ...), custom_call_target="tpu_custom_call" | custom-call | tf_op jit(solution)/shard_map/pallas_call | solution.py:506
  (66 shorter events, 2.2 us)
Async XLA Ops:
  0.0 1.6 copy-start
  1.6 0.9 copy-start.6
  2.5 0.8 copy-start.8
  3.4 0.8 copy-start.10
  4.2 0.7 copy-start.14
  4.9 33.4 %copy-start.1 = (bf16[1024,1024]{1,0:T(8,128)(2,1)S(1)}, bf16[1024,1024]{1,0:T(8,128)(2,1)}, u32[]{:S(2)}) copy-start(bf16[1024,1024]{1,0:T(8,128)(2,1)} %x_ref.3) | copy-start | bytes 6291460
  4.9 33.4 %copy-start.4 = (bf16[1024,128]{1,0:T(8,128)(2,1)S(1)}, bf16[1024,128]{1,0:T(8,128)(2,1)}, u32[]{:S(2)}) copy-start(bf16[1024,128]{1,0:T(8,128)(2,1)} %c_ref.5) | copy-start | bytes 786436
  4.9 33.4 %copy-start.9 = (f32[16,1024]{1,0:T(8,128)S(1)}, f32[16,1024]{1,0:T(8,128)}, u32[]{:S(2)}) copy-start(f32[16,1024]{1,0:T(8,128)} %st_ref.3) | copy-start | bytes 196612
  4.9 33.4 %copy-start.15 = (s32[8,16]{1,0:T(8,128)S(1)}, s32[8,16]{1,0:T(8,128)}, u32[]{:S(2)}) copy-start(s32[8,16]{1,0:T(8,128)} %sc_ref.3) | copy-start | bytes 1540
  4.9 33.4 %copy-start.17 = (f32[16]{0:T(128)S(1)}, f32[16]{0:T(128)}, u32[]{:S(2)}) copy-start(f32[16]{0:T(128)} %param.19) | copy-start | bytes 196
  8.6 3.1 %collective-permute-start = (bf16[144,1024]{1,0:T(8,128)(2,1)S(1)}, bf16[144,1024]{1,0:T(8,128)(2,1)S(1)}, u32[]{:S(2)}, u32[]{:S(2)}) collective-permute-start(bf16[144,1024]{1,0:T(8,128)(2,1)S(1)} %end_state.1.own_ref), channel_id=1, source_target_pairs={{0,4},{4,0},{8,12},{12,8},{16,20},{20,16},{24,28},{28,24},{1,5},{5... | collective-permute-start | bytes 884744 | tf_op jit(solution)/shard_map/ppermute | solution.py:300
  9.1 56.4 %collective-permute-start.16 = (bf16[512,768]{1,0:T(8,128)(2,1)}, bf16[512,768]{1,0:T(8,128)(2,1)S(1)}, u32[]{:S(2)}, u32[]{:S(2)}) collective-permute-start(bf16[512,768]{1,0:T(8,128)(2,1)} %refs_12_.3), channel_id=1, source_target_pairs={{0,8},{4,12},{8,0},{12,4},{16,24},{20,28},{24,16},{28,20},{1,9},{5... | collective-permute-start | bytes 2359304 | tf_op jit(solution)/shard_map/ppermute | solution.py:300
  11.8 21.7 %collective-permute-start.1 = (bf16[144,512]{1,0:T(8,128)(2,1)S(1)}, bf16[144,512]{1,0:T(8,128)(2,1)S(1)}, u32[]{:S(2)}, u32[]{:S(2)}) collective-permute-start(bf16[144,512]{1,0:T(8,128)(2,1)S(1)} %chip_state.1), channel_id=1, source_target_pairs={{0,8},{4,12},{8,0},{12,4},{16,24},{20,28},{24,16},{28,20},{1,9},{5... | collective-permute-start | bytes 442376 | tf_op jit(solution)/shard_map/ppermute | solution.py:300
  13.3 20.1 %collective-permute-start.2 = (bf16[144,512]{1,0:T(8,128)(2,1)S(1)}, bf16[144,512]{1,0:T(8,128)(2,1)S(1)}, u32[]{:S(2)}, u32[]{:S(2)}) collective-permute-start(bf16[144,512]{1,0:T(8,128)(2,1)S(1)} %chip_state.1), channel_id=1, source_target_pairs={{0,16},{4,20},{8,24},{12,28},{16,0},{20,4},{24,8},{28,12},{1,17},{... | collective-permute-start | bytes 442376 | tf_op jit(solution)/shard_map/ppermute | solution.py:300
  14.9 22.7 %collective-permute-start.3 = (bf16[144,512]{1,0:T(8,128)(2,1)S(1)}, bf16[144,512]{1,0:T(8,128)(2,1)S(1)}, u32[]{:S(2)}, u32[]{:S(2)}) collective-permute-start(bf16[144,512]{1,0:T(8,128)(2,1)S(1)} %chip_state.1), channel_id=1, source_target_pairs={{0,24},{4,28},{8,16},{12,20},{16,8},{20,12},{24,0},{28,4},{1,25},{... | collective-permute-start | bytes 442376 | tf_op jit(solution)/shard_map/ppermute | solution.py:300
  38.3 19.8 %collective-permute-start.4 = (bf16[128,512]{1,0:T(8,128)(2,1)}, bf16[128,512]{1,0:T(8,128)(2,1)}, u32[]{:S(2)}, u32[]{:S(2)}) collective-permute-start(bf16[128,512]{1,0:T(8,128)(2,1)} %prior.1.h_ref), channel_id=1, source_target_pairs={{0,4},{4,0},{8,12},{12,8},{16,20},{20,16},{24,28},{28,24},{1,5},{5... | collective-permute-start | bytes 393224 | tf_op jit(solution)/shard_map/ppermute | solution.py:300
  38.4 1.6 copy-start.5
  40.0 0.9 copy-start.7
  40.9 0.8 copy-start.11
  41.7 9.7 %copy-start.12 = (s32[1024]{0:T(1024)S(1)}, s32[1024]{0:T(1024)}, u32[]{:S(2)}) copy-start(s32[1024]{0:T(1024)} %param.24) | copy-start | bytes 12292
  41.7 9.7 %copy-start.16 = (f32[1024]{0:T(1024)S(1)}, f32[1024]{0:T(1024)}, u32[]{:S(2)}) copy-start(f32[1024]{0:T(1024)} %param.21) | copy-start | bytes 12292
  51.4 6.1 %copy-start.3 = (bf16[768,512]{1,0:T(8,128)(2,1)S(1)}, bf16[768,512]{1,0:T(8,128)(2,1)}, u32[]{:S(2)}) copy-start(bf16[768,512]{1,0:T(8,128)(2,1)} %refs_20_.3) | copy-start | bytes 2359300
  51.4 6.7 %copy-start.2 = (bf16[512,768]{1,0:T(8,128)(2,1)S(1)}, bf16[512,768]{1,0:T(8,128)(2,1)}, u32[]{:S(2)}) copy-start(bf16[512,768]{1,0:T(8,128)(2,1)} %refs_12_.3) | copy-start | bytes 2359300
  55.2 8.8 %collective-permute-start.5 = (bf16[256,512]{1,0:T(8,128)(2,1)S(1)}, bf16[256,512]{1,0:T(8,128)(2,1)S(1)}, u32[]{:S(2)}, u32[]{:S(2)}) collective-permute-start(bf16[256,512]{1,0:T(8,128)(2,1)S(1)} %get-tuple-element.23.refs_0_), channel_id=1, source_target_pairs={{0,1},{1,0},{2,3},{3,2},{4,5},{5,4},{6,7},{7,6},{8,9},{9,8},{10,11... | collective-permute-start | bytes 786440 | tf_op jit(solution)/shard_map/ppermute | solution.py:300
  56.9 8.6 %collective-permute-start.7 = (bf16[256,512]{1,0:T(8,128)(2,1)S(1)}, bf16[256,512]{1,0:T(8,128)(2,1)S(1)}, u32[]{:S(2)}, u32[]{:S(2)}) collective-permute-start(bf16[256,512]{1,0:T(8,128)(2,1)S(1)} %get-tuple-element.23.refs_0_), channel_id=1, source_target_pairs={{1,2},{2,1},{5,6},{6,5},{9,10},{10,9},{13,14},{14,13},{17,18},{18,... | collective-permute-start | bytes 786440 | tf_op jit(solution)/shard_map/ppermute | solution.py:330
  57.6 20.5 %collective-permute-start.25 = (bf16[768,512]{1,0:T(8,128)(2,1)S(1)}, bf16[768,512]{1,0:T(8,128)(2,1)S(1)}, u32[]{:S(2)}, u32[]{:S(2)}) collective-permute-start(bf16[768,512]{1,0:T(8,128)(2,1)S(1)} %copy-done.3), channel_id=1, source_target_pairs={{0,16},{4,20},{8,24},{12,28},{16,0},{20,4},{24,8},{28,12},{1,17},{... | collective-permute-start | bytes 2359304 | tf_op jit(solution)/shard_map/ppermute | solution.py:300
  58.1 36.0 %collective-permute-start.18 = (bf16[512,768]{1,0:T(8,128)(2,1)S(1)}, bf16[512,768]{1,0:T(8,128)(2,1)S(1)}, u32[]{:S(2)}, u32[]{:S(2)}) collective-permute-start(bf16[512,768]{1,0:T(8,128)(2,1)S(1)} %copy-done.2), channel_id=1, source_target_pairs={{0,16},{4,20},{8,24},{12,28},{16,0},{20,4},{24,8},{28,12},{1,17},{... | collective-permute-start | bytes 2359304 | tf_op jit(solution)/shard_map/ppermute | solution.py:300
  64.0 30.8 %collective-permute-start.23 = (bf16[768,512]{1,0:T(8,128)(2,1)S(1)}, bf16[768,512]{1,0:T(8,128)(2,1)S(1)}, u32[]{:S(2)}, u32[]{:S(2)}) collective-permute-start(bf16[768,512]{1,0:T(8,128)(2,1)S(1)} %copy-done.3), channel_id=1, source_target_pairs={{0,8},{4,12},{8,0},{12,4},{16,24},{20,28},{24,16},{28,20},{1,9},{5... | collective-permute-start | bytes 2359304 | tf_op jit(solution)/shard_map/ppermute | solution.py:300
  65.5 30.0 %collective-permute-start.15 = (bf16[512,768]{1,0:T(8,128)(2,1)S(1)}, bf16[512,768]{1,0:T(8,128)(2,1)S(1)}, u32[]{:S(2)}, u32[]{:S(2)}) collective-permute-start(bf16[512,768]{1,0:T(8,128)(2,1)S(1)} %copy-done.2), channel_id=1, source_target_pairs={{0,4},{4,0},{8,12},{12,8},{16,20},{20,16},{24,28},{28,24},{1,5},{5... | collective-permute-start | bytes 2359304 | tf_op jit(solution)/shard_map/ppermute | solution.py:300
  65.5 31.3 %collective-permute-start.22 = (bf16[768,512]{1,0:T(8,128)(2,1)S(1)}, bf16[768,512]{1,0:T(8,128)(2,1)S(1)}, u32[]{:S(2)}, u32[]{:S(2)}) collective-permute-start(bf16[768,512]{1,0:T(8,128)(2,1)S(1)} %copy-done.3), channel_id=1, source_target_pairs={{0,4},{4,0},{8,12},{12,8},{16,20},{20,16},{24,28},{28,24},{1,5},{5... | collective-permute-start | bytes 2359304 | tf_op jit(solution)/shard_map/ppermute | solution.py:300
  78.0 19.3 %collective-permute-start.10 = (bf16[256,512]{1,0:T(8,128)(2,1)S(1)}, bf16[256,512]{1,0:T(8,128)(2,1)S(1)}, u32[]{:S(2)}, u32[]{:S(2)}) collective-permute-start(bf16[256,512]{1,0:T(8,128)(2,1)S(1)} %get-tuple-element.24.refs_6_), channel_id=1, source_target_pairs={{0,1},{1,0},{2,3},{3,2},{4,5},{5,4},{6,7},{7,6},{8,9},{9,8},{10,11... | collective-permute-start | bytes 786440 | tf_op jit(solution)/shard_map/ppermute | solution.py:300
  94.1 4.8 %collective-permute-start.12 = (bf16[256,512]{1,0:T(8,128)(2,1)S(1)}, bf16[256,512]{1,0:T(8,128)(2,1)S(1)}, u32[]{:S(2)}, u32[]{:S(2)}) collective-permute-start(bf16[256,512]{1,0:T(8,128)(2,1)S(1)} %get-tuple-element.24.refs_6_), channel_id=1, source_target_pairs={{1,2},{2,1},{5,6},{6,5},{9,10},{10,9},{13,14},{14,13},{17,18},{18,... | collective-permute-start | bytes 786440 | tf_op jit(solution)/shard_map/ppermute | solution.py:330
  94.8 4.1 %collective-permute-start.6 = (bf16[256,512]{1,0:T(8,128)(2,1)S(1)}, bf16[256,512]{1,0:T(8,128)(2,1)S(1)}, u32[]{:S(2)}, u32[]{:S(2)}) collective-permute-start(bf16[256,512]{1,0:T(8,128)(2,1)S(1)} %collective-permute-done.5.refs_1_), channel_id=1, source_target_pairs={{1,2},{2,1},{5,6},{6,5},{9,10},{10,9},{13,14},{14,13},{17,18},{18,... | collective-permute-start | bytes 786440 | tf_op jit(solution)/shard_map/ppermute | solution.py:331
  95.5 14.9 %collective-permute-start.8 = (bf16[256,512]{1,0:T(8,128)(2,1)S(1)}, bf16[256,512]{1,0:T(8,128)(2,1)S(1)}, u32[]{:S(2)}, u32[]{:S(2)}) collective-permute-start(bf16[256,512]{1,0:T(8,128)(2,1)S(1)} %collective-permute-done.7.refs_4_), channel_id=1, source_target_pairs={{1,0},{2,3},{5,4},{6,7},{9,8},{10,11},{13,12},{14,15},{17,16},{18,... | collective-permute-start | bytes 786440 | tf_op jit(solution)/shard_map/ppermute | solution.py:332
  96.8 35.9 %collective-permute-start.20 = (bf16[512,768]{1,0:T(8,128)(2,1)S(1)}, bf16[512,768]{1,0:T(8,128)(2,1)S(1)}, u32[]{:S(2)}, u32[]{:S(2)}) collective-permute-start(bf16[512,768]{1,0:T(8,128)(2,1)S(1)} %collective-permute-done.16.refs_14_), channel_id=1, source_target_pairs={{0,16},{4,20},{8,24},{12,28},{16,0},{20,4},{24,8},{28,12},{1,17},{... | collective-permute-start | bytes 2359304 | tf_op jit(solution)/shard_map/ppermute | solution.py:300
  97.4 35.8 %collective-permute-start.27 = (bf16[768,512]{1,0:T(8,128)(2,1)S(1)}, bf16[768,512]{1,0:T(8,128)(2,1)S(1)}, u32[]{:S(2)}, u32[]{:S(2)}) collective-permute-start(bf16[768,512]{1,0:T(8,128)(2,1)S(1)} %collective-permute-done.25.refs_24_), channel_id=1, source_target_pairs={{0,8},{4,12},{8,0},{12,4},{16,24},{20,28},{24,16},{28,20},{1,9},{5... | collective-permute-start | bytes 2359304 | tf_op jit(solution)/shard_map/ppermute | solution.py:300
  98.9 34.4 %collective-permute-start.17 = (bf16[512,768]{1,0:T(8,128)(2,1)S(1)}, bf16[512,768]{1,0:T(8,128)(2,1)S(1)}, u32[]{:S(2)}, u32[]{:S(2)}) collective-permute-start(bf16[512,768]{1,0:T(8,128)(2,1)S(1)} %collective-permute-done.16.refs_14_), channel_id=1, source_target_pairs={{0,4},{4,0},{8,12},{12,8},{16,20},{20,16},{24,28},{28,24},{1,5},{5... | collective-permute-start | bytes 2359304 | tf_op jit(solution)/shard_map/ppermute | solution.py:300
  98.9 12.8 %collective-permute-start.11 = (bf16[256,512]{1,0:T(8,128)(2,1)S(1)}, bf16[256,512]{1,0:T(8,128)(2,1)S(1)}, u32[]{:S(2)}, u32[]{:S(2)}) collective-permute-start(bf16[256,512]{1,0:T(8,128)(2,1)S(1)} %collective-permute-done.10.refs_7_), channel_id=1, source_target_pairs={{1,2},{2,1},{5,6},{6,5},{9,10},{10,9},{13,14},{14,13},{17,18},{18,... | collective-permute-start | bytes 786440 | tf_op jit(solution)/shard_map/ppermute | solution.py:331
  110.4 11.8 %collective-permute-start.13 = (bf16[256,512]{1,0:T(8,128)(2,1)S(1)}, bf16[256,512]{1,0:T(8,128)(2,1)S(1)}, u32[]{:S(2)}, u32[]{:S(2)}) collective-permute-start(bf16[256,512]{1,0:T(8,128)(2,1)S(1)} %collective-permute-done.12.refs_10_), channel_id=1, source_target_pairs={{1,0},{2,3},{5,4},{6,7},{9,8},{10,11},{13,12},{14,15},{17,16},{18,... | collective-permute-start | bytes 786440 | tf_op jit(solution)/shard_map/ppermute | solution.py:332
  111.7 18.1 %collective-permute-start.9 = (bf16[256,512]{1,0:T(8,128)(2,1)S(1)}, bf16[256,512]{1,0:T(8,128)(2,1)S(1)}, u32[]{:S(2)}, u32[]{:S(2)}) collective-permute-start(bf16[256,512]{1,0:T(8,128)(2,1)S(1)} %collective-permute-done.6.refs_2_), channel_id=1, source_target_pairs={{1,0},{2,3},{5,4},{6,7},{9,8},{10,11},{13,12},{14,15},{17,16},{18,... | collective-permute-start | bytes 786440 | tf_op jit(solution)/shard_map/ppermute | solution.py:333
  122.1 10.6 %collective-permute-start.14 = (bf16[256,512]{1,0:T(8,128)(2,1)S(1)}, bf16[256,512]{1,0:T(8,128)(2,1)S(1)}, u32[]{:S(2)}, u32[]{:S(2)}) collective-permute-start(bf16[256,512]{1,0:T(8,128)(2,1)S(1)} %collective-permute-done.11.refs_8_), channel_id=1, source_target_pairs={{1,0},{2,3},{5,4},{6,7},{9,8},{10,11},{13,12},{14,15},{17,16},{18,... | collective-permute-start | bytes 786440 | tf_op jit(solution)/shard_map/ppermute | solution.py:333
  129.8 4.0 %collective-permute-start.26 = (bf16[768,512]{1,0:T(8,128)(2,1)S(1)}, bf16[768,512]{1,0:T(8,128)(2,1)S(1)}, u32[]{:S(2)}, u32[]{:S(2)}) collective-permute-start(bf16[768,512]{1,0:T(8,128)(2,1)S(1)} %collective-permute-done.25.refs_24_), channel_id=1, source_target_pairs={{0,4},{4,0},{8,12},{12,8},{16,20},{20,16},{24,28},{28,24},{1,5},{5... | collective-permute-start | bytes 2359304 | tf_op jit(solution)/shard_map/ppermute | solution.py:300
  132.7 2.3 %collective-permute-start.19 = (bf16[512,768]{1,0:T(8,128)(2,1)S(1)}, bf16[512,768]{1,0:T(8,128)(2,1)S(1)}, u32[]{:S(2)}, u32[]{:S(2)}) collective-permute-start(bf16[512,768]{1,0:T(8,128)(2,1)S(1)} %collective-permute-done.18.refs_16_), channel_id=1, source_target_pairs={{0,4},{4,0},{8,12},{12,8},{16,20},{20,16},{24,28},{28,24},{1,5},{5... | collective-permute-start | bytes 2359304 | tf_op jit(solution)/shard_map/ppermute | solution.py:300
  132.7 3.4 %collective-permute-start.24 = (bf16[768,512]{1,0:T(8,128)(2,1)S(1)}, bf16[768,512]{1,0:T(8,128)(2,1)S(1)}, u32[]{:S(2)}, u32[]{:S(2)}) collective-permute-start(bf16[768,512]{1,0:T(8,128)(2,1)S(1)} %collective-permute-done.23.refs_22_), channel_id=1, source_target_pairs={{0,4},{4,0},{8,12},{12,8},{16,20},{20,16},{24,28},{28,24},{1,5},{5... | collective-permute-start | bytes 2359304 | tf_op jit(solution)/shard_map/ppermute | solution.py:300
  133.2 4.0 %collective-permute-start.21 = (bf16[512,768]{1,0:T(8,128)(2,1)S(1)}, bf16[512,768]{1,0:T(8,128)(2,1)S(1)}, u32[]{:S(2)}, u32[]{:S(2)}) collective-permute-start(bf16[512,768]{1,0:T(8,128)(2,1)S(1)} %collective-permute-done.20.refs_18_), channel_id=1, source_target_pairs={{0,4},{4,0},{8,12},{12,8},{16,20},{20,16},{24,28},{28,24},{1,5},{5... | collective-permute-start | bytes 2359304 | tf_op jit(solution)/shard_map/ppermute | solution.py:300
  133.3 5.1 %collective-permute-start.28 = (bf16[768,512]{1,0:T(8,128)(2,1)S(1)}, bf16[768,512]{1,0:T(8,128)(2,1)S(1)}, u32[]{:S(2)}, u32[]{:S(2)}) collective-permute-start(bf16[768,512]{1,0:T(8,128)(2,1)S(1)} %collective-permute-done.27.refs_26_), channel_id=1, source_target_pairs={{0,4},{4,0},{8,12},{12,8},{16,20},{20,16},{24,28},{28,24},{1,5},{5... | collective-permute-start | bytes 2359304 | tf_op jit(solution)/shard_map/ppermute | solution.py:300
  143.6 10.7 %collective-permute-start.36 = (bf16[128,1024]{1,0:T(8,128)(2,1)S(1)}, bf16[128,1024]{1,0:T(8,128)(2,1)S(1)}, u32[]{:S(2)}, u32[]{:S(2)}) collective-permute-start(bf16[128,1024]{1,0:T(8,128)(2,1)S(1)} %get-tuple-element.30), channel_id=1, source_target_pairs={{0,1},{3,2},{4,5},{7,6},{8,9},{11,10},{12,13},{15,14},{16,17},{19,... | collective-permute-start | bytes 786440 | tf_op jit(solution)/shard_map/ppermute | solution.py:344
  150.4 8.0 %collective-permute-start.31 = (bf16[128,1024]{1,0:T(8,128)(2,1)S(1)}, bf16[128,1024]{1,0:T(8,128)(2,1)S(1)}, u32[]{:S(2)}, u32[]{:S(2)}) collective-permute-start(bf16[128,1024]{1,0:T(8,128)(2,1)S(1)} %get-tuple-element.26), channel_id=1, source_target_pairs={{0,1},{3,2},{4,5},{7,6},{8,9},{11,10},{12,13},{15,14},{16,17},{19,... | collective-permute-start | bytes 786440 | tf_op jit(solution)/shard_map/ppermute | solution.py:344
  151.7 12.3 %collective-permute-start.34 = (bf16[128,1024]{1,0:T(8,128)(2,1)S(1)}, bf16[128,1024]{1,0:T(8,128)(2,1)S(1)}, u32[]{:S(2)}, u32[]{:S(2)}) collective-permute-start(bf16[128,1024]{1,0:T(8,128)(2,1)S(1)} %get-tuple-element.31), channel_id=1, source_target_pairs={{0,1},{3,2},{4,5},{7,6},{8,9},{11,10},{12,13},{15,14},{16,17},{19,... | collective-permute-start | bytes 786440 | tf_op jit(solution)/shard_map/ppermute | solution.py:345
  153.0 15.9 %collective-permute-start.29 = (bf16[128,1024]{1,0:T(8,128)(2,1)S(1)}, bf16[128,1024]{1,0:T(8,128)(2,1)S(1)}, u32[]{:S(2)}, u32[]{:S(2)}) collective-permute-start(bf16[128,1024]{1,0:T(8,128)(2,1)S(1)} %get-tuple-element.27), channel_id=1, source_target_pairs={{0,1},{3,2},{4,5},{7,6},{8,9},{11,10},{12,13},{15,14},{16,17},{19,... | collective-permute-start | bytes 786440 | tf_op jit(solution)/shard_map/ppermute | solution.py:345
  154.4 27.4 %copy-start.13 = (f32[1024]{0:T(1024)S(1)}, f32[1024]{0:T(1024)}, u32[]{:S(2)}) copy-start(f32[1024]{0:T(1024)} %param.25) | copy-start | bytes 12292
  154.4 20.2 %collective-permute-start.37 = (bf16[128,1024]{1,0:T(8,128)(2,1)S(1)}, bf16[128,1024]{1,0:T(8,128)(2,1)S(1)}, u32[]{:S(2)}, u32[]{:S(2)}) collective-permute-start(bf16[128,1024]{1,0:T(8,128)(2,1)S(1)} %add_convert_fusion.1), channel_id=1, source_target_pairs={{1,2},{2,1},{5,6},{6,5},{9,10},{10,9},{13,14},{14,13},{17,18},{18,... | collective-permute-start | bytes 786440 | tf_op jit(solution)/shard_map/ppermute | solution.py:346
  158.4 11.2 %collective-permute-start.32 = (bf16[128,1024]{1,0:T(8,128)(2,1)S(1)}, bf16[128,1024]{1,0:T(8,128)(2,1)S(1)}, u32[]{:S(2)}, u32[]{:S(2)}) collective-permute-start(bf16[128,1024]{1,0:T(8,128)(2,1)S(1)} %add_convert_fusion.4), channel_id=1, source_target_pairs={{1,2},{2,1},{5,6},{6,5},{9,10},{10,9},{13,14},{14,13},{17,18},{18,... | collective-permute-start | bytes 786440 | tf_op jit(solution)/shard_map/ppermute | solution.py:346
  164.1 20.0 %collective-permute-start.35 = (bf16[128,1024]{1,0:T(8,128)(2,1)S(1)}, bf16[128,1024]{1,0:T(8,128)(2,1)S(1)}, u32[]{:S(2)}, u32[]{:S(2)}) collective-permute-start(bf16[128,1024]{1,0:T(8,128)(2,1)S(1)} %add_convert_fusion.2), channel_id=1, source_target_pairs={{1,2},{2,1},{5,6},{6,5},{9,10},{10,9},{13,14},{14,13},{17,18},{18,... | collective-permute-start | bytes 786440 | tf_op jit(solution)/shard_map/ppermute | solution.py:347
  169.0 5.9 %collective-permute-start.30 = (bf16[128,1024]{1,0:T(8,128)(2,1)S(1)}, bf16[128,1024]{1,0:T(8,128)(2,1)S(1)}, u32[]{:S(2)}, u32[]{:S(2)}) collective-permute-start(bf16[128,1024]{1,0:T(8,128)(2,1)S(1)} %add_convert_fusion.5), channel_id=1, source_target_pairs={{1,2},{2,1},{5,6},{6,5},{9,10},{10,9},{13,14},{14,13},{17,18},{18,... | collective-permute-start | bytes 786440 | tf_op jit(solution)/shard_map/ppermute | solution.py:347
  169.7 12.1 %collective-permute-start.33 = (bf16[128,1024]{1,0:T(8,128)(2,1)S(1)}, bf16[128,1024]{1,0:T(8,128)(2,1)S(1)}, u32[]{:S(2)}, u32[]{:S(2)}) collective-permute-start(bf16[128,1024]{1,0:T(8,128)(2,1)S(1)} %add_convert_fusion.3), channel_id=1, source_target_pairs={{0,1},{1,0},{2,3},{3,2},{4,5},{5,4},{6,7},{7,6},{8,9},{9,8},{10,11... | collective-permute-start | bytes 786440 | tf_op jit(solution)/shard_map/ppermute | solution.py:300
  174.7 11.1 %collective-permute-start.38 = (bf16[128,1024]{1,0:T(8,128)(2,1)S(1)}, bf16[128,1024]{1,0:T(8,128)(2,1)S(1)}, u32[]{:S(2)}, u32[]{:S(2)}) collective-permute-start(bf16[128,1024]{1,0:T(8,128)(2,1)S(1)} %add_convert_fusion), channel_id=1, source_target_pairs={{0,1},{1,0},{2,3},{3,2},{4,5},{5,4},{6,7},{7,6},{8,9},{9,8},{10,11... | collective-permute-start | bytes 786440 | tf_op jit(solution)/shard_map/ppermute | solution.py:300

commit v4 on v3

--- a/solution.py
+++ b/solution.py
@@ -108,7 +108,8 @@
     scores = jnp.where(same & (row >= col), scores, 0.0).astype(BF16)
     place = iota((heads, span), 1)
     g = g_ref[...].astype(F32)
-    gate = g / (1.0 + jnp.exp(-g))
+    gate = 0.5 * g
+    gate = gate + gate * jnp.tanh(gate)
     for part in range(span // SUB):
         lo = part * SUB
         hi = lo + SUB
@@ -123,9 +124,9 @@
         hs[...] = head_out * (mid + contract0(b[lo:hi], xv[lo:hi]))
         mid_growth = head_in * gr[0:1, :]
         gr[...] = jnp.broadcast_to(head_out * mid_growth, gr.shape)
-        u_part = u_wide[lo:hi]
-        a_ref[lo:hi, :] = (u_part * acc + skip * x[lo:hi]) * gate[lo:hi]
-        w_ref[lo:hi, :] = (u_part * mid_growth * gate[lo:hi]).astype(BF16)
+        u_gate = u_wide[lo:hi] * gate[lo:hi]
+        a_ref[lo:hi, :] = (u_gate * acc + skip * x[lo:hi] * gate[lo:hi]).astype(BF16)
+        w_ref[lo:hi, :] = (u_gate * mid_growth).astype(BF16)
 
 
 def turned(row):
@@ -193,7 +194,7 @@
     for k in range(0, half, group):
         for r in range(0, span, 128):
             handed = jnp.dot(c_ref[r : r + 128, :], start[:, k : k + group], preferred_element_type=F32)
-            t = a_ref[r : r + 128, k : k + group] + w_ref[r : r + 128, k : k + group].astype(F32) * handed
+            t = a_ref[r : r + 128, k : k + group].astype(F32) + w_ref[r : r + 128, k : k + group].astype(F32) * handed
             mean = jnp.dot((t * t).astype(BF16), mean_of, preferred_element_type=F32)
             normed = t * lax.rsqrt(mean + 1e-05) * gain_ref[:, k : k + group]
             n_ref[r : r + 128, k : k + group] = normed.astype(BF16)
@@ -401,7 +402,7 @@
         out_specs=whole((states + 16, chans)),
         out_shape=jax.ShapeDtypeStruct((states + 16, chans), BF16),
         scratch_shapes=[pltpu.VMEM((states, chans), F32), pltpu.VMEM((8, chans), F32)],
-        compiler_params=params(),
+        compiler_params=params(60),
         name="end_state",
     )(mixer_input, state_input, step_size, decay_log, scale_exponent)
 
@@ -428,9 +429,9 @@
         in_specs=[rows_spec(blk, chans), rows_spec(blk, chans), rows_spec(blk, states), rows_spec(blk, states),
                   cols_spec(heads, blk), cols_spec(heads, blk), whole(scale_exponent.shape), whole((1, heads))],
         out_specs=[rows_spec(blk, chans), rows_spec(blk, chans)],
-        out_shape=[jax.ShapeDtypeStruct((tokens, chans), F32), jax.ShapeDtypeStruct((tokens, chans), BF16)],
+        out_shape=[jax.ShapeDtypeStruct((tokens, chans), BF16)] * 2,
         scratch_shapes=[pltpu.VMEM((states, chans), F32), pltpu.VMEM((8, chans), F32)],
-        compiler_params=params(),
+        compiler_params=params(48),
         name="local_out",
     )(mixer_input, gate_input, state_input, state_output, step_size, decay_log, scale_exponent,
       skip_gain[None])

time: 190 us -> 183 us (0.963)
  local copies, waits for them, and re-layouts: 8.32 us -> 1.01 us
    unnamed x36 -> x24, local copies, waits for them, and re-layouts: 8.32 us -> 1.01 us
    pallas_call x1, Pallas kernels: 3.65 us -> 5.73 us  [body(): pl.pallas_call(functools.partial(end_kernel, blk=blk), grid=(tokens // sp...]
where the time goes in v4:
time: 183 us; the launch traced here: 182 us
  waiting for transfers between devices  101 us (55%)
  starting transfers between devices  40.9 us (22%)
  Pallas kernels  38.2 us (21%)
    ppermute x23, waiting for transfers between devices, swap(): return lax.ppermute(value, axis, [(i, i ^ mask) for i in range(count)])  59.8 us
    ppermute x23, starting transfers between devices, swap(): return lax.ppermute(value, axis, [(i, i ^ mask) for i in range(count)])  24.9 us
    ppermute x2, waiting for transfers between devices, gather_line(): out_near = lax.ppermute(cross, 'exp', OUTWARD)  19.8 us
    pallas_call x1, Pallas kernels, body(): pl.pallas_call(functools.partial(local_kernel, blk=blk), grid=(tokens //...  10.8 us
    pallas_call x2, Pallas kernels, body(): pl.pallas_call(functools.partial(expert_kernel, ring=ring, shards=ctx, gr...  10.5 us
    ppermute x2, waiting for transfers between devices, gather_line(): out_far = lax.ppermute(cross_far, 'exp', OUTWARD)  9.23 us
    ppermute x2, waiting for transfers between devices, sum_line(): near = lax.ppermute(terms[2], 'exp', ENDS)  8.98 us
    pallas_call x1, Pallas kernels, body(): pl.pallas_call(functools.partial(end_kernel, blk=blk), grid=(tokens // sp...  5.73 us
  transfers between devices with their start and end apart: 39, of which 18 were waited for; matrix products, arithmetic and copies ran while one was open for 0% of the time, Pallas kernels for 13%

profile of v4, /device:TPU:0, one launch (start us, length us, event | category | flops | bytes accessed | tf_op | source)
XLA Modules:
  0.0 182.0 jit_solution(2447963110097396800)
XLA Ops:
  0.0 5.7 %end_state.1.own_ref = bf16[144,1024]{1,0:T(8,128)(2,1)} custom-call(bf16[1024,1024]{1,0:T(8,128)(2,1)} %x_ref.3, bf16[1024,128]{1,0:T(8,128)(2,1)} %b_ref.3, f32[16,1024]{1,0:T(8,128)} %st_ref.3, f32[16,1024]{1,0:T(8,128)} %dl_ref.3, s32[8,16]{1,0:T(8,128)} %sc_ref.3), custom_call_target="tpu_custom_call" | custom-call | tf_op jit(solution)/shard_map/end_state/pallas_call | solution.py:397
  5.8 0.5 collective-permute-start
  6.3 2.5 %collective-permute-start.16 = (bf16[512,768]{1,0:T(8,128)(2,1)S(1)}, bf16[512,768]{1,0:T(8,128)(2,1)S(1)}, u32[]{:S(2)}, u32[]{:S(2)}) collective-permute-start(bf16[512,768]{1,0:T(8,128)(2,1)S(1)} %copy-done), channel_id=1, source_target_pairs={{0,8},{4,12},{8,0},{12,4},{16,24},{20,28},{24,16},{28,20},{1,9},{5... | collective-permute-start | bytes 2359304 | tf_op jit(solution)/shard_map/ppermute | solution.py:301
  8.8 1.0 copy-done.3
  9.8 0.1 chip_state.1
  9.9 1.8 collective-permute-start.1
  11.6 1.5 collective-permute-start.2
  13.2 0.3 collective-permute-start.3
  13.4 17.0 %collective-permute-done.1.refs_0_ = bf16[144,512]{1,0:T(8,128)(2,1)S(1)} collective-permute-done((bf16[144,512]{1,0:T(8,128)(2,1)S(1)}, bf16[144,512]{1,0:T(8,128)(2,1)S(1)}, u32[]{:S(2)}, u32[]{:S(2)}) %collective-permute-start.1) | collective-permute-done | bytes 147488 | tf_op jit(solution)/shard_map/ppermute | solution.py:301
  30.4 4.1 %collective-permute-done.3.refs_2_ = bf16[144,512]{1,0:T(8,128)(2,1)S(1)} collective-permute-done((bf16[144,512]{1,0:T(8,128)(2,1)S(1)}, bf16[144,512]{1,0:T(8,128)(2,1)S(1)}, u32[]{:S(2)}, u32[]{:S(2)}) %collective-permute-start.3) | collective-permute-done | bytes 147488 | tf_op jit(solution)/shard_map/ppermute | solution.py:301
  34.5 0.1 prior.1.h_ref
  34.6 0.1 collective-permute-start.4
  34.8 10.8 %local_out.1 = (bf16[1024,1024]{1,0:T(8,128)(2,1)S(1)}, bf16[1024,1024]{1,0:T(8,128)(2,1)S(1)}) custom-call(bf16[1024,1024]{1,0:T(8,128)(2,1)} %x_ref.3, bf16[1024,1024]{1,0:T(8,128)(2,1)} %g_ref.1, bf16[1024,128]{1,0:T(8,128)(2,1)S(1)} %copy-done.4, bf16[1024,128]{1,0:T(8,128)(2,1)S(1)} %copy-done.2, f32[16,1024]{1,0:T(8,128)S(1)} %copy-done.5, ...), custom_call_target="tpu_custom_call" | custom-call | tf_op jit(solution)/shard_map/local_out/pallas_call | solution.py:426
  45.6 2.8 %shard_map.127 = (bf16[1024,512]{1,0:T(8,128)(2,1)S(1)}, bf16[256,512]{1,0:T(8,128)(2,1)S(1)}) custom-call(s32[1]{0:T(128)} %bitcast.flip_ref, bf16[1024,128]{1,0:T(8,128)(2,1)S(1)} %copy-done.2, bf16[1024,1024]{1,0:T(8,128)(2,1)S(1)} %get-tuple-element.19.a_ref, bf16[1024,1024]{1,0:T(8,128)(2,1)S(1)} %get-tuple-element.20.w_ref, f32[1,1024]{1,0:T(1,128)S(1)} %bitcast.9, ...), custom_call_target="tpu_custom_call" | custom-call | tf_op jit(solution)/shard_map/pallas_call | solution.py:455
  48.4 1.6 collective-permute-start.5
  50.1 0.7 collective-permute-start.7
  50.8 0.5 collective-permute-start.25
  51.3 1.6 collective-permute-start.18
  52.8 4.3 %collective-permute-done.5.refs_1_ = bf16[256,512]{1,0:T(8,128)(2,1)S(1)} collective-permute-done((bf16[256,512]{1,0:T(8,128)(2,1)S(1)}, bf16[256,512]{1,0:T(8,128)(2,1)S(1)}, u32[]{:S(2)}, u32[]{:S(2)}) %collective-permute-start.5) | collective-permute-done | bytes 262176 | tf_op jit(solution)/shard_map/ppermute | solution.py:301
  57.1 1.5 collective-permute-start.23
  58.6 0.5 collective-permute-start.22
  59.1 2.7 %shard_map.128 = (bf16[1024,512]{1,0:T(8,128)(2,1)S(1)}, bf16[256,512]{1,0:T(8,128)(2,1)S(1)}) custom-call(s32[1]{0:T(128)} %bitcast.flip_ref, bf16[1024,128]{1,0:T(8,128)(2,1)S(1)} %copy-done.2, bf16[1024,1024]{1,0:T(8,128)(2,1)S(1)} %get-tuple-element.19.a_ref, bf16[1024,1024]{1,0:T(8,128)(2,1)S(1)} %get-tuple-element.20.w_ref, f32[1,1024]{1,0:T(1,128)S(1)} %bitcast.10, ...), custom_call_target="tpu_custom_call" | custom-call | tf_op jit(solution)/shard_map/pallas_call | solution.py:455
  61.9 9.4 %collective-permute-done.25.refs_24_ = bf16[768,512]{1,0:T(8,128)(2,1)S(1)} collective-permute-done((bf16[768,512]{1,0:T(8,128)(2,1)S(1)}, bf16[768,512]{1,0:T(8,128)(2,1)S(1)}, u32[]{:S(2)}, u32[]{:S(2)}) %collective-permute-start.25) | collective-permute-done | bytes 786464 | tf_op jit(solution)/shard_map/ppermute | solution.py:301
  71.2 4.4 %collective-permute-start.10 = (bf16[256,512]{1,0:T(8,128)(2,1)S(1)}, bf16[256,512]{1,0:T(8,128)(2,1)S(1)}, u32[]{:S(2)}, u32[]{:S(2)}) collective-permute-start(bf16[256,512]{1,0:T(8,128)(2,1)S(1)} %get-tuple-element.24.refs_6_), channel_id=1, source_target_pairs={{0,1},{1,0},{2,3},{3,2},{4,5},{5,4},{6,7},{7,6},{8,9},{9,8},{10,11... | collective-permute-start | bytes 786440 | tf_op jit(solution)/shard_map/ppermute | solution.py:301
  75.6 11.6 %collective-permute-done.18.refs_16_ = bf16[512,768]{1,0:T(8,128)(2,1)S(1)} collective-permute-done((bf16[512,768]{1,0:T(8,128)(2,1)S(1)}, bf16[512,768]{1,0:T(8,128)(2,1)S(1)}, u32[]{:S(2)}, u32[]{:S(2)}) %collective-permute-start.18) | collective-permute-done | bytes 786464 | tf_op jit(solution)/shard_map/ppermute | solution.py:301
  87.2 0.7 collective-permute-start.12
  87.9 0.7 collective-permute-start.6
  88.6 1.3 collective-permute-start.8
  89.9 0.6 collective-permute-start.20
  90.6 1.4 collective-permute-start.27
  92.0 0.7 collective-permute-start.11
  92.7 10.7 %collective-permute-done.8.refs_3_ = bf16[256,512]{1,0:T(8,128)(2,1)S(1)} collective-permute-done((bf16[256,512]{1,0:T(8,128)(2,1)S(1)}, bf16[256,512]{1,0:T(8,128)(2,1)S(1)}, u32[]{:S(2)}, u32[]{:S(2)}) %collective-permute-start.8) | collective-permute-done | bytes 262176 | tf_op jit(solution)/shard_map/ppermute | solution.py:333
  103.4 1.3 collective-permute-start.13
  104.7 1.3 collective-permute-start.9
  106.0 9.1 %collective-permute-done.13.refs_9_ = bf16[256,512]{1,0:T(8,128)(2,1)S(1)} collective-permute-done((bf16[256,512]{1,0:T(8,128)(2,1)S(1)}, bf16[256,512]{1,0:T(8,128)(2,1)S(1)}, u32[]{:S(2)}, u32[]{:S(2)}) %collective-permute-start.13) | collective-permute-done | bytes 262176 | tf_op jit(solution)/shard_map/ppermute | solution.py:333
  115.1 1.3 collective-permute-start.14
  116.4 6.3 %collective-permute-done.9.refs_5_ = bf16[256,512]{1,0:T(8,128)(2,1)S(1)} collective-permute-done((bf16[256,512]{1,0:T(8,128)(2,1)S(1)}, bf16[256,512]{1,0:T(8,128)(2,1)S(1)}, u32[]{:S(2)}, u32[]{:S(2)}) %collective-permute-start.9) | collective-permute-done | bytes 262176 | tf_op jit(solution)/shard_map/ppermute | solution.py:334
  122.7 2.9 %collective-permute-done.14.refs_11_ = bf16[256,512]{1,0:T(8,128)(2,1)S(1)} collective-permute-done((bf16[256,512]{1,0:T(8,128)(2,1)S(1)}, bf16[256,512]{1,0:T(8,128)(2,1)S(1)}, u32[]{:S(2)}, u32[]{:S(2)}) %collective-permute-start.14) | collective-permute-done | bytes 262176 | tf_op jit(solution)/shard_map/ppermute | solution.py:334
  125.7 0.5 collective-permute-start.24
  126.2 0.1 collective-permute-start.21
  126.2 0.4 collective-permute-start.28
  126.7 1.2 collective-permute-done.19.refs_17_
  127.9 1.1 collective-permute-done.24.refs_23_
  129.1 1.1 collective-permute-done.21.refs_19_
  130.2 1.1 collective-permute-done.28.refs_27_
  131.3 5.2 %shard_map.131 = (bf16[128,1024]{1,0:T(8,128)(2,1)S(1)}, bf16[128,1024]{1,0:T(8,128)(2,1)S(1)}, bf16[128,1024]{1,0:T(8,128)(2,1)S(1)}, bf16[128,1024]{1,0:T(8,128)(2,1)S(1)}) custom-call(s32[1]{0:T(128)} %bitcast.flip_ref, bf16[256,512]{1,0:T(8,128)(2,1)S(1)} %get-tuple-element.23.refs_0_, bf16[256,512]{1,0:T(8,128)(2,1)S(1)} %collective-permute-done.5.refs_1_, ...), custom_call_target="tpu_custom_call" | custom-call | tf_op jit(solution)/shard_map/pallas_call | solution.py:485
  136.6 1.5 collective-permute-start.36
  138.0 5.3 %shard_map.129 = (bf16[128,1024]{1,0:T(8,128)(2,1)S(1)}, bf16[128,1024]{1,0:T(8,128)(2,1)S(1)}, bf16[128,1024]{1,0:T(8,128)(2,1)S(1)}, bf16[128,1024]{1,0:T(8,128)(2,1)S(1)}) custom-call(s32[1]{0:T(128)} %bitcast.flip_ref, bf16[256,512]{1,0:T(8,128)(2,1)S(1)} %get-tuple-element.23.refs_0_, bf16[256,512]{1,0:T(8,128)(2,1)S(1)} %collective-permute-done.5.refs_1_, ...), custom_call_target="tpu_custom_call" | custom-call | tf_op jit(solution)/shard_map/pallas_call | solution.py:485
  143.3 1.3 collective-permute-start.31
  144.7 1.3 collective-permute-start.34
  146.0 1.3 collective-permute-start.29
  147.4 0.7 collective-permute-start.37
  148.1 3.3 %collective-permute-done.31 = bf16[128,1024]{1,0:T(8,128)(2,1)S(1)} collective-permute-done((bf16[128,1024]{1,0:T(8,128)(2,1)S(1)}, bf16[128,1024]{1,0:T(8,128)(2,1)S(1)}, u32[]{:S(2)}, u32[]{:S(2)}) %collective-permute-start.31) | collective-permute-done | bytes 262176 | tf_op jit(solution)/shard_map/ppermute | solution.py:345
  151.4 0.7 collective-permute-start.32
  152.1 4.9 %collective-permute-done.34 = bf16[128,1024]{1,0:T(8,128)(2,1)S(1)} collective-permute-done((bf16[128,1024]{1,0:T(8,128)(2,1)S(1)}, bf16[128,1024]{1,0:T(8,128)(2,1)S(1)}, u32[]{:S(2)}, u32[]{:S(2)}) %collective-permute-start.34) | collective-permute-done | bytes 262176 | tf_op jit(solution)/shard_map/ppermute | solution.py:346
  157.0 0.7 collective-permute-start.35
  157.7 4.1 %collective-permute-done.29 = bf16[128,1024]{1,0:T(8,128)(2,1)S(1)} collective-permute-done((bf16[128,1024]{1,0:T(8,128)(2,1)S(1)}, bf16[128,1024]{1,0:T(8,128)(2,1)S(1)}, u32[]{:S(2)}, u32[]{:S(2)}) %collective-permute-start.29) | collective-permute-done | bytes 262176 | tf_op jit(solution)/shard_map/ppermute | solution.py:346
  161.9 0.7 collective-permute-start.30
  162.7 5.0 %collective-permute-start.33 = (bf16[128,1024]{1,0:T(8,128)(2,1)S(1)}, bf16[128,1024]{1,0:T(8,128)(2,1)S(1)}, u32[]{:S(2)}, u32[]{:S(2)}) collective-permute-start(bf16[128,1024]{1,0:T(8,128)(2,1)S(1)} %add_convert_fusion.3), channel_id=1, source_target_pairs={{0,1},{1,0},{2,3},{3,2},{4,5},{5,4},{6,7},{7,6},{8,9},{9,8},{10,11... | collective-permute-start | bytes 786440 | tf_op jit(solution)/shard_map/ppermute | solution.py:301
  167.7 0.1 collective-permute-start.38
  167.8 7.0 %collective-permute-done.33.refs_4_ = bf16[128,1024]{1,0:T(8,128)(2,1)S(1)} collective-permute-done((bf16[128,1024]{1,0:T(8,128)(2,1)S(1)}, bf16[128,1024]{1,0:T(8,128)(2,1)S(1)}, u32[]{:S(2)}, u32[]{:S(2)}) %collective-permute-start.33) | collective-permute-done | bytes 262176 | tf_op jit(solution)/shard_map/ppermute | solution.py:301
  174.8 2.2 %shard_map.130.refs_0_ = bf16[1024,1024]{1,0:T(8,128)(2,1)S(1)} custom-call(s32[1]{0:T(128)} %bitcast.flip_ref, s32[1,1024]{1,0:T(1,128)S(1)} %bitcast.7, f32[1,1024]{1,0:T(1,128)S(1)} %bitcast.11, bf16[1024,512]{1,0:T(8,128)(2,1)S(1)} %get-tuple-element.21.refs_0_, bf16[1024,512]{1,0:T(8,128)(2,1)S(1)} %get-tuple-element.22.refs_1_, ...), custom_call_target="tpu_custom_call" | custom-call | tf_op jit(solution)/shard_map/pallas_call | solution.py:507
  177.0 1.8 %collective-permute-done.38.refs_3_ = bf16[128,1024]{1,0:T(8,128)(2,1)S(1)} collective-permute-done((bf16[128,1024]{1,0:T(8,128)(2,1)S(1)}, bf16[128,1024]{1,0:T(8,128)(2,1)S(1)}, u32[]{:S(2)}, u32[]{:S(2)}) %collective-permute-start.38) | collective-permute-done | bytes 262176 | tf_op jit(solution)/shard_map/ppermute | solution.py:301
  178.8 3.2 %shard_map.132 = bf16[1024,1024]{1,0:T(8,128)(2,1)} custom-call(s32[1]{0:T(128)} %bitcast.flip_ref, s32[1,1024]{1,0:T(1,128)S(1)} %bitcast.8, f32[1,1024]{1,0:T(1,128)S(1)} %bitcast.12, bf16[1024,1024]{1,0:T(8,128)(2,1)S(1)} %shard_map.130.refs_0_, bf16[128,1024]{1,0:T(8,128)(2,1)S(1)} %get-tuple-element.29.refs_1_, ...), custom_call_target="tpu_custom_call" | custom-call | tf_op jit(solution)/shard_map/pallas_call | solution.py:507
  (54 shorter events, 0.5 us)
Async XLA Ops:
  0.0 34.7 %copy-start.10 = (s32[8,16]{1,0:T(8,128)S(1)}, s32[8,16]{1,0:T(8,128)}, u32[]{:S(2)}) copy-start(s32[8,16]{1,0:T(8,128)} %sc_ref.3) | copy-start | bytes 1540
  0.0 34.7 %copy-start.5 = (f32[16,1024]{1,0:T(8,128)S(1)}, f32[16,1024]{1,0:T(8,128)}, u32[]{:S(2)}) copy-start(f32[16,1024]{1,0:T(8,128)} %st_ref.3) | copy-start | bytes 196612
  0.0 34.7 %copy-start.6 = (f32[16,1024]{1,0:T(8,128)S(1)}, f32[16,1024]{1,0:T(8,128)}, u32[]{:S(2)}) copy-start(f32[16,1024]{1,0:T(8,128)} %dl_ref.3) | copy-start | bytes 196612
  0.0 34.7 %copy-start.4 = (bf16[1024,128]{1,0:T(8,128)(2,1)S(1)}, bf16[1024,128]{1,0:T(8,128)(2,1)}, u32[]{:S(2)}) copy-start(bf16[1024,128]{1,0:T(8,128)(2,1)} %b_ref.3) | copy-start | bytes 786436
  0.0 6.3 %copy-start = (bf16[512,768]{1,0:T(8,128)(2,1)S(1)}, bf16[512,768]{1,0:T(8,128)(2,1)}, u32[]{:S(2)}) copy-start(bf16[512,768]{1,0:T(8,128)(2,1)} %refs_12_.3) | copy-start | bytes 2359300
  0.0 34.7 %copy-start.11 = (f32[16]{0:T(128)S(1)}, f32[16]{0:T(128)}, u32[]{:S(2)}) copy-start(f32[16]{0:T(128)} %param.19) | copy-start | bytes 196
  0.0 34.7 %copy-start.2 = (bf16[1024,128]{1,0:T(8,128)(2,1)S(1)}, bf16[1024,128]{1,0:T(8,128)(2,1)}, u32[]{:S(2)}) copy-start(bf16[1024,128]{1,0:T(8,128)(2,1)} %c_ref.5) | copy-start | bytes 786436
  5.8 3.1 %collective-permute-start = (bf16[144,1024]{1,0:T(8,128)(2,1)}, bf16[144,1024]{1,0:T(8,128)(2,1)S(1)}, u32[]{:S(2)}, u32[]{:S(2)}) collective-permute-start(bf16[144,1024]{1,0:T(8,128)(2,1)} %end_state.1.own_ref), channel_id=1, source_target_pairs={{0,4},{4,0},{8,12},{12,8},{16,20},{20,16},{24,28},{28,24},{1,5},{5... | collective-permute-start | bytes 884744 | tf_op jit(solution)/shard_map/ppermute | solution.py:301
  6.3 52.3 %collective-permute-start.16 = (bf16[512,768]{1,0:T(8,128)(2,1)S(1)}, bf16[512,768]{1,0:T(8,128)(2,1)S(1)}, u32[]{:S(2)}, u32[]{:S(2)}) collective-permute-start(bf16[512,768]{1,0:T(8,128)(2,1)S(1)} %copy-done), channel_id=1, source_target_pairs={{0,8},{4,12},{8,0},{12,4},{16,24},{20,28},{24,16},{28,20},{1,9},{5... | collective-permute-start | bytes 2359304 | tf_op jit(solution)/shard_map/ppermute | solution.py:301
  8.8 1.0 copy-start.3
  9.9 20.5 %collective-permute-start.1 = (bf16[144,512]{1,0:T(8,128)(2,1)S(1)}, bf16[144,512]{1,0:T(8,128)(2,1)S(1)}, u32[]{:S(2)}, u32[]{:S(2)}) collective-permute-start(bf16[144,512]{1,0:T(8,128)(2,1)S(1)} %chip_state.1), channel_id=1, source_target_pairs={{0,8},{4,12},{8,0},{12,4},{16,24},{20,28},{24,16},{28,20},{1,9},{5... | collective-permute-start | bytes 442376 | tf_op jit(solution)/shard_map/ppermute | solution.py:301
  11.6 18.7 %collective-permute-start.2 = (bf16[144,512]{1,0:T(8,128)(2,1)S(1)}, bf16[144,512]{1,0:T(8,128)(2,1)S(1)}, u32[]{:S(2)}, u32[]{:S(2)}) collective-permute-start(bf16[144,512]{1,0:T(8,128)(2,1)S(1)} %chip_state.1), channel_id=1, source_target_pairs={{0,16},{4,20},{8,24},{12,28},{16,0},{20,4},{24,8},{28,12},{1,17},{... | collective-permute-start | bytes 442376 | tf_op jit(solution)/shard_map/ppermute | solution.py:301
  13.2 21.3 %collective-permute-start.3 = (bf16[144,512]{1,0:T(8,128)(2,1)S(1)}, bf16[144,512]{1,0:T(8,128)(2,1)S(1)}, u32[]{:S(2)}, u32[]{:S(2)}) collective-permute-start(bf16[144,512]{1,0:T(8,128)(2,1)S(1)} %chip_state.1), channel_id=1, source_target_pairs={{0,24},{4,28},{8,16},{12,20},{16,8},{20,12},{24,0},{28,4},{1,25},{... | collective-permute-start | bytes 442376 | tf_op jit(solution)/shard_map/ppermute | solution.py:301
  34.6 16.7 %collective-permute-start.4 = (bf16[128,512]{1,0:T(8,128)(2,1)S(1)}, bf16[128,512]{1,0:T(8,128)(2,1)S(1)}, u32[]{:S(2)}, u32[]{:S(2)}) collective-permute-start(bf16[128,512]{1,0:T(8,128)(2,1)S(1)} %prior.1.h_ref), channel_id=1, source_target_pairs={{0,4},{4,0},{8,12},{12,8},{16,20},{20,16},{24,28},{28,24},{1,5},{5... | collective-permute-start | bytes 393224 | tf_op jit(solution)/shard_map/ppermute | solution.py:301
  34.7 10.9 %copy-start.7 = (s32[1024]{0:T(1024)S(1)}, s32[1024]{0:T(1024)}, u32[]{:S(2)}) copy-start(s32[1024]{0:T(1024)} %param.24) | copy-start | bytes 12292
  34.8 10.9 %copy-start.8 = (f32[1024]{0:T(1024)S(1)}, f32[1024]{0:T(1024)}, u32[]{:S(2)}) copy-start(f32[1024]{0:T(1024)} %param.21) | copy-start | bytes 12292
  45.6 5.1 %copy-start.1 = (bf16[768,512]{1,0:T(8,128)(2,1)S(1)}, bf16[768,512]{1,0:T(8,128)(2,1)}, u32[]{:S(2)}) copy-start(bf16[768,512]{1,0:T(8,128)(2,1)} %refs_20_.3) | copy-start | bytes 2359300
  48.4 8.7 %collective-permute-start.5 = (bf16[256,512]{1,0:T(8,128)(2,1)S(1)}, bf16[256,512]{1,0:T(8,128)(2,1)S(1)}, u32[]{:S(2)}, u32[]{:S(2)}) collective-permute-start(bf16[256,512]{1,0:T(8,128)(2,1)S(1)} %get-tuple-element.23.refs_0_), channel_id=1, source_target_pairs={{0,1},{1,0},{2,3},{3,2},{4,5},{5,4},{6,7},{7,6},{8,9},{9,8},{10,11... | collective-permute-start | bytes 786440 | tf_op jit(solution)/shard_map/ppermute | solution.py:301
  50.1 8.5 %collective-permute-start.7 = (bf16[256,512]{1,0:T(8,128)(2,1)S(1)}, bf16[256,512]{1,0:T(8,128)(2,1)S(1)}, u32[]{:S(2)}, u32[]{:S(2)}) collective-permute-start(bf16[256,512]{1,0:T(8,128)(2,1)S(1)} %get-tuple-element.23.refs_0_), channel_id=1, source_target_pairs={{1,2},{2,1},{5,6},{6,5},{9,10},{10,9},{13,14},{14,13},{17,18},{18,... | collective-permute-start | bytes 786440 | tf_op jit(solution)/shard_map/ppermute | solution.py:331
  50.8 20.5 %collective-permute-start.25 = (bf16[768,512]{1,0:T(8,128)(2,1)S(1)}, bf16[768,512]{1,0:T(8,128)(2,1)S(1)}, u32[]{:S(2)}, u32[]{:S(2)}) collective-permute-start(bf16[768,512]{1,0:T(8,128)(2,1)S(1)} %copy-done.1), channel_id=1, source_target_pairs={{0,16},{4,20},{8,24},{12,28},{16,0},{20,4},{24,8},{28,12},{1,17},{... | collective-permute-start | bytes 2359304 | tf_op jit(solution)/shard_map/ppermute | solution.py:301
  51.3 36.0 %collective-permute-start.18 = (bf16[512,768]{1,0:T(8,128)(2,1)S(1)}, bf16[512,768]{1,0:T(8,128)(2,1)S(1)}, u32[]{:S(2)}, u32[]{:S(2)}) collective-permute-start(bf16[512,768]{1,0:T(8,128)(2,1)S(1)} %copy-done), channel_id=1, source_target_pairs={{0,16},{4,20},{8,24},{12,28},{16,0},{20,4},{24,8},{28,12},{1,17},{... | collective-permute-start | bytes 2359304 | tf_op jit(solution)/shard_map/ppermute | solution.py:301
  57.1 30.8 %collective-permute-start.23 = (bf16[768,512]{1,0:T(8,128)(2,1)S(1)}, bf16[768,512]{1,0:T(8,128)(2,1)S(1)}, u32[]{:S(2)}, u32[]{:S(2)}) collective-permute-start(bf16[768,512]{1,0:T(8,128)(2,1)S(1)} %copy-done.1), channel_id=1, source_target_pairs={{0,8},{4,12},{8,0},{12,4},{16,24},{20,28},{24,16},{28,20},{1,9},{5... | collective-permute-start | bytes 2359304 | tf_op jit(solution)/shard_map/ppermute | solution.py:301
  58.6 30.0 %collective-permute-start.15 = (bf16[512,768]{1,0:T(8,128)(2,1)S(1)}, bf16[512,768]{1,0:T(8,128)(2,1)S(1)}, u32[]{:S(2)}, u32[]{:S(2)}) collective-permute-start(bf16[512,768]{1,0:T(8,128)(2,1)S(1)} %copy-done), channel_id=1, source_target_pairs={{0,4},{4,0},{8,12},{12,8},{16,20},{20,16},{24,28},{28,24},{1,5},{5... | collective-permute-start | bytes 2359304 | tf_op jit(solution)/shard_map/ppermute | solution.py:301
  58.6 31.3 %collective-permute-start.22 = (bf16[768,512]{1,0:T(8,128)(2,1)S(1)}, bf16[768,512]{1,0:T(8,128)(2,1)S(1)}, u32[]{:S(2)}, u32[]{:S(2)}) collective-permute-start(bf16[768,512]{1,0:T(8,128)(2,1)S(1)} %copy-done.1), channel_id=1, source_target_pairs={{0,4},{4,0},{8,12},{12,8},{16,20},{20,16},{24,28},{28,24},{1,5},{5... | collective-permute-start | bytes 2359304 | tf_op jit(solution)/shard_map/ppermute | solution.py:301
  71.2 19.3 %collective-permute-start.10 = (bf16[256,512]{1,0:T(8,128)(2,1)S(1)}, bf16[256,512]{1,0:T(8,128)(2,1)S(1)}, u32[]{:S(2)}, u32[]{:S(2)}) collective-permute-start(bf16[256,512]{1,0:T(8,128)(2,1)S(1)} %get-tuple-element.24.refs_6_), channel_id=1, source_target_pairs={{0,1},{1,0},{2,3},{3,2},{4,5},{5,4},{6,7},{7,6},{8,9},{9,8},{10,11... | collective-permute-start | bytes 786440 | tf_op jit(solution)/shard_map/ppermute | solution.py:301
  87.2 4.8 %collective-permute-start.12 = (bf16[256,512]{1,0:T(8,128)(2,1)S(1)}, bf16[256,512]{1,0:T(8,128)(2,1)S(1)}, u32[]{:S(2)}, u32[]{:S(2)}) collective-permute-start(bf16[256,512]{1,0:T(8,128)(2,1)S(1)} %get-tuple-element.24.refs_6_), channel_id=1, source_target_pairs={{1,2},{2,1},{5,6},{6,5},{9,10},{10,9},{13,14},{14,13},{17,18},{18,... | collective-permute-start | bytes 786440 | tf_op jit(solution)/shard_map/ppermute | solution.py:331
  87.9 4.1 %collective-permute-start.6 = (bf16[256,512]{1,0:T(8,128)(2,1)S(1)}, bf16[256,512]{1,0:T(8,128)(2,1)S(1)}, u32[]{:S(2)}, u32[]{:S(2)}) collective-permute-start(bf16[256,512]{1,0:T(8,128)(2,1)S(1)} %collective-permute-done.5.refs_1_), channel_id=1, source_target_pairs={{1,2},{2,1},{5,6},{6,5},{9,10},{10,9},{13,14},{14,13},{17,18},{18,... | collective-permute-start | bytes 786440 | tf_op jit(solution)/shard_map/ppermute | solution.py:332
  88.6 14.8 %collective-permute-start.8 = (bf16[256,512]{1,0:T(8,128)(2,1)S(1)}, bf16[256,512]{1,0:T(8,128)(2,1)S(1)}, u32[]{:S(2)}, u32[]{:S(2)}) collective-permute-start(bf16[256,512]{1,0:T(8,128)(2,1)S(1)} %collective-permute-done.7.refs_4_), channel_id=1, source_target_pairs={{1,0},{2,3},{5,4},{6,7},{9,8},{10,11},{13,12},{14,15},{17,16},{18,... | collective-permute-start | bytes 786440 | tf_op jit(solution)/shard_map/ppermute | solution.py:333
  89.9 35.7 %collective-permute-start.20 = (bf16[512,768]{1,0:T(8,128)(2,1)S(1)}, bf16[512,768]{1,0:T(8,128)(2,1)S(1)}, u32[]{:S(2)}, u32[]{:S(2)}) collective-permute-start(bf16[512,768]{1,0:T(8,128)(2,1)S(1)} %collective-permute-done.16.refs_14_), channel_id=1, source_target_pairs={{0,16},{4,20},{8,24},{12,28},{16,0},{20,4},{24,8},{28,12},{1,17},{... | collective-permute-start | bytes 2359304 | tf_op jit(solution)/shard_map/ppermute | solution.py:301
  90.6 35.6 %collective-permute-start.27 = (bf16[768,512]{1,0:T(8,128)(2,1)S(1)}, bf16[768,512]{1,0:T(8,128)(2,1)S(1)}, u32[]{:S(2)}, u32[]{:S(2)}) collective-permute-start(bf16[768,512]{1,0:T(8,128)(2,1)S(1)} %collective-permute-done.25.refs_24_), channel_id=1, source_target_pairs={{0,8},{4,12},{8,0},{12,4},{16,24},{20,28},{24,16},{28,20},{1,9},{5... | collective-permute-start | bytes 2359304 | tf_op jit(solution)/shard_map/ppermute | solution.py:301
  92.0 34.2 %collective-permute-start.17 = (bf16[512,768]{1,0:T(8,128)(2,1)S(1)}, bf16[512,768]{1,0:T(8,128)(2,1)S(1)}, u32[]{:S(2)}, u32[]{:S(2)}) collective-permute-start(bf16[512,768]{1,0:T(8,128)(2,1)S(1)} %collective-permute-done.16.refs_14_), channel_id=1, source_target_pairs={{0,4},{4,0},{8,12},{12,8},{16,20},{20,16},{24,28},{28,24},{1,5},{5... | collective-permute-start | bytes 2359304 | tf_op jit(solution)/shard_map/ppermute | solution.py:301
  92.0 12.7 %collective-permute-start.11 = (bf16[256,512]{1,0:T(8,128)(2,1)S(1)}, bf16[256,512]{1,0:T(8,128)(2,1)S(1)}, u32[]{:S(2)}, u32[]{:S(2)}) collective-permute-start(bf16[256,512]{1,0:T(8,128)(2,1)S(1)} %collective-permute-done.10.refs_7_), channel_id=1, source_target_pairs={{1,2},{2,1},{5,6},{6,5},{9,10},{10,9},{13,14},{14,13},{17,18},{18,... | collective-permute-start | bytes 786440 | tf_op jit(solution)/shard_map/ppermute | solution.py:332
  103.4 11.7 %collective-permute-start.13 = (bf16[256,512]{1,0:T(8,128)(2,1)S(1)}, bf16[256,512]{1,0:T(8,128)(2,1)S(1)}, u32[]{:S(2)}, u32[]{:S(2)}) collective-permute-start(bf16[256,512]{1,0:T(8,128)(2,1)S(1)} %collective-permute-done.12.refs_10_), channel_id=1, source_target_pairs={{1,0},{2,3},{5,4},{6,7},{9,8},{10,11},{13,12},{14,15},{17,16},{18,... | collective-permute-start | bytes 786440 | tf_op jit(solution)/shard_map/ppermute | solution.py:333
  104.7 18.0 %collective-permute-start.9 = (bf16[256,512]{1,0:T(8,128)(2,1)S(1)}, bf16[256,512]{1,0:T(8,128)(2,1)S(1)}, u32[]{:S(2)}, u32[]{:S(2)}) collective-permute-start(bf16[256,512]{1,0:T(8,128)(2,1)S(1)} %collective-permute-done.6.refs_2_), channel_id=1, source_target_pairs={{1,0},{2,3},{5,4},{6,7},{9,8},{10,11},{13,12},{14,15},{17,16},{18,... | collective-permute-start | bytes 786440 | tf_op jit(solution)/shard_map/ppermute | solution.py:334
  115.1 10.5 %collective-permute-start.14 = (bf16[256,512]{1,0:T(8,128)(2,1)S(1)}, bf16[256,512]{1,0:T(8,128)(2,1)S(1)}, u32[]{:S(2)}, u32[]{:S(2)}) collective-permute-start(bf16[256,512]{1,0:T(8,128)(2,1)S(1)} %collective-permute-done.11.refs_8_), channel_id=1, source_target_pairs={{1,0},{2,3},{5,4},{6,7},{9,8},{10,11},{13,12},{14,15},{17,16},{18,... | collective-permute-start | bytes 786440 | tf_op jit(solution)/shard_map/ppermute | solution.py:334
  122.7 4.0 %collective-permute-start.26 = (bf16[768,512]{1,0:T(8,128)(2,1)S(1)}, bf16[768,512]{1,0:T(8,128)(2,1)S(1)}, u32[]{:S(2)}, u32[]{:S(2)}) collective-permute-start(bf16[768,512]{1,0:T(8,128)(2,1)S(1)} %collective-permute-done.25.refs_24_), channel_id=1, source_target_pairs={{0,4},{4,0},{8,12},{12,8},{16,20},{20,16},{24,28},{28,24},{1,5},{5... | collective-permute-start | bytes 2359304 | tf_op jit(solution)/shard_map/ppermute | solution.py:301
  125.7 2.3 %collective-permute-start.19 = (bf16[512,768]{1,0:T(8,128)(2,1)S(1)}, bf16[512,768]{1,0:T(8,128)(2,1)S(1)}, u32[]{:S(2)}, u32[]{:S(2)}) collective-permute-start(bf16[512,768]{1,0:T(8,128)(2,1)S(1)} %collective-permute-done.18.refs_16_), channel_id=1, source_target_pairs={{0,4},{4,0},{8,12},{12,8},{16,20},{20,16},{24,28},{28,24},{1,5},{5... | collective-permute-start | bytes 2359304 | tf_op jit(solution)/shard_map/ppermute | solution.py:301
  125.7 3.4 %collective-permute-start.24 = (bf16[768,512]{1,0:T(8,128)(2,1)S(1)}, bf16[768,512]{1,0:T(8,128)(2,1)S(1)}, u32[]{:S(2)}, u32[]{:S(2)}) collective-permute-start(bf16[768,512]{1,0:T(8,128)(2,1)S(1)} %collective-permute-done.23.refs_22_), channel_id=1, source_target_pairs={{0,4},{4,0},{8,12},{12,8},{16,20},{20,16},{24,28},{28,24},{1,5},{5... | collective-permute-start | bytes 2359304 | tf_op jit(solution)/shard_map/ppermute | solution.py:301
  126.2 4.0 %collective-permute-start.21 = (bf16[512,768]{1,0:T(8,128)(2,1)S(1)}, bf16[512,768]{1,0:T(8,128)(2,1)S(1)}, u32[]{:S(2)}, u32[]{:S(2)}) collective-permute-start(bf16[512,768]{1,0:T(8,128)(2,1)S(1)} %collective-permute-done.20.refs_18_), channel_id=1, source_target_pairs={{0,4},{4,0},{8,12},{12,8},{16,20},{20,16},{24,28},{28,24},{1,5},{5... | collective-permute-start | bytes 2359304 | tf_op jit(solution)/shard_map/ppermute | solution.py:301
  126.2 5.1 %collective-permute-start.28 = (bf16[768,512]{1,0:T(8,128)(2,1)S(1)}, bf16[768,512]{1,0:T(8,128)(2,1)S(1)}, u32[]{:S(2)}, u32[]{:S(2)}) collective-permute-start(bf16[768,512]{1,0:T(8,128)(2,1)S(1)} %collective-permute-done.27.refs_26_), channel_id=1, source_target_pairs={{0,4},{4,0},{8,12},{12,8},{16,20},{20,16},{24,28},{28,24},{1,5},{5... | collective-permute-start | bytes 2359304 | tf_op jit(solution)/shard_map/ppermute | solution.py:301
  136.6 10.7 %collective-permute-start.36 = (bf16[128,1024]{1,0:T(8,128)(2,1)S(1)}, bf16[128,1024]{1,0:T(8,128)(2,1)S(1)}, u32[]{:S(2)}, u32[]{:S(2)}) collective-permute-start(bf16[128,1024]{1,0:T(8,128)(2,1)S(1)} %get-tuple-element.30), channel_id=1, source_target_pairs={{0,1},{3,2},{4,5},{7,6},{8,9},{11,10},{12,13},{15,14},{16,17},{19,... | collective-permute-start | bytes 786440 | tf_op jit(solution)/shard_map/ppermute | solution.py:345
  143.3 8.0 %collective-permute-start.31 = (bf16[128,1024]{1,0:T(8,128)(2,1)S(1)}, bf16[128,1024]{1,0:T(8,128)(2,1)S(1)}, u32[]{:S(2)}, u32[]{:S(2)}) collective-permute-start(bf16[128,1024]{1,0:T(8,128)(2,1)S(1)} %get-tuple-element.26), channel_id=1, source_target_pairs={{0,1},{3,2},{4,5},{7,6},{8,9},{11,10},{12,13},{15,14},{16,17},{19,... | collective-permute-start | bytes 786440 | tf_op jit(solution)/shard_map/ppermute | solution.py:345
  144.7 12.3 %collective-permute-start.34 = (bf16[128,1024]{1,0:T(8,128)(2,1)S(1)}, bf16[128,1024]{1,0:T(8,128)(2,1)S(1)}, u32[]{:S(2)}, u32[]{:S(2)}) collective-permute-start(bf16[128,1024]{1,0:T(8,128)(2,1)S(1)} %get-tuple-element.31), channel_id=1, source_target_pairs={{0,1},{3,2},{4,5},{7,6},{8,9},{11,10},{12,13},{15,14},{16,17},{19,... | collective-permute-start | bytes 786440 | tf_op jit(solution)/shard_map/ppermute | solution.py:346
  146.0 15.9 %collective-permute-start.29 = (bf16[128,1024]{1,0:T(8,128)(2,1)S(1)}, bf16[128,1024]{1,0:T(8,128)(2,1)S(1)}, u32[]{:S(2)}, u32[]{:S(2)}) collective-permute-start(bf16[128,1024]{1,0:T(8,128)(2,1)S(1)} %get-tuple-element.27), channel_id=1, source_target_pairs={{0,1},{3,2},{4,5},{7,6},{8,9},{11,10},{12,13},{15,14},{16,17},{19,... | collective-permute-start | bytes 786440 | tf_op jit(solution)/shard_map/ppermute | solution.py:346
  147.4 27.4 %copy-start.9 = (f32[1024]{0:T(1024)S(1)}, f32[1024]{0:T(1024)}, u32[]{:S(2)}) copy-start(f32[1024]{0:T(1024)} %param.25) | copy-start | bytes 12292
  147.4 20.3 %collective-permute-start.37 = (bf16[128,1024]{1,0:T(8,128)(2,1)S(1)}, bf16[128,1024]{1,0:T(8,128)(2,1)S(1)}, u32[]{:S(2)}, u32[]{:S(2)}) collective-permute-start(bf16[128,1024]{1,0:T(8,128)(2,1)S(1)} %add_convert_fusion.1), channel_id=1, source_target_pairs={{1,2},{2,1},{5,6},{6,5},{9,10},{10,9},{13,14},{14,13},{17,18},{18,... | collective-permute-start | bytes 786440 | tf_op jit(solution)/shard_map/ppermute | solution.py:347
  151.4 11.2 %collective-permute-start.32 = (bf16[128,1024]{1,0:T(8,128)(2,1)S(1)}, bf16[128,1024]{1,0:T(8,128)(2,1)S(1)}, u32[]{:S(2)}, u32[]{:S(2)}) collective-permute-start(bf16[128,1024]{1,0:T(8,128)(2,1)S(1)} %add_convert_fusion.4), channel_id=1, source_target_pairs={{1,2},{2,1},{5,6},{6,5},{9,10},{10,9},{13,14},{14,13},{17,18},{18,... | collective-permute-start | bytes 786440 | tf_op jit(solution)/shard_map/ppermute | solution.py:347
  157.0 20.0 %collective-permute-start.35 = (bf16[128,1024]{1,0:T(8,128)(2,1)S(1)}, bf16[128,1024]{1,0:T(8,128)(2,1)S(1)}, u32[]{:S(2)}, u32[]{:S(2)}) collective-permute-start(bf16[128,1024]{1,0:T(8,128)(2,1)S(1)} %add_convert_fusion.2), channel_id=1, source_target_pairs={{1,2},{2,1},{5,6},{6,5},{9,10},{10,9},{13,14},{14,13},{17,18},{18,... | collective-permute-start | bytes 786440 | tf_op jit(solution)/shard_map/ppermute | solution.py:348
  161.9 5.9 %collective-permute-start.30 = (bf16[128,1024]{1,0:T(8,128)(2,1)S(1)}, bf16[128,1024]{1,0:T(8,128)(2,1)S(1)}, u32[]{:S(2)}, u32[]{:S(2)}) collective-permute-start(bf16[128,1024]{1,0:T(8,128)(2,1)S(1)} %add_convert_fusion.5), channel_id=1, source_target_pairs={{1,2},{2,1},{5,6},{6,5},{9,10},{10,9},{13,14},{14,13},{17,18},{18,... | collective-permute-start | bytes 786440 | tf_op jit(solution)/shard_map/ppermute | solution.py:348
  162.7 12.1 %collective-permute-start.33 = (bf16[128,1024]{1,0:T(8,128)(2,1)S(1)}, bf16[128,1024]{1,0:T(8,128)(2,1)S(1)}, u32[]{:S(2)}, u32[]{:S(2)}) collective-permute-start(bf16[128,1024]{1,0:T(8,128)(2,1)S(1)} %add_convert_fusion.3), channel_id=1, source_target_pairs={{0,1},{1,0},{2,3},{3,2},{4,5},{5,4},{6,7},{7,6},{8,9},{9,8},{10,11... | collective-permute-start | bytes 786440 | tf_op jit(solution)/shard_map/ppermute | solution.py:301
  167.7 11.1 %collective-permute-start.38 = (bf16[128,1024]{1,0:T(8,128)(2,1)S(1)}, bf16[128,1024]{1,0:T(8,128)(2,1)S(1)}, u32[]{:S(2)}, u32[]{:S(2)}) collective-permute-start(bf16[128,1024]{1,0:T(8,128)(2,1)S(1)} %add_convert_fusion), channel_id=1, source_target_pairs={{0,1},{1,0},{2,3},{3,2},{4,5},{5,4},{6,7},{7,6},{8,9},{9,8},{10,11... | collective-permute-start | bytes 786440 | tf_op jit(solution)/shard_map/ppermute | solution.py:301

commit v5 on v4

--- a/solution.py
+++ b/solution.py
@@ -12,7 +12,6 @@
 SUB = 64
 F32 = jnp.float32
 BF16 = jnp.bfloat16
-HI = lax.Precision.HIGHEST
 MIB = 1024 * 1024
 
 
@@ -27,6 +26,16 @@
 def split2(v):
     high = v.astype(BF16)
     return jnp.concatenate([high, (v - high.astype(F32)).astype(BF16)], axis=0)
+
+
+def summed_over(decay, pattern):
+    heads = decay.shape[0]
+    high = decay.astype(BF16)
+    rest = decay - high.astype(F32)
+    middle = rest.astype(BF16)
+    low = (rest - middle.astype(F32)).astype(BF16)
+    total = jnp.dot(jnp.concatenate([high, middle, low], axis=0), pattern, preferred_element_type=F32)
+    return total[:heads] + total[heads : 2 * heads] + total[2 * heads :]
 
 
 def spread_of(heads, chans):
@@ -54,9 +63,9 @@
         hs[...] = jnp.zeros_like(hs)
         ds[...] = jnp.ones_like(ds)
 
-    later = (iota((span, span), 0) > iota((span, span), 1)).astype(F32)
+    later = (iota((span, span), 0) > iota((span, span), 1)).astype(BF16)
     decay = dl_ref[...]
-    tail = jnp.dot(decay, later, precision=HI, preferred_element_type=F32)
+    tail = summed_over(decay, later)
     w = jnp.exp(tail) * st_ref[...] * scale_cols(sc_ref, step * span, span, blk)
     spread = spread_of(heads, chans)
     hot = spread.astype(BF16)
@@ -90,7 +99,7 @@
     col = iota((span, span), 1)
     same = row // SUB == col // SUB
     upto = jnp.where(row <= col, 1.0, 0.0) - jnp.where(row % SUB < SUB // 2, 1.0, 0.0)
-    rel = jnp.dot(decay, jnp.where(same, upto, 0.0), precision=HI, preferred_element_type=F32)
+    rel = summed_over(decay, jnp.where(same, upto, 0.0).astype(BF16))
     scale = scale_cols(sc_ref, step * span, span, blk)
     u = jnp.exp(rel)
     v = jnp.exp(-rel) * st_ref[...] * scale
@@ -212,22 +221,11 @@
     inputs = refs[:count]
     hbm = refs[count : count + 2 * shards]
     outs = refs[count + 2 * shards : count + 2 * shards + ring]
-    act, terms, u_buf, d_buf, sem = refs[count + 2 * shards + ring :]
+    act, terms = refs[count + 2 * shards + ring :]
     z = lax.axis_index("exp")
     c = lax.axis_index("ctx")
     rows = inputs[0].shape[0]
     chans = half * halves
-    copies = [pltpu.make_async_copy(hbm[k], u_buf.at[k], sem.at[k]) for k in range(shards)]
-    copies += [pltpu.make_async_copy(hbm[shards + k], d_buf.at[k], sem.at[shards + k]) for k in range(shards)]
-    ahead = min(3, len(copies))
-    for copy in copies[:ahead]:
-        copy.start()
-
-    def ready(index):
-        if index + ahead < len(copies):
-            copies[index + ahead].start()
-        copies[index].wait()
-
     at = 0
     for q in range(halves):
         lanes = pl.ds(pl.multiple_of(jnp.bitwise_xor(flip_ref[0], q) * half, 128), half)
@@ -237,19 +235,17 @@
                 piece = piece + inputs[other][...]
             act[k, :, lanes] = piece
             at += groups[q][k]
-    feats = u_buf.shape[1]
-    total = jnp.zeros((rows, u_buf.shape[2]), F32)
+    feats = hbm[0].shape[0]
+    total = jnp.zeros((rows, hbm[0].shape[1]), F32)
     for k in range(shards):
-        ready(k)
         first = jnp.bitwise_xor(c, k) * feats
         a = act[jnp.bitwise_xor(z, first // chans), :, pl.ds(pl.multiple_of(lax.rem(first, chans), 128), feats)]
-        total = total + jnp.dot(a, u_buf[k], preferred_element_type=F32)
+        total = total + jnp.dot(a, hbm[k][...], preferred_element_type=F32)
     hidden = (total / (1.0 + jnp.exp(-total))).astype(BF16)
-    cols = d_buf.shape[2]
+    cols = hbm[shards].shape[1]
     for k in range(shards):
-        ready(shards + k)
         first = jnp.bitwise_xor(c, k) * cols
-        term = jnp.dot(hidden, d_buf[k], preferred_element_type=F32).astype(BF16)
+        term = jnp.dot(hidden, hbm[shards + k][...], preferred_element_type=F32).astype(BF16)
         terms[jnp.bitwise_xor(z, first // chans), :, pl.ds(pl.multiple_of(lax.rem(first, chans), 128), cols)] = term
     for k in range(ring):
         outs[k][...] = terms[k]
@@ -394,6 +390,7 @@
     flip = lax.rem(lax.axis_index("ctx"), 2)[None] if paired else jnp.zeros((1,), jnp.int32)
 
     span = 256
+    wide = min(512, tokens)
     message = pl.pallas_call(
         functools.partial(end_kernel, blk=blk),
         grid=(tokens // span,),
@@ -456,10 +453,10 @@
             functools.partial(norm_kernel, width=width),
             grid_spec=pltpu.PrefetchScalarGridSpec(
                 num_scalar_prefetch=1,
-                grid=(tokens // span,),
-                in_specs=[rows_spec(span, states), pl.BlockSpec((span, half), block), pl.BlockSpec((span, half), block),
-                          pl.BlockSpec((1, half), col), cols_spec(1, span)] + entry,
-                out_specs=[rows_spec(span, half), whole((CAP, half))],
+                grid=(tokens // wide,),
+                in_specs=[rows_spec(wide, states), pl.BlockSpec((wide, half), block), pl.BlockSpec((wide, half), block),
+                          pl.BlockSpec((1, half), col), cols_spec(1, wide)] + entry,
+                out_specs=[rows_spec(wide, half), whole((CAP, half))],
                 scratch_shapes=[pltpu.VMEM((CAP, half), F32), pltpu.VMEM((states, half), BF16)],
             ),
             out_shape=[jax.ShapeDtypeStruct((tokens, half), BF16), jax.ShapeDtypeStruct((CAP, half), BF16)],
@@ -478,7 +475,7 @@
         pieces += got
         groups.append(group)
 
-    any_spec = pl.BlockSpec(memory_space=pl.ANY)
+    any_spec = pl.BlockSpec(memory_space=pltpu.VMEM)
     rests = normed
     summed = []
     for part in range(parts):
@@ -493,9 +490,6 @@
                 scratch_shapes=[
                     pltpu.VMEM((ring, rows, chans), BF16),
                     pltpu.VMEM((ring, rows, chans), BF16),
-                    pltpu.VMEM((ctx,) + up_weight.shape, BF16),
-                    pltpu.VMEM((ctx,) + down_weight.shape, BF16),
-                    pltpu.SemaphoreType.DMA((2 * ctx,)),
                 ],
             ),
             out_shape=[jax.ShapeDtypeStruct((rows, chans), BF16)] * ring,
@@ -508,11 +502,11 @@
             functools.partial(final_kernel, base=part * rows, count=len(rests)),
             grid_spec=pltpu.PrefetchScalarGridSpec(
                 num_scalar_prefetch=1,
-                grid=(tokens // span,),
-                in_specs=[cols_spec(1, span), cols_spec(1, span)]
-                + [rows_spec(span, chans // len(rests))] * len(rests)
+                grid=(tokens // wide,),
+                in_specs=[cols_spec(1, wide), cols_spec(1, wide)]
+                + [rows_spec(wide, chans // len(rests))] * len(rests)
                 + [whole((rows, chans))] * len(summed[part]),
-                out_specs=rows_spec(span, chans),
+                out_specs=rows_spec(wide, chans),
                 scratch_shapes=[pltpu.VMEM((rows, chans), BF16)],
             ),
             out_shape=jax.ShapeDtypeStruct((tokens, chans), BF16),

time: 183 us -> 176 us (0.962)
  Pallas kernels: 38.2 us -> 29 us
  waiting for transfers between devices: 101 us -> 104 us
    pallas_call x2, Pallas kernels: 10.5 us -> 5.33 us  [body(): pl.pallas_call(functools.partial(expert_kernel, ring=ring, shards=ctx, gr...]
  transfers between devices with their start and end apart: 39 -> 39, of which waited for: 18 -> 18; matrix products, arithmetic and copies ran while one was open for 0% -> 0% of each run, Pallas kernels for 13% -> 11%
where the time goes in v5:
time: 176 us
  waiting for transfers between devices  104 us (59%)
  starting transfers between devices  40.9 us (23%)
  Pallas kernels  29 us (16%)
    ppermute x23, waiting for transfers between devices, swap(): return lax.ppermute(value, axis, [(i, i ^ mask) for i in range(count)])  60.9 us
    ppermute x23, starting transfers between devices, swap(): return lax.ppermute(value, axis, [(i, i ^ mask) for i in range(count)])  25 us
    ppermute x2, waiting for transfers between devices, gather_line(): out_near = lax.ppermute(cross, 'exp', OUTWARD)  19.9 us
    pallas_call x1, Pallas kernels, body(): pl.pallas_call(functools.partial(local_kernel, blk=blk), grid=(tokens //...  9.96 us
    ppermute x2, waiting for transfers between devices, gather_line(): out_far = lax.ppermute(cross_far, 'exp', OUTWARD)  9.25 us
    ppermute x2, waiting for transfers between devices, sum_line(): near = lax.ppermute(terms[2], 'exp', ENDS)  9.01 us
    pallas_call x2, Pallas kernels, body(): pl.pallas_call(functools.partial(expert_kernel, ring=ring, shards=ctx, gr...  5.33 us
    pallas_call x1, Pallas kernels, body(): pl.pallas_call(functools.partial(end_kernel, blk=blk), grid=(tokens // sp...  5.12 us
  transfers between devices with their start and end apart: 39, of which 18 were waited for; matrix products, arithmetic and copies ran while one was open for 0% of the time, Pallas kernels for 11%

profile of v5, /device:TPU:0, one launch (start us, length us, event | category | flops | bytes accessed | tf_op | source)
XLA Modules:
  0.0 175.8 jit_solution(8204255530160754292)
XLA Ops:
  0.0 5.1 %end_state.1.own_ref = bf16[144,1024]{1,0:T(8,128)(2,1)} custom-call(bf16[1024,1024]{1,0:T(8,128)(2,1)} %x_ref.3, bf16[1024,128]{1,0:T(8,128)(2,1)} %b_ref.3, f32[16,1024]{1,0:T(8,128)} %st_ref.3, f32[16,1024]{1,0:T(8,128)} %dl_ref.3, s32[8,16]{1,0:T(8,128)} %sc_ref.3), custom_call_target="tpu_custom_call" | custom-call | tf_op jit(solution)/shard_map/end_state/pallas_call | solution.py:394
  5.2 0.5 collective-permute-start
  5.7 2.5 %collective-permute-start.16 = (bf16[512,768]{1,0:T(8,128)(2,1)S(1)}, bf16[512,768]{1,0:T(8,128)(2,1)S(1)}, u32[]{:S(2)}, u32[]{:S(2)}) collective-permute-start(bf16[512,768]{1,0:T(8,128)(2,1)S(1)} %copy-done), channel_id=1, source_target_pairs={{0,8},{4,12},{8,0},{12,4},{16,24},{20,28},{24,16},{28,20},{1,9},{5... | collective-permute-start | bytes 2359304 | tf_op jit(solution)/shard_map/ppermute | solution.py:297
  8.2 1.0 copy-done.3
  9.2 0.1 chip_state.1
  9.3 1.8 %collective-permute-start.1 = (bf16[144,512]{1,0:T(8,128)(2,1)S(1)}, bf16[144,512]{1,0:T(8,128)(2,1)S(1)}, u32[]{:S(2)}, u32[]{:S(2)}) collective-permute-start(bf16[144,512]{1,0:T(8,128)(2,1)S(1)} %chip_state.1), channel_id=1, source_target_pairs={{0,8},{4,12},{8,0},{12,4},{16,24},{20,28},{24,16},{28,20},{1,9},{5... | collective-permute-start | bytes 442376 | tf_op jit(solution)/shard_map/ppermute | solution.py:297
  11.0 1.5 collective-permute-start.2
  12.6 0.2 collective-permute-start.3
  12.8 17.0 %collective-permute-done.1.refs_0_ = bf16[144,512]{1,0:T(8,128)(2,1)S(1)} collective-permute-done((bf16[144,512]{1,0:T(8,128)(2,1)S(1)}, bf16[144,512]{1,0:T(8,128)(2,1)S(1)}, u32[]{:S(2)}, u32[]{:S(2)}) %collective-permute-start.1) | collective-permute-done | bytes 147488 | tf_op jit(solution)/shard_map/ppermute | solution.py:297
  29.8 4.1 %collective-permute-done.3.refs_2_ = bf16[144,512]{1,0:T(8,128)(2,1)S(1)} collective-permute-done((bf16[144,512]{1,0:T(8,128)(2,1)S(1)}, bf16[144,512]{1,0:T(8,128)(2,1)S(1)}, u32[]{:S(2)}, u32[]{:S(2)}) %collective-permute-start.3) | collective-permute-done | bytes 147488 | tf_op jit(solution)/shard_map/ppermute | solution.py:297
  33.9 0.1 prior.1.h_ref
  34.0 0.1 collective-permute-start.4
  34.2 10.0 %local_out.1 = (bf16[1024,1024]{1,0:T(8,128)(2,1)S(1)}, bf16[1024,1024]{1,0:T(8,128)(2,1)S(1)}) custom-call(bf16[1024,1024]{1,0:T(8,128)(2,1)} %x_ref.3, bf16[1024,1024]{1,0:T(8,128)(2,1)} %g_ref.1, bf16[1024,128]{1,0:T(8,128)(2,1)S(1)} %copy-done.4, bf16[1024,128]{1,0:T(8,128)(2,1)S(1)} %copy-done.2, f32[16,1024]{1,0:T(8,128)S(1)} %copy-done.5, ...), custom_call_target="tpu_custom_call" | custom-call | tf_op jit(solution)/shard_map/local_out/pallas_call | solution.py:423
  44.2 2.0 %shard_map.127 = (bf16[1024,512]{1,0:T(8,128)(2,1)S(1)}, bf16[256,512]{1,0:T(8,128)(2,1)S(1)}) custom-call(s32[1]{0:T(128)} %bitcast.flip_ref, bf16[1024,128]{1,0:T(8,128)(2,1)S(1)} %copy-done.2, bf16[1024,1024]{1,0:T(8,128)(2,1)S(1)} %get-tuple-element.19.a_ref, bf16[1024,1024]{1,0:T(8,128)(2,1)S(1)} %get-tuple-element.20.w_ref, f32[1,1024]{1,0:T(1,128)S(1)} %bitcast.9, ...), custom_call_target="tpu_custom_call" | custom-call | tf_op jit(solution)/shard_map/pallas_call | solution.py:452
  46.2 1.6 collective-permute-start.5
  47.8 0.7 collective-permute-start.7
  48.5 0.6 collective-permute-start.25
  49.1 1.5 collective-permute-start.18
  50.6 4.3 %collective-permute-done.5.refs_1_ = bf16[256,512]{1,0:T(8,128)(2,1)S(1)} collective-permute-done((bf16[256,512]{1,0:T(8,128)(2,1)S(1)}, bf16[256,512]{1,0:T(8,128)(2,1)S(1)}, u32[]{:S(2)}, u32[]{:S(2)}) %collective-permute-start.5) | collective-permute-done | bytes 262176 | tf_op jit(solution)/shard_map/ppermute | solution.py:297
  54.9 1.6 collective-permute-start.23
  56.4 0.5 collective-permute-start.22
  56.9 2.0 %shard_map.128 = (bf16[1024,512]{1,0:T(8,128)(2,1)S(1)}, bf16[256,512]{1,0:T(8,128)(2,1)S(1)}) custom-call(s32[1]{0:T(128)} %bitcast.flip_ref, bf16[1024,128]{1,0:T(8,128)(2,1)S(1)} %copy-done.2, bf16[1024,1024]{1,0:T(8,128)(2,1)S(1)} %get-tuple-element.19.a_ref, bf16[1024,1024]{1,0:T(8,128)(2,1)S(1)} %get-tuple-element.20.w_ref, f32[1,1024]{1,0:T(1,128)S(1)} %bitcast.10, ...), custom_call_target="tpu_custom_call" | custom-call | tf_op jit(solution)/shard_map/pallas_call | solution.py:452
  58.9 10.0 %collective-permute-done.25.refs_24_ = bf16[768,512]{1,0:T(8,128)(2,1)S(1)} collective-permute-done((bf16[768,512]{1,0:T(8,128)(2,1)S(1)}, bf16[768,512]{1,0:T(8,128)(2,1)S(1)}, u32[]{:S(2)}, u32[]{:S(2)}) %collective-permute-start.25) | collective-permute-done | bytes 786464 | tf_op jit(solution)/shard_map/ppermute | solution.py:297
  69.0 4.4 %collective-permute-start.10 = (bf16[256,512]{1,0:T(8,128)(2,1)S(1)}, bf16[256,512]{1,0:T(8,128)(2,1)S(1)}, u32[]{:S(2)}, u32[]{:S(2)}) collective-permute-start(bf16[256,512]{1,0:T(8,128)(2,1)S(1)} %get-tuple-element.24.refs_6_), channel_id=1, source_target_pairs={{0,1},{1,0},{2,3},{3,2},{4,5},{5,4},{6,7},{7,6},{8,9},{9,8},{10,11... | collective-permute-start | bytes 786440 | tf_op jit(solution)/shard_map/ppermute | solution.py:297
  73.4 11.6 %collective-permute-done.18.refs_16_ = bf16[512,768]{1,0:T(8,128)(2,1)S(1)} collective-permute-done((bf16[512,768]{1,0:T(8,128)(2,1)S(1)}, bf16[512,768]{1,0:T(8,128)(2,1)S(1)}, u32[]{:S(2)}, u32[]{:S(2)}) %collective-permute-start.18) | collective-permute-done | bytes 786464 | tf_op jit(solution)/shard_map/ppermute | solution.py:297
  85.0 0.7 collective-permute-start.12
  85.7 0.7 collective-permute-start.6
  86.4 1.3 collective-permute-start.8
  87.7 0.6 collective-permute-start.20
  88.3 1.4 collective-permute-start.27
  89.8 0.7 collective-permute-start.11
  90.5 10.8 %collective-permute-done.8.refs_3_ = bf16[256,512]{1,0:T(8,128)(2,1)S(1)} collective-permute-done((bf16[256,512]{1,0:T(8,128)(2,1)S(1)}, bf16[256,512]{1,0:T(8,128)(2,1)S(1)}, u32[]{:S(2)}, u32[]{:S(2)}) %collective-permute-start.8) | collective-permute-done | bytes 262176 | tf_op jit(solution)/shard_map/ppermute | solution.py:329
  101.2 1.3 collective-permute-start.13
  102.5 1.3 collective-permute-start.9
  103.8 9.2 %collective-permute-done.13.refs_9_ = bf16[256,512]{1,0:T(8,128)(2,1)S(1)} collective-permute-done((bf16[256,512]{1,0:T(8,128)(2,1)S(1)}, bf16[256,512]{1,0:T(8,128)(2,1)S(1)}, u32[]{:S(2)}, u32[]{:S(2)}) %collective-permute-start.13) | collective-permute-done | bytes 262176 | tf_op jit(solution)/shard_map/ppermute | solution.py:329
  113.0 1.3 collective-permute-start.14
  114.3 6.3 %collective-permute-done.9.refs_5_ = bf16[256,512]{1,0:T(8,128)(2,1)S(1)} collective-permute-done((bf16[256,512]{1,0:T(8,128)(2,1)S(1)}, bf16[256,512]{1,0:T(8,128)(2,1)S(1)}, u32[]{:S(2)}, u32[]{:S(2)}) %collective-permute-start.9) | collective-permute-done | bytes 262176 | tf_op jit(solution)/shard_map/ppermute | solution.py:330
  120.6 2.9 %collective-permute-done.14.refs_11_ = bf16[256,512]{1,0:T(8,128)(2,1)S(1)} collective-permute-done((bf16[256,512]{1,0:T(8,128)(2,1)S(1)}, bf16[256,512]{1,0:T(8,128)(2,1)S(1)}, u32[]{:S(2)}, u32[]{:S(2)}) %collective-permute-start.14) | collective-permute-done | bytes 262176 | tf_op jit(solution)/shard_map/ppermute | solution.py:330
  123.6 0.5 collective-permute-start.24
  124.1 0.1 collective-permute-start.21
  124.1 0.4 collective-permute-start.28
  124.6 1.2 collective-permute-done.19.refs_17_
  125.8 1.1 collective-permute-done.24.refs_23_
  127.0 1.1 collective-permute-done.21.refs_19_
  128.1 1.1 collective-permute-done.28.refs_27_
  129.2 2.6 %shard_map.131 = (bf16[128,1024]{1,0:T(8,128)(2,1)S(1)}, bf16[128,1024]{1,0:T(8,128)(2,1)S(1)}, bf16[128,1024]{1,0:T(8,128)(2,1)S(1)}, bf16[128,1024]{1,0:T(8,128)(2,1)S(1)}) custom-call(s32[1]{0:T(128)} %bitcast.flip_ref, bf16[256,512]{1,0:T(8,128)(2,1)S(1)} %get-tuple-element.23.refs_0_, bf16[256,512]{1,0:T(8,128)(2,1)S(1)} %collective-permute-done.5.refs_1_, ...), custom_call_target="tpu_custom_call" | custom-call | tf_op jit(solution)/shard_map/pallas_call | solution.py:482
  131.9 1.5 collective-permute-start.36
  133.3 2.7 %shard_map.129 = (bf16[128,1024]{1,0:T(8,128)(2,1)S(1)}, bf16[128,1024]{1,0:T(8,128)(2,1)S(1)}, bf16[128,1024]{1,0:T(8,128)(2,1)S(1)}, bf16[128,1024]{1,0:T(8,128)(2,1)S(1)}) custom-call(s32[1]{0:T(128)} %bitcast.flip_ref, bf16[256,512]{1,0:T(8,128)(2,1)S(1)} %get-tuple-element.23.refs_0_, bf16[256,512]{1,0:T(8,128)(2,1)S(1)} %collective-permute-done.5.refs_1_, ...), custom_call_target="tpu_custom_call" | custom-call | tf_op jit(solution)/shard_map/pallas_call | solution.py:482
  136.0 1.3 collective-permute-start.31
  137.3 1.3 collective-permute-start.34
  138.7 1.3 collective-permute-start.29
  140.1 0.7 collective-permute-start.37
  140.8 4.8 %collective-permute-done.31 = bf16[128,1024]{1,0:T(8,128)(2,1)S(1)} collective-permute-done((bf16[128,1024]{1,0:T(8,128)(2,1)S(1)}, bf16[128,1024]{1,0:T(8,128)(2,1)S(1)}, u32[]{:S(2)}, u32[]{:S(2)}) %collective-permute-start.31) | collective-permute-done | bytes 262176 | tf_op jit(solution)/shard_map/ppermute | solution.py:341
  145.7 0.7 collective-permute-start.32
  146.4 4.9 %collective-permute-done.34 = bf16[128,1024]{1,0:T(8,128)(2,1)S(1)} collective-permute-done((bf16[128,1024]{1,0:T(8,128)(2,1)S(1)}, bf16[128,1024]{1,0:T(8,128)(2,1)S(1)}, u32[]{:S(2)}, u32[]{:S(2)}) %collective-permute-start.34) | collective-permute-done | bytes 262176 | tf_op jit(solution)/shard_map/ppermute | solution.py:342
  151.3 0.7 collective-permute-start.35
  152.0 4.2 %collective-permute-done.29 = bf16[128,1024]{1,0:T(8,128)(2,1)S(1)} collective-permute-done((bf16[128,1024]{1,0:T(8,128)(2,1)S(1)}, bf16[128,1024]{1,0:T(8,128)(2,1)S(1)}, u32[]{:S(2)}, u32[]{:S(2)}) %collective-permute-start.29) | collective-permute-done | bytes 262176 | tf_op jit(solution)/shard_map/ppermute | solution.py:342
  156.2 0.7 collective-permute-start.30
  157.0 5.0 %collective-permute-start.33 = (bf16[128,1024]{1,0:T(8,128)(2,1)S(1)}, bf16[128,1024]{1,0:T(8,128)(2,1)S(1)}, u32[]{:S(2)}, u32[]{:S(2)}) collective-permute-start(bf16[128,1024]{1,0:T(8,128)(2,1)S(1)} %add_convert_fusion.3), channel_id=1, source_target_pairs={{0,1},{1,0},{2,3},{3,2},{4,5},{5,4},{6,7},{7,6},{8,9},{9,8},{10,11... | collective-permute-start | bytes 786440 | tf_op jit(solution)/shard_map/ppermute | solution.py:297
  162.0 0.1 collective-permute-start.38
  162.1 7.0 %collective-permute-done.33.refs_4_ = bf16[128,1024]{1,0:T(8,128)(2,1)S(1)} collective-permute-done((bf16[128,1024]{1,0:T(8,128)(2,1)S(1)}, bf16[128,1024]{1,0:T(8,128)(2,1)S(1)}, u32[]{:S(2)}, u32[]{:S(2)}) %collective-permute-start.33) | collective-permute-done | bytes 262176 | tf_op jit(solution)/shard_map/ppermute | solution.py:297
  169.1 1.7 shard_map.130.refs_0_
  170.9 2.3 %collective-permute-done.38.refs_3_ = bf16[128,1024]{1,0:T(8,128)(2,1)S(1)} collective-permute-done((bf16[128,1024]{1,0:T(8,128)(2,1)S(1)}, bf16[128,1024]{1,0:T(8,128)(2,1)S(1)}, u32[]{:S(2)}, u32[]{:S(2)}) %collective-permute-start.38) | collective-permute-done | bytes 262176 | tf_op jit(solution)/shard_map/ppermute | solution.py:297
  173.2 2.7 %shard_map.132 = bf16[1024,1024]{1,0:T(8,128)(2,1)} custom-call(s32[1]{0:T(128)} %bitcast.flip_ref, s32[1,1024]{1,0:T(1,128)S(1)} %bitcast.8, f32[1,1024]{1,0:T(1,128)S(1)} %bitcast.12, bf16[1024,1024]{1,0:T(8,128)(2,1)S(1)} %shard_map.130.refs_0_, bf16[128,1024]{1,0:T(8,128)(2,1)S(1)} %get-tuple-element.29.refs_1_, ...), custom_call_target="tpu_custom_call" | custom-call | tf_op jit(solution)/shard_map/pallas_call | solution.py:501
  (54 shorter events, 0.5 us)
Async XLA Ops:
  0.0 34.1 %copy-start.10 = (s32[8,16]{1,0:T(8,128)S(1)}, s32[8,16]{1,0:T(8,128)}, u32[]{:S(2)}) copy-start(s32[8,16]{1,0:T(8,128)} %sc_ref.3) | copy-start | bytes 1540
  0.0 34.1 %copy-start.5 = (f32[16,1024]{1,0:T(8,128)S(1)}, f32[16,1024]{1,0:T(8,128)}, u32[]{:S(2)}) copy-start(f32[16,1024]{1,0:T(8,128)} %st_ref.3) | copy-start | bytes 196612
  0.0 34.1 %copy-start.6 = (f32[16,1024]{1,0:T(8,128)S(1)}, f32[16,1024]{1,0:T(8,128)}, u32[]{:S(2)}) copy-start(f32[16,1024]{1,0:T(8,128)} %dl_ref.3) | copy-start | bytes 196612
  0.0 34.1 %copy-start.4 = (bf16[1024,128]{1,0:T(8,128)(2,1)S(1)}, bf16[1024,128]{1,0:T(8,128)(2,1)}, u32[]{:S(2)}) copy-start(bf16[1024,128]{1,0:T(8,128)(2,1)} %b_ref.3) | copy-start | bytes 786436
  0.0 5.7 %copy-start = (bf16[512,768]{1,0:T(8,128)(2,1)S(1)}, bf16[512,768]{1,0:T(8,128)(2,1)}, u32[]{:S(2)}) copy-start(bf16[512,768]{1,0:T(8,128)(2,1)} %refs_12_.3) | copy-start | bytes 2359300
  0.0 34.1 %copy-start.11 = (f32[16]{0:T(128)S(1)}, f32[16]{0:T(128)}, u32[]{:S(2)}) copy-start(f32[16]{0:T(128)} %param.19) | copy-start | bytes 196
  0.0 34.1 %copy-start.2 = (bf16[1024,128]{1,0:T(8,128)(2,1)S(1)}, bf16[1024,128]{1,0:T(8,128)(2,1)}, u32[]{:S(2)}) copy-start(bf16[1024,128]{1,0:T(8,128)(2,1)} %c_ref.5) | copy-start | bytes 786436
  5.2 3.1 %collective-permute-start = (bf16[144,1024]{1,0:T(8,128)(2,1)}, bf16[144,1024]{1,0:T(8,128)(2,1)S(1)}, u32[]{:S(2)}, u32[]{:S(2)}) collective-permute-start(bf16[144,1024]{1,0:T(8,128)(2,1)} %end_state.1.own_ref), channel_id=1, source_target_pairs={{0,4},{4,0},{8,12},{12,8},{16,20},{20,16},{24,28},{28,24},{1,5},{5... | collective-permute-start | bytes 884744 | tf_op jit(solution)/shard_map/ppermute | solution.py:297
  5.7 50.8 %collective-permute-start.16 = (bf16[512,768]{1,0:T(8,128)(2,1)S(1)}, bf16[512,768]{1,0:T(8,128)(2,1)S(1)}, u32[]{:S(2)}, u32[]{:S(2)}) collective-permute-start(bf16[512,768]{1,0:T(8,128)(2,1)S(1)} %copy-done), channel_id=1, source_target_pairs={{0,8},{4,12},{8,0},{12,4},{16,24},{20,28},{24,16},{28,20},{1,9},{5... | collective-permute-start | bytes 2359304 | tf_op jit(solution)/shard_map/ppermute | solution.py:297
  8.2 1.0 copy-start.3
  9.3 20.5 %collective-permute-start.1 = (bf16[144,512]{1,0:T(8,128)(2,1)S(1)}, bf16[144,512]{1,0:T(8,128)(2,1)S(1)}, u32[]{:S(2)}, u32[]{:S(2)}) collective-permute-start(bf16[144,512]{1,0:T(8,128)(2,1)S(1)} %chip_state.1), channel_id=1, source_target_pairs={{0,8},{4,12},{8,0},{12,4},{16,24},{20,28},{24,16},{28,20},{1,9},{5... | collective-permute-start | bytes 442376 | tf_op jit(solution)/shard_map/ppermute | solution.py:297
  11.0 18.7 %collective-permute-start.2 = (bf16[144,512]{1,0:T(8,128)(2,1)S(1)}, bf16[144,512]{1,0:T(8,128)(2,1)S(1)}, u32[]{:S(2)}, u32[]{:S(2)}) collective-permute-start(bf16[144,512]{1,0:T(8,128)(2,1)S(1)} %chip_state.1), channel_id=1, source_target_pairs={{0,16},{4,20},{8,24},{12,28},{16,0},{20,4},{24,8},{28,12},{1,17},{... | collective-permute-start | bytes 442376 | tf_op jit(solution)/shard_map/ppermute | solution.py:297
  12.6 21.3 %collective-permute-start.3 = (bf16[144,512]{1,0:T(8,128)(2,1)S(1)}, bf16[144,512]{1,0:T(8,128)(2,1)S(1)}, u32[]{:S(2)}, u32[]{:S(2)}) collective-permute-start(bf16[144,512]{1,0:T(8,128)(2,1)S(1)} %chip_state.1), channel_id=1, source_target_pairs={{0,24},{4,28},{8,16},{12,20},{16,8},{20,12},{24,0},{28,4},{1,25},{... | collective-permute-start | bytes 442376 | tf_op jit(solution)/shard_map/ppermute | solution.py:297
  34.0 15.1 %collective-permute-start.4 = (bf16[128,512]{1,0:T(8,128)(2,1)S(1)}, bf16[128,512]{1,0:T(8,128)(2,1)S(1)}, u32[]{:S(2)}, u32[]{:S(2)}) collective-permute-start(bf16[128,512]{1,0:T(8,128)(2,1)S(1)} %prior.1.h_ref), channel_id=1, source_target_pairs={{0,4},{4,0},{8,12},{12,8},{16,20},{20,16},{24,28},{28,24},{1,5},{5... | collective-permute-start | bytes 393224 | tf_op jit(solution)/shard_map/ppermute | solution.py:297
  34.1 10.0 %copy-start.7 = (s32[1024]{0:T(1024)S(1)}, s32[1024]{0:T(1024)}, u32[]{:S(2)}) copy-start(s32[1024]{0:T(1024)} %param.24) | copy-start | bytes 12292
  34.1 10.0 %copy-start.8 = (f32[1024]{0:T(1024)S(1)}, f32[1024]{0:T(1024)}, u32[]{:S(2)}) copy-start(f32[1024]{0:T(1024)} %param.21) | copy-start | bytes 12292
  44.1 4.4 %copy-start.1 = (bf16[768,512]{1,0:T(8,128)(2,1)S(1)}, bf16[768,512]{1,0:T(8,128)(2,1)}, u32[]{:S(2)}) copy-start(bf16[768,512]{1,0:T(8,128)(2,1)} %refs_20_.3) | copy-start | bytes 2359300
  46.2 8.7 %collective-permute-start.5 = (bf16[256,512]{1,0:T(8,128)(2,1)S(1)}, bf16[256,512]{1,0:T(8,128)(2,1)S(1)}, u32[]{:S(2)}, u32[]{:S(2)}) collective-permute-start(bf16[256,512]{1,0:T(8,128)(2,1)S(1)} %get-tuple-element.23.refs_0_), channel_id=1, source_target_pairs={{0,1},{1,0},{2,3},{3,2},{4,5},{5,4},{6,7},{7,6},{8,9},{9,8},{10,11... | collective-permute-start | bytes 786440 | tf_op jit(solution)/shard_map/ppermute | solution.py:297
  47.8 8.6 %collective-permute-start.7 = (bf16[256,512]{1,0:T(8,128)(2,1)S(1)}, bf16[256,512]{1,0:T(8,128)(2,1)S(1)}, u32[]{:S(2)}, u32[]{:S(2)}) collective-permute-start(bf16[256,512]{1,0:T(8,128)(2,1)S(1)} %get-tuple-element.23.refs_0_), channel_id=1, source_target_pairs={{1,2},{2,1},{5,6},{6,5},{9,10},{10,9},{13,14},{14,13},{17,18},{18,... | collective-permute-start | bytes 786440 | tf_op jit(solution)/shard_map/ppermute | solution.py:327
  48.5 20.5 %collective-permute-start.25 = (bf16[768,512]{1,0:T(8,128)(2,1)S(1)}, bf16[768,512]{1,0:T(8,128)(2,1)S(1)}, u32[]{:S(2)}, u32[]{:S(2)}) collective-permute-start(bf16[768,512]{1,0:T(8,128)(2,1)S(1)} %copy-done.1), channel_id=1, source_target_pairs={{0,16},{4,20},{8,24},{12,28},{16,0},{20,4},{24,8},{28,12},{1,17},{... | collective-permute-start | bytes 2359304 | tf_op jit(solution)/shard_map/ppermute | solution.py:297
  49.1 35.9 %collective-permute-start.18 = (bf16[512,768]{1,0:T(8,128)(2,1)S(1)}, bf16[512,768]{1,0:T(8,128)(2,1)S(1)}, u32[]{:S(2)}, u32[]{:S(2)}) collective-permute-start(bf16[512,768]{1,0:T(8,128)(2,1)S(1)} %copy-done), channel_id=1, source_target_pairs={{0,16},{4,20},{8,24},{12,28},{16,0},{20,4},{24,8},{28,12},{1,17},{... | collective-permute-start | bytes 2359304 | tf_op jit(solution)/shard_map/ppermute | solution.py:297
  54.9 30.8 %collective-permute-start.23 = (bf16[768,512]{1,0:T(8,128)(2,1)S(1)}, bf16[768,512]{1,0:T(8,128)(2,1)S(1)}, u32[]{:S(2)}, u32[]{:S(2)}) collective-permute-start(bf16[768,512]{1,0:T(8,128)(2,1)S(1)} %copy-done.1), channel_id=1, source_target_pairs={{0,8},{4,12},{8,0},{12,4},{16,24},{20,28},{24,16},{28,20},{1,9},{5... | collective-permute-start | bytes 2359304 | tf_op jit(solution)/shard_map/ppermute | solution.py:297
  56.4 29.9 %collective-permute-start.15 = (bf16[512,768]{1,0:T(8,128)(2,1)S(1)}, bf16[512,768]{1,0:T(8,128)(2,1)S(1)}, u32[]{:S(2)}, u32[]{:S(2)}) collective-permute-start(bf16[512,768]{1,0:T(8,128)(2,1)S(1)} %copy-done), channel_id=1, source_target_pairs={{0,4},{4,0},{8,12},{12,8},{16,20},{20,16},{24,28},{28,24},{1,5},{5... | collective-permute-start | bytes 2359304 | tf_op jit(solution)/shard_map/ppermute | solution.py:297
  56.4 31.2 %collective-permute-start.22 = (bf16[768,512]{1,0:T(8,128)(2,1)S(1)}, bf16[768,512]{1,0:T(8,128)(2,1)S(1)}, u32[]{:S(2)}, u32[]{:S(2)}) collective-permute-start(bf16[768,512]{1,0:T(8,128)(2,1)S(1)} %copy-done.1), channel_id=1, source_target_pairs={{0,4},{4,0},{8,12},{12,8},{16,20},{20,16},{24,28},{28,24},{1,5},{5... | collective-permute-start | bytes 2359304 | tf_op jit(solution)/shard_map/ppermute | solution.py:297
  69.0 19.3 %collective-permute-start.10 = (bf16[256,512]{1,0:T(8,128)(2,1)S(1)}, bf16[256,512]{1,0:T(8,128)(2,1)S(1)}, u32[]{:S(2)}, u32[]{:S(2)}) collective-permute-start(bf16[256,512]{1,0:T(8,128)(2,1)S(1)} %get-tuple-element.24.refs_6_), channel_id=1, source_target_pairs={{0,1},{1,0},{2,3},{3,2},{4,5},{5,4},{6,7},{7,6},{8,9},{9,8},{10,11... | collective-permute-start | bytes 786440 | tf_op jit(solution)/shard_map/ppermute | solution.py:297
  85.0 4.8 %collective-permute-start.12 = (bf16[256,512]{1,0:T(8,128)(2,1)S(1)}, bf16[256,512]{1,0:T(8,128)(2,1)S(1)}, u32[]{:S(2)}, u32[]{:S(2)}) collective-permute-start(bf16[256,512]{1,0:T(8,128)(2,1)S(1)} %get-tuple-element.24.refs_6_), channel_id=1, source_target_pairs={{1,2},{2,1},{5,6},{6,5},{9,10},{10,9},{13,14},{14,13},{17,18},{18,... | collective-permute-start | bytes 786440 | tf_op jit(solution)/shard_map/ppermute | solution.py:327
  85.7 4.1 %collective-permute-start.6 = (bf16[256,512]{1,0:T(8,128)(2,1)S(1)}, bf16[256,512]{1,0:T(8,128)(2,1)S(1)}, u32[]{:S(2)}, u32[]{:S(2)}) collective-permute-start(bf16[256,512]{1,0:T(8,128)(2,1)S(1)} %collective-permute-done.5.refs_1_), channel_id=1, source_target_pairs={{1,2},{2,1},{5,6},{6,5},{9,10},{10,9},{13,14},{14,13},{17,18},{18,... | collective-permute-start | bytes 786440 | tf_op jit(solution)/shard_map/ppermute | solution.py:328
  86.4 14.9 %collective-permute-start.8 = (bf16[256,512]{1,0:T(8,128)(2,1)S(1)}, bf16[256,512]{1,0:T(8,128)(2,1)S(1)}, u32[]{:S(2)}, u32[]{:S(2)}) collective-permute-start(bf16[256,512]{1,0:T(8,128)(2,1)S(1)} %collective-permute-done.7.refs_4_), channel_id=1, source_target_pairs={{1,0},{2,3},{5,4},{6,7},{9,8},{10,11},{13,12},{14,15},{17,16},{18,... | collective-permute-start | bytes 786440 | tf_op jit(solution)/shard_map/ppermute | solution.py:329
  87.7 35.9 %collective-permute-start.20 = (bf16[512,768]{1,0:T(8,128)(2,1)S(1)}, bf16[512,768]{1,0:T(8,128)(2,1)S(1)}, u32[]{:S(2)}, u32[]{:S(2)}) collective-permute-start(bf16[512,768]{1,0:T(8,128)(2,1)S(1)} %collective-permute-done.16.refs_14_), channel_id=1, source_target_pairs={{0,16},{4,20},{8,24},{12,28},{16,0},{20,4},{24,8},{28,12},{1,17},{... | collective-permute-start | bytes 2359304 | tf_op jit(solution)/shard_map/ppermute | solution.py:297
  88.3 35.7 %collective-permute-start.27 = (bf16[768,512]{1,0:T(8,128)(2,1)S(1)}, bf16[768,512]{1,0:T(8,128)(2,1)S(1)}, u32[]{:S(2)}, u32[]{:S(2)}) collective-permute-start(bf16[768,512]{1,0:T(8,128)(2,1)S(1)} %collective-permute-done.25.refs_24_), channel_id=1, source_target_pairs={{0,8},{4,12},{8,0},{12,4},{16,24},{20,28},{24,16},{28,20},{1,9},{5... | collective-permute-start | bytes 2359304 | tf_op jit(solution)/shard_map/ppermute | solution.py:297
  89.8 34.4 %collective-permute-start.17 = (bf16[512,768]{1,0:T(8,128)(2,1)S(1)}, bf16[512,768]{1,0:T(8,128)(2,1)S(1)}, u32[]{:S(2)}, u32[]{:S(2)}) collective-permute-start(bf16[512,768]{1,0:T(8,128)(2,1)S(1)} %collective-permute-done.16.refs_14_), channel_id=1, source_target_pairs={{0,4},{4,0},{8,12},{12,8},{16,20},{20,16},{24,28},{28,24},{1,5},{5... | collective-permute-start | bytes 2359304 | tf_op jit(solution)/shard_map/ppermute | solution.py:297
  89.8 12.8 %collective-permute-start.11 = (bf16[256,512]{1,0:T(8,128)(2,1)S(1)}, bf16[256,512]{1,0:T(8,128)(2,1)S(1)}, u32[]{:S(2)}, u32[]{:S(2)}) collective-permute-start(bf16[256,512]{1,0:T(8,128)(2,1)S(1)} %collective-permute-done.10.refs_7_), channel_id=1, source_target_pairs={{1,2},{2,1},{5,6},{6,5},{9,10},{10,9},{13,14},{14,13},{17,18},{18,... | collective-permute-start | bytes 786440 | tf_op jit(solution)/shard_map/ppermute | solution.py:328
  101.2 11.8 %collective-permute-start.13 = (bf16[256,512]{1,0:T(8,128)(2,1)S(1)}, bf16[256,512]{1,0:T(8,128)(2,1)S(1)}, u32[]{:S(2)}, u32[]{:S(2)}) collective-permute-start(bf16[256,512]{1,0:T(8,128)(2,1)S(1)} %collective-permute-done.12.refs_10_), channel_id=1, source_target_pairs={{1,0},{2,3},{5,4},{6,7},{9,8},{10,11},{13,12},{14,15},{17,16},{18,... | collective-permute-start | bytes 786440 | tf_op jit(solution)/shard_map/ppermute | solution.py:329
  102.5 18.1 %collective-permute-start.9 = (bf16[256,512]{1,0:T(8,128)(2,1)S(1)}, bf16[256,512]{1,0:T(8,128)(2,1)S(1)}, u32[]{:S(2)}, u32[]{:S(2)}) collective-permute-start(bf16[256,512]{1,0:T(8,128)(2,1)S(1)} %collective-permute-done.6.refs_2_), channel_id=1, source_target_pairs={{1,0},{2,3},{5,4},{6,7},{9,8},{10,11},{13,12},{14,15},{17,16},{18,... | collective-permute-start | bytes 786440 | tf_op jit(solution)/shard_map/ppermute | solution.py:330
  113.0 10.5 %collective-permute-start.14 = (bf16[256,512]{1,0:T(8,128)(2,1)S(1)}, bf16[256,512]{1,0:T(8,128)(2,1)S(1)}, u32[]{:S(2)}, u32[]{:S(2)}) collective-permute-start(bf16[256,512]{1,0:T(8,128)(2,1)S(1)} %collective-permute-done.11.refs_8_), channel_id=1, source_target_pairs={{1,0},{2,3},{5,4},{6,7},{9,8},{10,11},{13,12},{14,15},{17,16},{18,... | collective-permute-start | bytes 786440 | tf_op jit(solution)/shard_map/ppermute | solution.py:330
  120.6 4.0 %collective-permute-start.26 = (bf16[768,512]{1,0:T(8,128)(2,1)S(1)}, bf16[768,512]{1,0:T(8,128)(2,1)S(1)}, u32[]{:S(2)}, u32[]{:S(2)}) collective-permute-start(bf16[768,512]{1,0:T(8,128)(2,1)S(1)} %collective-permute-done.25.refs_24_), channel_id=1, source_target_pairs={{0,4},{4,0},{8,12},{12,8},{16,20},{20,16},{24,28},{28,24},{1,5},{5... | collective-permute-start | bytes 2359304 | tf_op jit(solution)/shard_map/ppermute | solution.py:297
  123.5 2.3 %collective-permute-start.19 = (bf16[512,768]{1,0:T(8,128)(2,1)S(1)}, bf16[512,768]{1,0:T(8,128)(2,1)S(1)}, u32[]{:S(2)}, u32[]{:S(2)}) collective-permute-start(bf16[512,768]{1,0:T(8,128)(2,1)S(1)} %collective-permute-done.18.refs_16_), channel_id=1, source_target_pairs={{0,4},{4,0},{8,12},{12,8},{16,20},{20,16},{24,28},{28,24},{1,5},{5... | collective-permute-start | bytes 2359304 | tf_op jit(solution)/shard_map/ppermute | solution.py:297
  123.6 3.4 %collective-permute-start.24 = (bf16[768,512]{1,0:T(8,128)(2,1)S(1)}, bf16[768,512]{1,0:T(8,128)(2,1)S(1)}, u32[]{:S(2)}, u32[]{:S(2)}) collective-permute-start(bf16[768,512]{1,0:T(8,128)(2,1)S(1)} %collective-permute-done.23.refs_22_), channel_id=1, source_target_pairs={{0,4},{4,0},{8,12},{12,8},{16,20},{20,16},{24,28},{28,24},{1,5},{5... | collective-permute-start | bytes 2359304 | tf_op jit(solution)/shard_map/ppermute | solution.py:297
  124.1 4.0 %collective-permute-start.21 = (bf16[512,768]{1,0:T(8,128)(2,1)S(1)}, bf16[512,768]{1,0:T(8,128)(2,1)S(1)}, u32[]{:S(2)}, u32[]{:S(2)}) collective-permute-start(bf16[512,768]{1,0:T(8,128)(2,1)S(1)} %collective-permute-done.20.refs_18_), channel_id=1, source_target_pairs={{0,4},{4,0},{8,12},{12,8},{16,20},{20,16},{24,28},{28,24},{1,5},{5... | collective-permute-start | bytes 2359304 | tf_op jit(solution)/shard_map/ppermute | solution.py:297
  124.1 5.1 %collective-permute-start.28 = (bf16[768,512]{1,0:T(8,128)(2,1)S(1)}, bf16[768,512]{1,0:T(8,128)(2,1)S(1)}, u32[]{:S(2)}, u32[]{:S(2)}) collective-permute-start(bf16[768,512]{1,0:T(8,128)(2,1)S(1)} %collective-permute-done.27.refs_26_), channel_id=1, source_target_pairs={{0,4},{4,0},{8,12},{12,8},{16,20},{20,16},{24,28},{28,24},{1,5},{5... | collective-permute-start | bytes 2359304 | tf_op jit(solution)/shard_map/ppermute | solution.py:297
  131.9 8.1 %collective-permute-start.36 = (bf16[128,1024]{1,0:T(8,128)(2,1)S(1)}, bf16[128,1024]{1,0:T(8,128)(2,1)S(1)}, u32[]{:S(2)}, u32[]{:S(2)}) collective-permute-start(bf16[128,1024]{1,0:T(8,128)(2,1)S(1)} %get-tuple-element.30), channel_id=1, source_target_pairs={{0,1},{3,2},{4,5},{7,6},{8,9},{11,10},{12,13},{15,14},{16,17},{19,... | collective-permute-start | bytes 786440 | tf_op jit(solution)/shard_map/ppermute | solution.py:341
  136.0 9.6 %collective-permute-start.31 = (bf16[128,1024]{1,0:T(8,128)(2,1)S(1)}, bf16[128,1024]{1,0:T(8,128)(2,1)S(1)}, u32[]{:S(2)}, u32[]{:S(2)}) collective-permute-start(bf16[128,1024]{1,0:T(8,128)(2,1)S(1)} %get-tuple-element.26), channel_id=1, source_target_pairs={{0,1},{3,2},{4,5},{7,6},{8,9},{11,10},{12,13},{15,14},{16,17},{19,... | collective-permute-start | bytes 786440 | tf_op jit(solution)/shard_map/ppermute | solution.py:341
  137.3 13.9 %collective-permute-start.34 = (bf16[128,1024]{1,0:T(8,128)(2,1)S(1)}, bf16[128,1024]{1,0:T(8,128)(2,1)S(1)}, u32[]{:S(2)}, u32[]{:S(2)}) collective-permute-start(bf16[128,1024]{1,0:T(8,128)(2,1)S(1)} %get-tuple-element.31), channel_id=1, source_target_pairs={{0,1},{3,2},{4,5},{7,6},{8,9},{11,10},{12,13},{15,14},{16,17},{19,... | collective-permute-start | bytes 786440 | tf_op jit(solution)/shard_map/ppermute | solution.py:342
  138.7 17.5 %collective-permute-start.29 = (bf16[128,1024]{1,0:T(8,128)(2,1)S(1)}, bf16[128,1024]{1,0:T(8,128)(2,1)S(1)}, u32[]{:S(2)}, u32[]{:S(2)}) collective-permute-start(bf16[128,1024]{1,0:T(8,128)(2,1)S(1)} %get-tuple-element.27), channel_id=1, source_target_pairs={{0,1},{3,2},{4,5},{7,6},{8,9},{11,10},{12,13},{15,14},{16,17},{19,... | collective-permute-start | bytes 786440 | tf_op jit(solution)/shard_map/ppermute | solution.py:342
  140.1 29.0 %copy-start.9 = (f32[1024]{0:T(1024)S(1)}, f32[1024]{0:T(1024)}, u32[]{:S(2)}) copy-start(f32[1024]{0:T(1024)} %param.25) | copy-start | bytes 12292
  140.1 21.9 %collective-permute-start.37 = (bf16[128,1024]{1,0:T(8,128)(2,1)S(1)}, bf16[128,1024]{1,0:T(8,128)(2,1)S(1)}, u32[]{:S(2)}, u32[]{:S(2)}) collective-permute-start(bf16[128,1024]{1,0:T(8,128)(2,1)S(1)} %add_convert_fusion.1), channel_id=1, source_target_pairs={{1,2},{2,1},{5,6},{6,5},{9,10},{10,9},{13,14},{14,13},{17,18},{18,... | collective-permute-start | bytes 786440 | tf_op jit(solution)/shard_map/ppermute | solution.py:343
  145.7 11.2 %collective-permute-start.32 = (bf16[128,1024]{1,0:T(8,128)(2,1)S(1)}, bf16[128,1024]{1,0:T(8,128)(2,1)S(1)}, u32[]{:S(2)}, u32[]{:S(2)}) collective-permute-start(bf16[128,1024]{1,0:T(8,128)(2,1)S(1)} %add_convert_fusion.4), channel_id=1, source_target_pairs={{1,2},{2,1},{5,6},{6,5},{9,10},{10,9},{13,14},{14,13},{17,18},{18,... | collective-permute-start | bytes 786440 | tf_op jit(solution)/shard_map/ppermute | solution.py:343
  151.3 19.5 %collective-permute-start.35 = (bf16[128,1024]{1,0:T(8,128)(2,1)S(1)}, bf16[128,1024]{1,0:T(8,128)(2,1)S(1)}, u32[]{:S(2)}, u32[]{:S(2)}) collective-permute-start(bf16[128,1024]{1,0:T(8,128)(2,1)S(1)} %add_convert_fusion.2), channel_id=1, source_target_pairs={{1,2},{2,1},{5,6},{6,5},{9,10},{10,9},{13,14},{14,13},{17,18},{18,... | collective-permute-start | bytes 786440 | tf_op jit(solution)/shard_map/ppermute | solution.py:344
  156.2 5.9 %collective-permute-start.30 = (bf16[128,1024]{1,0:T(8,128)(2,1)S(1)}, bf16[128,1024]{1,0:T(8,128)(2,1)S(1)}, u32[]{:S(2)}, u32[]{:S(2)}) collective-permute-start(bf16[128,1024]{1,0:T(8,128)(2,1)S(1)} %add_convert_fusion.5), channel_id=1, source_target_pairs={{1,2},{2,1},{5,6},{6,5},{9,10},{10,9},{13,14},{14,13},{17,18},{18,... | collective-permute-start | bytes 786440 | tf_op jit(solution)/shard_map/ppermute | solution.py:344
  157.0 12.1 %collective-permute-start.33 = (bf16[128,1024]{1,0:T(8,128)(2,1)S(1)}, bf16[128,1024]{1,0:T(8,128)(2,1)S(1)}, u32[]{:S(2)}, u32[]{:S(2)}) collective-permute-start(bf16[128,1024]{1,0:T(8,128)(2,1)S(1)} %add_convert_fusion.3), channel_id=1, source_target_pairs={{0,1},{1,0},{2,3},{3,2},{4,5},{5,4},{6,7},{7,6},{8,9},{9,8},{10,11... | collective-permute-start | bytes 786440 | tf_op jit(solution)/shard_map/ppermute | solution.py:297
  162.0 11.1 %collective-permute-start.38 = (bf16[128,1024]{1,0:T(8,128)(2,1)S(1)}, bf16[128,1024]{1,0:T(8,128)(2,1)S(1)}, u32[]{:S(2)}, u32[]{:S(2)}) collective-permute-start(bf16[128,1024]{1,0:T(8,128)(2,1)S(1)} %add_convert_fusion), channel_id=1, source_target_pairs={{0,1},{1,0},{2,3},{3,2},{4,5},{5,4},{6,7},{7,6},{8,9},{9,8},{10,11... | collective-permute-start | bytes 786440 | tf_op jit(solution)/shard_map/ppermute | solution.py:297

commit v6 on v5

--- a/solution.py
+++ b/solution.py
@@ -277,6 +277,27 @@
         o_ref[:, lanes] = (rests[q][...].astype(F32) + prob * token).astype(BF16)
 
 
+def last_kernel(slot_ref, prob_ref, rest_ref, *refs, base, span):
+    terms = refs[:-3]
+    o_hbm, out, sem = refs[-3:]
+    total = terms[0][...].astype(F32)
+    for other in terms[1:]:
+        total = total + other[...].astype(F32)
+    sums = total.astype(BF16)
+    rows = sums.shape[0]
+    copies = []
+    for k in range(out.shape[0] // span):
+        lines = slice(k * span, (k + 1) * span)
+        slot = turned(slot_ref[:, lines].astype(F32)).astype(jnp.int32)
+        pick = (iota((span, rows), 1) + base == slot).astype(BF16)
+        token = jnp.dot(pick, sums, preferred_element_type=F32)
+        out[lines, :] = (rest_ref[lines, :].astype(F32) + turned(prob_ref[:, lines]) * token).astype(BF16)
+        copies.append(pltpu.make_async_copy(out.at[pl.ds(k * span, span)], o_hbm.at[pl.ds(k * span, span)], sem.at[k]))
+        copies[k].start()
+    for copy in copies:
+        copy.wait()
+
+
 def params(size=16):
     return pltpu.CompilerParams(vmem_limit_bytes=size * MIB)
 
@@ -453,14 +474,14 @@
             functools.partial(norm_kernel, width=width),
             grid_spec=pltpu.PrefetchScalarGridSpec(
                 num_scalar_prefetch=1,
-                grid=(tokens // wide,),
-                in_specs=[rows_spec(wide, states), pl.BlockSpec((wide, half), block), pl.BlockSpec((wide, half), block),
-                          pl.BlockSpec((1, half), col), cols_spec(1, wide)] + entry,
-                out_specs=[rows_spec(wide, half), whole((CAP, half))],
+                grid=(tokens // tokens,),
+                in_specs=[rows_spec(tokens, states), pl.BlockSpec((tokens, half), block), pl.BlockSpec((tokens, half), block),
+                          pl.BlockSpec((1, half), col), cols_spec(1, tokens)] + entry,
+                out_specs=[rows_spec(tokens, half), whole((CAP, half))],
                 scratch_shapes=[pltpu.VMEM((CAP, half), F32), pltpu.VMEM((states, half), BF16)],
             ),
             out_shape=[jax.ShapeDtypeStruct((tokens, half), BF16), jax.ShapeDtypeStruct((CAP, half), BF16)],
-            compiler_params=params(),
+            compiler_params=params(24),
         )(flip, state_output, local, weight, norm_gain[None], expert_slot[None], *values)
         normed.append(outs[0])
         dispatched.append(outs[1])
@@ -493,11 +514,11 @@
                 ],
             ),
             out_shape=[jax.ShapeDtypeStruct((rows, chans), BF16)] * ring,
-            compiler_params=params(26),
+            compiler_params=params(10),
         )(flip, *pieces, *ups, *downs)
         summed.append(sum_line(terms, ring))
 
-    for part in range(parts):
+    for part in range(parts - 1):
         rests = [pl.pallas_call(
             functools.partial(final_kernel, base=part * rows, count=len(rests)),
             grid_spec=pltpu.PrefetchScalarGridSpec(
@@ -512,7 +533,16 @@
             out_shape=jax.ShapeDtypeStruct((tokens, chans), BF16),
             compiler_params=params(),
         )(flip, expert_slot[None], gate_prob[None], *rests, *summed[part])]
-    return rests[0]
+    chip = pl.BlockSpec(memory_space=pltpu.VMEM)
+    return pl.pallas_call(
+        functools.partial(last_kernel, base=(parts - 1) * rows, span=span),
+        in_specs=[chip] * (3 + len(summed[-1])),
+        out_specs=pl.BlockSpec(memory_space=pl.ANY),
+        scratch_shapes=[pltpu.VMEM((tokens, chans), BF16), pltpu.SemaphoreType.DMA((tokens // span,))],
+        out_shape=jax.ShapeDtypeStruct((tokens, chans), BF16),
+        compiler_params=params(),
+        name="combineB",
+    )(expert_slot[None], gate_prob[None], *rests, *summed[-1])
 
 
 def solution(mesh):

time: 176 us -> 175 us (level)
    pallas_call x2 -> x1, Pallas kernels: 4.4 us -> 1.74 us  [body(): pl.pallas_call(functools.partial(final_kernel, base=part * rows, count=le...]
    pallas_call x0 -> x1, Pallas kernels: none -> 2.22 us  [body(): pl.pallas_call(functools.partial(last_kernel, base=(parts - 1) * rows, sp...]
  transfers between devices with their start and end apart: 39 -> 39, of which waited for: 18 -> 18; matrix products, arithmetic and copies ran while one was open for 0% -> 0% of each run, Pallas kernels for 11% -> 10%
where the time goes in v6:
time: 175 us
  waiting for transfers between devices  105 us (60%)
  starting transfers between devices  40.9 us (23%)
  Pallas kernels  27.3 us (16%)
    ppermute x23, waiting for transfers between devices, swap(): return lax.ppermute(value, axis, [(i, i ^ mask) for i in range(count)])  61.6 us
    ppermute x23, starting transfers between devices, swap(): return lax.ppermute(value, axis, [(i, i ^ mask) for i in range(count)])  25 us
    ppermute x2, waiting for transfers between devices, gather_line(): out_near = lax.ppermute(cross, 'exp', OUTWARD)  20 us
    pallas_call x1, Pallas kernels, body(): pl.pallas_call(functools.partial(local_kernel, blk=blk), grid=(tokens //...  9.96 us
    ppermute x2, waiting for transfers between devices, gather_line(): out_far = lax.ppermute(cross_far, 'exp', OUTWARD)  9.29 us
    ppermute x2, waiting for transfers between devices, sum_line(): near = lax.ppermute(terms[2], 'exp', ENDS)  9.02 us
    pallas_call x2, Pallas kernels, body(): pl.pallas_call(functools.partial(expert_kernel, ring=ring, shards=ctx, gr...  5.33 us
    pallas_call x1, Pallas kernels, body(): pl.pallas_call(functools.partial(end_kernel, blk=blk), grid=(tokens // sp...  5.12 us
  transfers between devices with their start and end apart: 39, of which 18 were waited for; matrix products, arithmetic and copies ran while one was open for 0% of the time, Pallas kernels for 10%

profile of v6, /device:TPU:0, one launch (start us, length us, event | category | flops | bytes accessed | tf_op | source)
XLA Modules:
  0.0 174.9 jit_solution(14340553042545916302)
XLA Ops:
  0.0 5.1 %end_state.1.own_ref = bf16[144,1024]{1,0:T(8,128)(2,1)} custom-call(bf16[1024,1024]{1,0:T(8,128)(2,1)} %x_ref.3, bf16[1024,128]{1,0:T(8,128)(2,1)} %b_ref.3, f32[16,1024]{1,0:T(8,128)} %st_ref.3, f32[16,1024]{1,0:T(8,128)} %dl_ref.3, s32[8,16]{1,0:T(8,128)} %sc_ref.3), custom_call_target="tpu_custom_call" | custom-call | tf_op jit(solution)/shard_map/end_state/pallas_call | solution.py:415
  5.2 0.5 collective-permute-start
  5.7 2.5 %collective-permute-start.16 = (bf16[512,768]{1,0:T(8,128)(2,1)S(1)}, bf16[512,768]{1,0:T(8,128)(2,1)S(1)}, u32[]{:S(2)}, u32[]{:S(2)}) collective-permute-start(bf16[512,768]{1,0:T(8,128)(2,1)S(1)} %copy-done), channel_id=1, source_target_pairs={{0,8},{4,12},{8,0},{12,4},{16,24},{20,28},{24,16},{28,20},{1,9},{5... | collective-permute-start | bytes 2359304 | tf_op jit(solution)/shard_map/ppermute | solution.py:318
  8.2 1.0 copy-done.3
  9.2 0.1 chip_state.1
  9.3 1.8 %collective-permute-start.1 = (bf16[144,512]{1,0:T(8,128)(2,1)S(1)}, bf16[144,512]{1,0:T(8,128)(2,1)S(1)}, u32[]{:S(2)}, u32[]{:S(2)}) collective-permute-start(bf16[144,512]{1,0:T(8,128)(2,1)S(1)} %chip_state.1), channel_id=1, source_target_pairs={{0,8},{4,12},{8,0},{12,4},{16,24},{20,28},{24,16},{28,20},{1,9},{5... | collective-permute-start | bytes 442376 | tf_op jit(solution)/shard_map/ppermute | solution.py:318
  11.0 1.5 collective-permute-start.2
  12.6 0.2 collective-permute-start.3
  12.8 17.0 %collective-permute-done.1.refs_0_ = bf16[144,512]{1,0:T(8,128)(2,1)S(1)} collective-permute-done((bf16[144,512]{1,0:T(8,128)(2,1)S(1)}, bf16[144,512]{1,0:T(8,128)(2,1)S(1)}, u32[]{:S(2)}, u32[]{:S(2)}) %collective-permute-start.1) | collective-permute-done | bytes 147488 | tf_op jit(solution)/shard_map/ppermute | solution.py:318
  29.8 4.1 %collective-permute-done.3.refs_2_ = bf16[144,512]{1,0:T(8,128)(2,1)S(1)} collective-permute-done((bf16[144,512]{1,0:T(8,128)(2,1)S(1)}, bf16[144,512]{1,0:T(8,128)(2,1)S(1)}, u32[]{:S(2)}, u32[]{:S(2)}) %collective-permute-start.3) | collective-permute-done | bytes 147488 | tf_op jit(solution)/shard_map/ppermute | solution.py:318
  33.9 0.1 prior.1.h_ref
  34.0 0.1 collective-permute-start.4
  34.2 10.0 %local_out.1 = (bf16[1024,1024]{1,0:T(8,128)(2,1)S(1)}, bf16[1024,1024]{1,0:T(8,128)(2,1)S(1)}) custom-call(bf16[1024,1024]{1,0:T(8,128)(2,1)} %x_ref.3, bf16[1024,1024]{1,0:T(8,128)(2,1)} %g_ref.1, bf16[1024,128]{1,0:T(8,128)(2,1)S(1)} %copy-done.4, bf16[1024,128]{1,0:T(8,128)(2,1)S(1)} %copy-done.2, f32[16,1024]{1,0:T(8,128)S(1)} %copy-done.5, ...), custom_call_target="tpu_custom_call" | custom-call | tf_op jit(solution)/shard_map/local_out/pallas_call | solution.py:444
  44.2 1.4 shard_map.127
  45.5 1.6 collective-permute-start.5
  47.2 0.7 collective-permute-start.7
  47.9 0.6 collective-permute-start.25
  48.5 1.5 collective-permute-start.18
  50.0 4.3 %collective-permute-done.5.refs_1_ = bf16[256,512]{1,0:T(8,128)(2,1)S(1)} collective-permute-done((bf16[256,512]{1,0:T(8,128)(2,1)S(1)}, bf16[256,512]{1,0:T(8,128)(2,1)S(1)}, u32[]{:S(2)}, u32[]{:S(2)}) %collective-permute-start.5) | collective-permute-done | bytes 262176 | tf_op jit(solution)/shard_map/ppermute | solution.py:318
  54.3 1.6 collective-permute-start.23
  55.8 0.5 collective-permute-start.22
  56.3 1.4 shard_map.128
  57.7 10.6 %collective-permute-done.25.refs_24_ = bf16[768,512]{1,0:T(8,128)(2,1)S(1)} collective-permute-done((bf16[768,512]{1,0:T(8,128)(2,1)S(1)}, bf16[768,512]{1,0:T(8,128)(2,1)S(1)}, u32[]{:S(2)}, u32[]{:S(2)}) %collective-permute-start.25) | collective-permute-done | bytes 786464 | tf_op jit(solution)/shard_map/ppermute | solution.py:318
  68.4 4.4 %collective-permute-start.10 = (bf16[256,512]{1,0:T(8,128)(2,1)S(1)}, bf16[256,512]{1,0:T(8,128)(2,1)S(1)}, u32[]{:S(2)}, u32[]{:S(2)}) collective-permute-start(bf16[256,512]{1,0:T(8,128)(2,1)S(1)} %get-tuple-element.24.refs_6_), channel_id=1, source_target_pairs={{0,1},{1,0},{2,3},{3,2},{4,5},{5,4},{6,7},{7,6},{8,9},{9,8},{10,11... | collective-permute-start | bytes 786440 | tf_op jit(solution)/shard_map/ppermute | solution.py:318
  72.7 11.7 %collective-permute-done.18.refs_16_ = bf16[512,768]{1,0:T(8,128)(2,1)S(1)} collective-permute-done((bf16[512,768]{1,0:T(8,128)(2,1)S(1)}, bf16[512,768]{1,0:T(8,128)(2,1)S(1)}, u32[]{:S(2)}, u32[]{:S(2)}) %collective-permute-start.18) | collective-permute-done | bytes 786464 | tf_op jit(solution)/shard_map/ppermute | solution.py:318
  84.4 0.7 collective-permute-start.12
  85.1 0.7 collective-permute-start.6
  85.8 1.3 collective-permute-start.8
  87.1 0.6 collective-permute-start.20
  87.7 1.4 collective-permute-start.27
  89.2 0.7 collective-permute-start.11
  89.9 10.8 %collective-permute-done.8.refs_3_ = bf16[256,512]{1,0:T(8,128)(2,1)S(1)} collective-permute-done((bf16[256,512]{1,0:T(8,128)(2,1)S(1)}, bf16[256,512]{1,0:T(8,128)(2,1)S(1)}, u32[]{:S(2)}, u32[]{:S(2)}) %collective-permute-start.8) | collective-permute-done | bytes 262176 | tf_op jit(solution)/shard_map/ppermute | solution.py:350
  100.7 1.3 collective-permute-start.13
  102.0 1.3 collective-permute-start.9
  103.3 9.2 %collective-permute-done.13.refs_9_ = bf16[256,512]{1,0:T(8,128)(2,1)S(1)} collective-permute-done((bf16[256,512]{1,0:T(8,128)(2,1)S(1)}, bf16[256,512]{1,0:T(8,128)(2,1)S(1)}, u32[]{:S(2)}, u32[]{:S(2)}) %collective-permute-start.13) | collective-permute-done | bytes 262176 | tf_op jit(solution)/shard_map/ppermute | solution.py:350
  112.5 1.3 collective-permute-start.14
  113.7 6.3 %collective-permute-done.9.refs_5_ = bf16[256,512]{1,0:T(8,128)(2,1)S(1)} collective-permute-done((bf16[256,512]{1,0:T(8,128)(2,1)S(1)}, bf16[256,512]{1,0:T(8,128)(2,1)S(1)}, u32[]{:S(2)}, u32[]{:S(2)}) %collective-permute-start.9) | collective-permute-done | bytes 262176 | tf_op jit(solution)/shard_map/ppermute | solution.py:351
  120.1 2.9 %collective-permute-done.14.refs_11_ = bf16[256,512]{1,0:T(8,128)(2,1)S(1)} collective-permute-done((bf16[256,512]{1,0:T(8,128)(2,1)S(1)}, bf16[256,512]{1,0:T(8,128)(2,1)S(1)}, u32[]{:S(2)}, u32[]{:S(2)}) %collective-permute-start.14) | collective-permute-done | bytes 262176 | tf_op jit(solution)/shard_map/ppermute | solution.py:351
  123.0 0.5 collective-permute-start.24
  123.6 0.1 collective-permute-start.21
  123.6 0.4 collective-permute-start.28
  124.1 1.2 collective-permute-done.19.refs_17_
  125.3 1.1 collective-permute-done.24.refs_23_
  126.4 1.1 collective-permute-done.21.refs_19_
  127.6 1.1 collective-permute-done.28.refs_27_
  128.7 2.6 %shard_map.131 = (bf16[128,1024]{1,0:T(8,128)(2,1)S(1)}, bf16[128,1024]{1,0:T(8,128)(2,1)S(1)}, bf16[128,1024]{1,0:T(8,128)(2,1)S(1)}, bf16[128,1024]{1,0:T(8,128)(2,1)S(1)}) custom-call(s32[1]{0:T(128)} %bitcast.2.flip_ref, bf16[256,512]{1,0:T(8,128)(2,1)S(1)} %get-tuple-element.23.refs_0_, bf16[256,512]{1,0:T(8,128)(2,1)S(1)} %collective-permute-done.5.refs_1_, ...), custom_call_target="tpu_custom_call" | custom-call | tf_op jit(solution)/shard_map/pallas_call | solution.py:503
  131.4 1.5 collective-permute-start.36
  132.8 2.7 %shard_map.129 = (bf16[128,1024]{1,0:T(8,128)(2,1)S(1)}, bf16[128,1024]{1,0:T(8,128)(2,1)S(1)}, bf16[128,1024]{1,0:T(8,128)(2,1)S(1)}, bf16[128,1024]{1,0:T(8,128)(2,1)S(1)}) custom-call(s32[1]{0:T(128)} %bitcast.2.flip_ref, bf16[256,512]{1,0:T(8,128)(2,1)S(1)} %get-tuple-element.23.refs_0_, bf16[256,512]{1,0:T(8,128)(2,1)S(1)} %collective-permute-done.5.refs_1_, ...), custom_call_target="tpu_custom_call" | custom-call | tf_op jit(solution)/shard_map/pallas_call | solution.py:503
  135.5 1.3 collective-permute-start.31
  136.8 1.3 collective-permute-start.34
  138.2 1.3 collective-permute-start.29
  139.6 0.7 collective-permute-start.37
  140.3 4.8 %collective-permute-done.31 = bf16[128,1024]{1,0:T(8,128)(2,1)S(1)} collective-permute-done((bf16[128,1024]{1,0:T(8,128)(2,1)S(1)}, bf16[128,1024]{1,0:T(8,128)(2,1)S(1)}, u32[]{:S(2)}, u32[]{:S(2)}) %collective-permute-start.31) | collective-permute-done | bytes 262176 | tf_op jit(solution)/shard_map/ppermute | solution.py:362
  145.2 0.7 collective-permute-start.32
  145.9 4.9 %collective-permute-done.34 = bf16[128,1024]{1,0:T(8,128)(2,1)S(1)} collective-permute-done((bf16[128,1024]{1,0:T(8,128)(2,1)S(1)}, bf16[128,1024]{1,0:T(8,128)(2,1)S(1)}, u32[]{:S(2)}, u32[]{:S(2)}) %collective-permute-start.34) | collective-permute-done | bytes 262176 | tf_op jit(solution)/shard_map/ppermute | solution.py:363
  150.8 0.7 collective-permute-start.35
  151.5 4.2 %collective-permute-done.29 = bf16[128,1024]{1,0:T(8,128)(2,1)S(1)} collective-permute-done((bf16[128,1024]{1,0:T(8,128)(2,1)S(1)}, bf16[128,1024]{1,0:T(8,128)(2,1)S(1)}, u32[]{:S(2)}, u32[]{:S(2)}) %collective-permute-start.29) | collective-permute-done | bytes 262176 | tf_op jit(solution)/shard_map/ppermute | solution.py:363
  155.7 0.7 collective-permute-start.30
  156.5 5.0 %collective-permute-start.33 = (bf16[128,1024]{1,0:T(8,128)(2,1)S(1)}, bf16[128,1024]{1,0:T(8,128)(2,1)S(1)}, u32[]{:S(2)}, u32[]{:S(2)}) collective-permute-start(bf16[128,1024]{1,0:T(8,128)(2,1)S(1)} %add_convert_fusion.3), channel_id=1, source_target_pairs={{0,1},{1,0},{2,3},{3,2},{4,5},{5,4},{6,7},{7,6},{8,9},{9,8},{10,11... | collective-permute-start | bytes 786440 | tf_op jit(solution)/shard_map/ppermute | solution.py:318
  161.5 0.1 collective-permute-start.38
  161.6 7.0 %collective-permute-done.33.refs_4_ = bf16[128,1024]{1,0:T(8,128)(2,1)S(1)} collective-permute-done((bf16[128,1024]{1,0:T(8,128)(2,1)S(1)}, bf16[128,1024]{1,0:T(8,128)(2,1)S(1)}, u32[]{:S(2)}, u32[]{:S(2)}) %collective-permute-start.33) | collective-permute-done | bytes 262176 | tf_op jit(solution)/shard_map/ppermute | solution.py:318
  168.6 1.7 shard_map.130.rest_ref
  170.4 2.3 %collective-permute-done.38.refs_2_ = bf16[128,1024]{1,0:T(8,128)(2,1)S(1)} collective-permute-done((bf16[128,1024]{1,0:T(8,128)(2,1)S(1)}, bf16[128,1024]{1,0:T(8,128)(2,1)S(1)}, u32[]{:S(2)}, u32[]{:S(2)}) %collective-permute-start.38) | collective-permute-done | bytes 262176 | tf_op jit(solution)/shard_map/ppermute | solution.py:318
  172.7 2.2 %combineB.1 = bf16[1024,1024]{1,0:T(8,128)(2,1)} custom-call(s32[1,1024]{1,0:T(1,128)S(1)} %bitcast.8, f32[1,1024]{1,0:T(1,128)S(1)} %bitcast.12, bf16[1024,1024]{1,0:T(8,128)(2,1)S(1)} %shard_map.130.rest_ref, bf16[128,1024]{1,0:T(8,128)(2,1)S(1)} %get-tuple-element.29.refs_0_, bf16[128,1024]{1,0:T(8,128)(2,1)S(1)} %collective-permute-done.35.refs_1_, ...), custom_call_target="tpu_custom_call" | custom-call | tf_op jit(solution)/shard_map/combineB/pallas_call | solution.py:537
  (54 shorter events, 0.6 us)
Async XLA Ops:
  0.0 34.1 %copy-start.10 = (s32[8,16]{1,0:T(8,128)S(1)}, s32[8,16]{1,0:T(8,128)}, u32[]{:S(2)}) copy-start(s32[8,16]{1,0:T(8,128)} %sc_ref.3) | copy-start | bytes 1540
  0.0 34.1 %copy-start.5 = (f32[16,1024]{1,0:T(8,128)S(1)}, f32[16,1024]{1,0:T(8,128)}, u32[]{:S(2)}) copy-start(f32[16,1024]{1,0:T(8,128)} %st_ref.3) | copy-start | bytes 196612
  0.0 34.1 %copy-start.6 = (f32[16,1024]{1,0:T(8,128)S(1)}, f32[16,1024]{1,0:T(8,128)}, u32[]{:S(2)}) copy-start(f32[16,1024]{1,0:T(8,128)} %dl_ref.3) | copy-start | bytes 196612
  0.0 34.1 %copy-start.4 = (bf16[1024,128]{1,0:T(8,128)(2,1)S(1)}, bf16[1024,128]{1,0:T(8,128)(2,1)}, u32[]{:S(2)}) copy-start(bf16[1024,128]{1,0:T(8,128)(2,1)} %b_ref.3) | copy-start | bytes 786436
  0.0 5.7 %copy-start = (bf16[512,768]{1,0:T(8,128)(2,1)S(1)}, bf16[512,768]{1,0:T(8,128)(2,1)}, u32[]{:S(2)}) copy-start(bf16[512,768]{1,0:T(8,128)(2,1)} %refs_12_.3) | copy-start | bytes 2359300
  0.0 34.1 %copy-start.11 = (f32[16]{0:T(128)S(1)}, f32[16]{0:T(128)}, u32[]{:S(2)}) copy-start(f32[16]{0:T(128)} %param.19) | copy-start | bytes 196
  0.0 34.1 %copy-start.2 = (bf16[1024,128]{1,0:T(8,128)(2,1)S(1)}, bf16[1024,128]{1,0:T(8,128)(2,1)}, u32[]{:S(2)}) copy-start(bf16[1024,128]{1,0:T(8,128)(2,1)} %c_ref.5) | copy-start | bytes 786436
  5.2 3.1 %collective-permute-start = (bf16[144,1024]{1,0:T(8,128)(2,1)}, bf16[144,1024]{1,0:T(8,128)(2,1)S(1)}, u32[]{:S(2)}, u32[]{:S(2)}) collective-permute-start(bf16[144,1024]{1,0:T(8,128)(2,1)} %end_state.1.own_ref), channel_id=1, source_target_pairs={{0,4},{4,0},{8,12},{12,8},{16,20},{20,16},{24,28},{28,24},{1,5},{5... | collective-permute-start | bytes 884744 | tf_op jit(solution)/shard_map/ppermute | solution.py:318
  5.7 50.2 %collective-permute-start.16 = (bf16[512,768]{1,0:T(8,128)(2,1)S(1)}, bf16[512,768]{1,0:T(8,128)(2,1)S(1)}, u32[]{:S(2)}, u32[]{:S(2)}) collective-permute-start(bf16[512,768]{1,0:T(8,128)(2,1)S(1)} %copy-done), channel_id=1, source_target_pairs={{0,8},{4,12},{8,0},{12,4},{16,24},{20,28},{24,16},{28,20},{1,9},{5... | collective-permute-start | bytes 2359304 | tf_op jit(solution)/shard_map/ppermute | solution.py:318
  8.2 1.0 copy-start.3
  9.3 20.5 %collective-permute-start.1 = (bf16[144,512]{1,0:T(8,128)(2,1)S(1)}, bf16[144,512]{1,0:T(8,128)(2,1)S(1)}, u32[]{:S(2)}, u32[]{:S(2)}) collective-permute-start(bf16[144,512]{1,0:T(8,128)(2,1)S(1)} %chip_state.1), channel_id=1, source_target_pairs={{0,8},{4,12},{8,0},{12,4},{16,24},{20,28},{24,16},{28,20},{1,9},{5... | collective-permute-start | bytes 442376 | tf_op jit(solution)/shard_map/ppermute | solution.py:318
  11.0 18.7 %collective-permute-start.2 = (bf16[144,512]{1,0:T(8,128)(2,1)S(1)}, bf16[144,512]{1,0:T(8,128)(2,1)S(1)}, u32[]{:S(2)}, u32[]{:S(2)}) collective-permute-start(bf16[144,512]{1,0:T(8,128)(2,1)S(1)} %chip_state.1), channel_id=1, source_target_pairs={{0,16},{4,20},{8,24},{12,28},{16,0},{20,4},{24,8},{28,12},{1,17},{... | collective-permute-start | bytes 442376 | tf_op jit(solution)/shard_map/ppermute | solution.py:318
  12.6 21.3 %collective-permute-start.3 = (bf16[144,512]{1,0:T(8,128)(2,1)S(1)}, bf16[144,512]{1,0:T(8,128)(2,1)S(1)}, u32[]{:S(2)}, u32[]{:S(2)}) collective-permute-start(bf16[144,512]{1,0:T(8,128)(2,1)S(1)} %chip_state.1), channel_id=1, source_target_pairs={{0,24},{4,28},{8,16},{12,20},{16,8},{20,12},{24,0},{28,4},{1,25},{... | collective-permute-start | bytes 442376 | tf_op jit(solution)/shard_map/ppermute | solution.py:318
  34.0 14.5 %collective-permute-start.4 = (bf16[128,512]{1,0:T(8,128)(2,1)S(1)}, bf16[128,512]{1,0:T(8,128)(2,1)S(1)}, u32[]{:S(2)}, u32[]{:S(2)}) collective-permute-start(bf16[128,512]{1,0:T(8,128)(2,1)S(1)} %prior.1.h_ref), channel_id=1, source_target_pairs={{0,4},{4,0},{8,12},{12,8},{16,20},{20,16},{24,28},{28,24},{1,5},{5... | collective-permute-start | bytes 393224 | tf_op jit(solution)/shard_map/ppermute | solution.py:318
  34.1 10.0 %copy-start.7 = (s32[1024]{0:T(1024)S(1)}, s32[1024]{0:T(1024)}, u32[]{:S(2)}) copy-start(s32[1024]{0:T(1024)} %param.24) | copy-start | bytes 12292
  34.1 10.0 %copy-start.8 = (f32[1024]{0:T(1024)S(1)}, f32[1024]{0:T(1024)}, u32[]{:S(2)}) copy-start(f32[1024]{0:T(1024)} %param.21) | copy-start | bytes 12292
  44.1 3.7 %copy-start.1 = (bf16[768,512]{1,0:T(8,128)(2,1)S(1)}, bf16[768,512]{1,0:T(8,128)(2,1)}, u32[]{:S(2)}) copy-start(bf16[768,512]{1,0:T(8,128)(2,1)} %refs_20_.3) | copy-start | bytes 2359300
  45.5 8.7 %collective-permute-start.5 = (bf16[256,512]{1,0:T(8,128)(2,1)S(1)}, bf16[256,512]{1,0:T(8,128)(2,1)S(1)}, u32[]{:S(2)}, u32[]{:S(2)}) collective-permute-start(bf16[256,512]{1,0:T(8,128)(2,1)S(1)} %get-tuple-element.23.refs_0_), channel_id=1, source_target_pairs={{0,1},{1,0},{2,3},{3,2},{4,5},{5,4},{6,7},{7,6},{8,9},{9,8},{10,11... | collective-permute-start | bytes 786440 | tf_op jit(solution)/shard_map/ppermute | solution.py:318
  47.2 8.6 %collective-permute-start.7 = (bf16[256,512]{1,0:T(8,128)(2,1)S(1)}, bf16[256,512]{1,0:T(8,128)(2,1)S(1)}, u32[]{:S(2)}, u32[]{:S(2)}) collective-permute-start(bf16[256,512]{1,0:T(8,128)(2,1)S(1)} %get-tuple-element.23.refs_0_), channel_id=1, source_target_pairs={{1,2},{2,1},{5,6},{6,5},{9,10},{10,9},{13,14},{14,13},{17,18},{18,... | collective-permute-start | bytes 786440 | tf_op jit(solution)/shard_map/ppermute | solution.py:348
  47.9 20.5 %collective-permute-start.25 = (bf16[768,512]{1,0:T(8,128)(2,1)S(1)}, bf16[768,512]{1,0:T(8,128)(2,1)S(1)}, u32[]{:S(2)}, u32[]{:S(2)}) collective-permute-start(bf16[768,512]{1,0:T(8,128)(2,1)S(1)} %copy-done.1), channel_id=1, source_target_pairs={{0,16},{4,20},{8,24},{12,28},{16,0},{20,4},{24,8},{28,12},{1,17},{... | collective-permute-start | bytes 2359304 | tf_op jit(solution)/shard_map/ppermute | solution.py:318
  48.5 36.0 %collective-permute-start.18 = (bf16[512,768]{1,0:T(8,128)(2,1)S(1)}, bf16[512,768]{1,0:T(8,128)(2,1)S(1)}, u32[]{:S(2)}, u32[]{:S(2)}) collective-permute-start(bf16[512,768]{1,0:T(8,128)(2,1)S(1)} %copy-done), channel_id=1, source_target_pairs={{0,16},{4,20},{8,24},{12,28},{16,0},{20,4},{24,8},{28,12},{1,17},{... | collective-permute-start | bytes 2359304 | tf_op jit(solution)/shard_map/ppermute | solution.py:318
  54.3 30.8 %collective-permute-start.23 = (bf16[768,512]{1,0:T(8,128)(2,1)S(1)}, bf16[768,512]{1,0:T(8,128)(2,1)S(1)}, u32[]{:S(2)}, u32[]{:S(2)}) collective-permute-start(bf16[768,512]{1,0:T(8,128)(2,1)S(1)} %copy-done.1), channel_id=1, source_target_pairs={{0,8},{4,12},{8,0},{12,4},{16,24},{20,28},{24,16},{28,20},{1,9},{5... | collective-permute-start | bytes 2359304 | tf_op jit(solution)/shard_map/ppermute | solution.py:318
  55.8 29.9 %collective-permute-start.15 = (bf16[512,768]{1,0:T(8,128)(2,1)S(1)}, bf16[512,768]{1,0:T(8,128)(2,1)S(1)}, u32[]{:S(2)}, u32[]{:S(2)}) collective-permute-start(bf16[512,768]{1,0:T(8,128)(2,1)S(1)} %copy-done), channel_id=1, source_target_pairs={{0,4},{4,0},{8,12},{12,8},{16,20},{20,16},{24,28},{28,24},{1,5},{5... | collective-permute-start | bytes 2359304 | tf_op jit(solution)/shard_map/ppermute | solution.py:318
  55.8 31.2 %collective-permute-start.22 = (bf16[768,512]{1,0:T(8,128)(2,1)S(1)}, bf16[768,512]{1,0:T(8,128)(2,1)S(1)}, u32[]{:S(2)}, u32[]{:S(2)}) collective-permute-start(bf16[768,512]{1,0:T(8,128)(2,1)S(1)} %copy-done.1), channel_id=1, source_target_pairs={{0,4},{4,0},{8,12},{12,8},{16,20},{20,16},{24,28},{28,24},{1,5},{5... | collective-permute-start | bytes 2359304 | tf_op jit(solution)/shard_map/ppermute | solution.py:318
  68.4 19.4 %collective-permute-start.10 = (bf16[256,512]{1,0:T(8,128)(2,1)S(1)}, bf16[256,512]{1,0:T(8,128)(2,1)S(1)}, u32[]{:S(2)}, u32[]{:S(2)}) collective-permute-start(bf16[256,512]{1,0:T(8,128)(2,1)S(1)} %get-tuple-element.24.refs_6_), channel_id=1, source_target_pairs={{0,1},{1,0},{2,3},{3,2},{4,5},{5,4},{6,7},{7,6},{8,9},{9,8},{10,11... | collective-permute-start | bytes 786440 | tf_op jit(solution)/shard_map/ppermute | solution.py:318
  84.4 4.8 %collective-permute-start.12 = (bf16[256,512]{1,0:T(8,128)(2,1)S(1)}, bf16[256,512]{1,0:T(8,128)(2,1)S(1)}, u32[]{:S(2)}, u32[]{:S(2)}) collective-permute-start(bf16[256,512]{1,0:T(8,128)(2,1)S(1)} %get-tuple-element.24.refs_6_), channel_id=1, source_target_pairs={{1,2},{2,1},{5,6},{6,5},{9,10},{10,9},{13,14},{14,13},{17,18},{18,... | collective-permute-start | bytes 786440 | tf_op jit(solution)/shard_map/ppermute | solution.py:348
  85.1 4.1 %collective-permute-start.6 = (bf16[256,512]{1,0:T(8,128)(2,1)S(1)}, bf16[256,512]{1,0:T(8,128)(2,1)S(1)}, u32[]{:S(2)}, u32[]{:S(2)}) collective-permute-start(bf16[256,512]{1,0:T(8,128)(2,1)S(1)} %collective-permute-done.5.refs_1_), channel_id=1, source_target_pairs={{1,2},{2,1},{5,6},{6,5},{9,10},{10,9},{13,14},{14,13},{17,18},{18,... | collective-permute-start | bytes 786440 | tf_op jit(solution)/shard_map/ppermute | solution.py:349
  85.8 14.9 %collective-permute-start.8 = (bf16[256,512]{1,0:T(8,128)(2,1)S(1)}, bf16[256,512]{1,0:T(8,128)(2,1)S(1)}, u32[]{:S(2)}, u32[]{:S(2)}) collective-permute-start(bf16[256,512]{1,0:T(8,128)(2,1)S(1)} %collective-permute-done.7.refs_4_), channel_id=1, source_target_pairs={{1,0},{2,3},{5,4},{6,7},{9,8},{10,11},{13,12},{14,15},{17,16},{18,... | collective-permute-start | bytes 786440 | tf_op jit(solution)/shard_map/ppermute | solution.py:350
  87.1 36.0 %collective-permute-start.20 = (bf16[512,768]{1,0:T(8,128)(2,1)S(1)}, bf16[512,768]{1,0:T(8,128)(2,1)S(1)}, u32[]{:S(2)}, u32[]{:S(2)}) collective-permute-start(bf16[512,768]{1,0:T(8,128)(2,1)S(1)} %collective-permute-done.16.refs_14_), channel_id=1, source_target_pairs={{0,16},{4,20},{8,24},{12,28},{16,0},{20,4},{24,8},{28,12},{1,17},{... | collective-permute-start | bytes 2359304 | tf_op jit(solution)/shard_map/ppermute | solution.py:318
  87.7 35.8 %collective-permute-start.27 = (bf16[768,512]{1,0:T(8,128)(2,1)S(1)}, bf16[768,512]{1,0:T(8,128)(2,1)S(1)}, u32[]{:S(2)}, u32[]{:S(2)}) collective-permute-start(bf16[768,512]{1,0:T(8,128)(2,1)S(1)} %collective-permute-done.25.refs_24_), channel_id=1, source_target_pairs={{0,8},{4,12},{8,0},{12,4},{16,24},{20,28},{24,16},{28,20},{1,9},{5... | collective-permute-start | bytes 2359304 | tf_op jit(solution)/shard_map/ppermute | solution.py:318
  89.2 34.5 %collective-permute-start.17 = (bf16[512,768]{1,0:T(8,128)(2,1)S(1)}, bf16[512,768]{1,0:T(8,128)(2,1)S(1)}, u32[]{:S(2)}, u32[]{:S(2)}) collective-permute-start(bf16[512,768]{1,0:T(8,128)(2,1)S(1)} %collective-permute-done.16.refs_14_), channel_id=1, source_target_pairs={{0,4},{4,0},{8,12},{12,8},{16,20},{20,16},{24,28},{28,24},{1,5},{5... | collective-permute-start | bytes 2359304 | tf_op jit(solution)/shard_map/ppermute | solution.py:318
  89.2 12.8 %collective-permute-start.11 = (bf16[256,512]{1,0:T(8,128)(2,1)S(1)}, bf16[256,512]{1,0:T(8,128)(2,1)S(1)}, u32[]{:S(2)}, u32[]{:S(2)}) collective-permute-start(bf16[256,512]{1,0:T(8,128)(2,1)S(1)} %collective-permute-done.10.refs_7_), channel_id=1, source_target_pairs={{1,2},{2,1},{5,6},{6,5},{9,10},{10,9},{13,14},{14,13},{17,18},{18,... | collective-permute-start | bytes 786440 | tf_op jit(solution)/shard_map/ppermute | solution.py:349
  100.7 11.8 %collective-permute-start.13 = (bf16[256,512]{1,0:T(8,128)(2,1)S(1)}, bf16[256,512]{1,0:T(8,128)(2,1)S(1)}, u32[]{:S(2)}, u32[]{:S(2)}) collective-permute-start(bf16[256,512]{1,0:T(8,128)(2,1)S(1)} %collective-permute-done.12.refs_10_), channel_id=1, source_target_pairs={{1,0},{2,3},{5,4},{6,7},{9,8},{10,11},{13,12},{14,15},{17,16},{18,... | collective-permute-start | bytes 786440 | tf_op jit(solution)/shard_map/ppermute | solution.py:350
  102.0 18.1 %collective-permute-start.9 = (bf16[256,512]{1,0:T(8,128)(2,1)S(1)}, bf16[256,512]{1,0:T(8,128)(2,1)S(1)}, u32[]{:S(2)}, u32[]{:S(2)}) collective-permute-start(bf16[256,512]{1,0:T(8,128)(2,1)S(1)} %collective-permute-done.6.refs_2_), channel_id=1, source_target_pairs={{1,0},{2,3},{5,4},{6,7},{9,8},{10,11},{13,12},{14,15},{17,16},{18,... | collective-permute-start | bytes 786440 | tf_op jit(solution)/shard_map/ppermute | solution.py:351
  112.5 10.6 %collective-permute-start.14 = (bf16[256,512]{1,0:T(8,128)(2,1)S(1)}, bf16[256,512]{1,0:T(8,128)(2,1)S(1)}, u32[]{:S(2)}, u32[]{:S(2)}) collective-permute-start(bf16[256,512]{1,0:T(8,128)(2,1)S(1)} %collective-permute-done.11.refs_8_), channel_id=1, source_target_pairs={{1,0},{2,3},{5,4},{6,7},{9,8},{10,11},{13,12},{14,15},{17,16},{18,... | collective-permute-start | bytes 786440 | tf_op jit(solution)/shard_map/ppermute | solution.py:351
  120.1 4.0 %collective-permute-start.26 = (bf16[768,512]{1,0:T(8,128)(2,1)S(1)}, bf16[768,512]{1,0:T(8,128)(2,1)S(1)}, u32[]{:S(2)}, u32[]{:S(2)}) collective-permute-start(bf16[768,512]{1,0:T(8,128)(2,1)S(1)} %collective-permute-done.25.refs_24_), channel_id=1, source_target_pairs={{0,4},{4,0},{8,12},{12,8},{16,20},{20,16},{24,28},{28,24},{1,5},{5... | collective-permute-start | bytes 2359304 | tf_op jit(solution)/shard_map/ppermute | solution.py:318
  123.0 2.3 %collective-permute-start.19 = (bf16[512,768]{1,0:T(8,128)(2,1)S(1)}, bf16[512,768]{1,0:T(8,128)(2,1)S(1)}, u32[]{:S(2)}, u32[]{:S(2)}) collective-permute-start(bf16[512,768]{1,0:T(8,128)(2,1)S(1)} %collective-permute-done.18.refs_16_), channel_id=1, source_target_pairs={{0,4},{4,0},{8,12},{12,8},{16,20},{20,16},{24,28},{28,24},{1,5},{5... | collective-permute-start | bytes 2359304 | tf_op jit(solution)/shard_map/ppermute | solution.py:318
  123.0 3.4 %collective-permute-start.24 = (bf16[768,512]{1,0:T(8,128)(2,1)S(1)}, bf16[768,512]{1,0:T(8,128)(2,1)S(1)}, u32[]{:S(2)}, u32[]{:S(2)}) collective-permute-start(bf16[768,512]{1,0:T(8,128)(2,1)S(1)} %collective-permute-done.23.refs_22_), channel_id=1, source_target_pairs={{0,4},{4,0},{8,12},{12,8},{16,20},{20,16},{24,28},{28,24},{1,5},{5... | collective-permute-start | bytes 2359304 | tf_op jit(solution)/shard_map/ppermute | solution.py:318
  123.6 4.0 %collective-permute-start.21 = (bf16[512,768]{1,0:T(8,128)(2,1)S(1)}, bf16[512,768]{1,0:T(8,128)(2,1)S(1)}, u32[]{:S(2)}, u32[]{:S(2)}) collective-permute-start(bf16[512,768]{1,0:T(8,128)(2,1)S(1)} %collective-permute-done.20.refs_18_), channel_id=1, source_target_pairs={{0,4},{4,0},{8,12},{12,8},{16,20},{20,16},{24,28},{28,24},{1,5},{5... | collective-permute-start | bytes 2359304 | tf_op jit(solution)/shard_map/ppermute | solution.py:318
  123.6 5.1 %collective-permute-start.28 = (bf16[768,512]{1,0:T(8,128)(2,1)S(1)}, bf16[768,512]{1,0:T(8,128)(2,1)S(1)}, u32[]{:S(2)}, u32[]{:S(2)}) collective-permute-start(bf16[768,512]{1,0:T(8,128)(2,1)S(1)} %collective-permute-done.27.refs_26_), channel_id=1, source_target_pairs={{0,4},{4,0},{8,12},{12,8},{16,20},{20,16},{24,28},{28,24},{1,5},{5... | collective-permute-start | bytes 2359304 | tf_op jit(solution)/shard_map/ppermute | solution.py:318
  131.4 8.1 %collective-permute-start.36 = (bf16[128,1024]{1,0:T(8,128)(2,1)S(1)}, bf16[128,1024]{1,0:T(8,128)(2,1)S(1)}, u32[]{:S(2)}, u32[]{:S(2)}) collective-permute-start(bf16[128,1024]{1,0:T(8,128)(2,1)S(1)} %get-tuple-element.30), channel_id=1, source_target_pairs={{0,1},{3,2},{4,5},{7,6},{8,9},{11,10},{12,13},{15,14},{16,17},{19,... | collective-permute-start | bytes 786440 | tf_op jit(solution)/shard_map/ppermute | solution.py:362
  135.5 9.6 %collective-permute-start.31 = (bf16[128,1024]{1,0:T(8,128)(2,1)S(1)}, bf16[128,1024]{1,0:T(8,128)(2,1)S(1)}, u32[]{:S(2)}, u32[]{:S(2)}) collective-permute-start(bf16[128,1024]{1,0:T(8,128)(2,1)S(1)} %get-tuple-element.26), channel_id=1, source_target_pairs={{0,1},{3,2},{4,5},{7,6},{8,9},{11,10},{12,13},{15,14},{16,17},{19,... | collective-permute-start | bytes 786440 | tf_op jit(solution)/shard_map/ppermute | solution.py:362
  136.8 13.9 %collective-permute-start.34 = (bf16[128,1024]{1,0:T(8,128)(2,1)S(1)}, bf16[128,1024]{1,0:T(8,128)(2,1)S(1)}, u32[]{:S(2)}, u32[]{:S(2)}) collective-permute-start(bf16[128,1024]{1,0:T(8,128)(2,1)S(1)} %get-tuple-element.31), channel_id=1, source_target_pairs={{0,1},{3,2},{4,5},{7,6},{8,9},{11,10},{12,13},{15,14},{16,17},{19,... | collective-permute-start | bytes 786440 | tf_op jit(solution)/shard_map/ppermute | solution.py:363
  138.2 17.5 %collective-permute-start.29 = (bf16[128,1024]{1,0:T(8,128)(2,1)S(1)}, bf16[128,1024]{1,0:T(8,128)(2,1)S(1)}, u32[]{:S(2)}, u32[]{:S(2)}) collective-permute-start(bf16[128,1024]{1,0:T(8,128)(2,1)S(1)} %get-tuple-element.27), channel_id=1, source_target_pairs={{0,1},{3,2},{4,5},{7,6},{8,9},{11,10},{12,13},{15,14},{16,17},{19,... | collective-permute-start | bytes 786440 | tf_op jit(solution)/shard_map/ppermute | solution.py:363
  139.6 29.0 %copy-start.9 = (f32[1024]{0:T(1024)S(1)}, f32[1024]{0:T(1024)}, u32[]{:S(2)}) copy-start(f32[1024]{0:T(1024)} %param.25) | copy-start | bytes 12292
  139.6 21.9 %collective-permute-start.37 = (bf16[128,1024]{1,0:T(8,128)(2,1)S(1)}, bf16[128,1024]{1,0:T(8,128)(2,1)S(1)}, u32[]{:S(2)}, u32[]{:S(2)}) collective-permute-start(bf16[128,1024]{1,0:T(8,128)(2,1)S(1)} %add_convert_fusion.1), channel_id=1, source_target_pairs={{1,2},{2,1},{5,6},{6,5},{9,10},{10,9},{13,14},{14,13},{17,18},{18,... | collective-permute-start | bytes 786440 | tf_op jit(solution)/shard_map/ppermute | solution.py:364
  145.2 11.2 %collective-permute-start.32 = (bf16[128,1024]{1,0:T(8,128)(2,1)S(1)}, bf16[128,1024]{1,0:T(8,128)(2,1)S(1)}, u32[]{:S(2)}, u32[]{:S(2)}) collective-permute-start(bf16[128,1024]{1,0:T(8,128)(2,1)S(1)} %add_convert_fusion.4), channel_id=1, source_target_pairs={{1,2},{2,1},{5,6},{6,5},{9,10},{10,9},{13,14},{14,13},{17,18},{18,... | collective-permute-start | bytes 786440 | tf_op jit(solution)/shard_map/ppermute | solution.py:364
  150.8 19.5 %collective-permute-start.35 = (bf16[128,1024]{1,0:T(8,128)(2,1)S(1)}, bf16[128,1024]{1,0:T(8,128)(2,1)S(1)}, u32[]{:S(2)}, u32[]{:S(2)}) collective-permute-start(bf16[128,1024]{1,0:T(8,128)(2,1)S(1)} %add_convert_fusion.2), channel_id=1, source_target_pairs={{1,2},{2,1},{5,6},{6,5},{9,10},{10,9},{13,14},{14,13},{17,18},{18,... | collective-permute-start | bytes 786440 | tf_op jit(solution)/shard_map/ppermute | solution.py:365
  155.7 5.9 %collective-permute-start.30 = (bf16[128,1024]{1,0:T(8,128)(2,1)S(1)}, bf16[128,1024]{1,0:T(8,128)(2,1)S(1)}, u32[]{:S(2)}, u32[]{:S(2)}) collective-permute-start(bf16[128,1024]{1,0:T(8,128)(2,1)S(1)} %add_convert_fusion.5), channel_id=1, source_target_pairs={{1,2},{2,1},{5,6},{6,5},{9,10},{10,9},{13,14},{14,13},{17,18},{18,... | collective-permute-start | bytes 786440 | tf_op jit(solution)/shard_map/ppermute | solution.py:365
  156.5 12.1 %collective-permute-start.33 = (bf16[128,1024]{1,0:T(8,128)(2,1)S(1)}, bf16[128,1024]{1,0:T(8,128)(2,1)S(1)}, u32[]{:S(2)}, u32[]{:S(2)}) collective-permute-start(bf16[128,1024]{1,0:T(8,128)(2,1)S(1)} %add_convert_fusion.3), channel_id=1, source_target_pairs={{0,1},{1,0},{2,3},{3,2},{4,5},{5,4},{6,7},{7,6},{8,9},{9,8},{10,11... | collective-permute-start | bytes 786440 | tf_op jit(solution)/shard_map/ppermute | solution.py:318
  161.5 11.1 %collective-permute-start.38 = (bf16[128,1024]{1,0:T(8,128)(2,1)S(1)}, bf16[128,1024]{1,0:T(8,128)(2,1)S(1)}, u32[]{:S(2)}, u32[]{:S(2)}) collective-permute-start(bf16[128,1024]{1,0:T(8,128)(2,1)S(1)} %add_convert_fusion), channel_id=1, source_target_pairs={{0,1},{1,0},{2,3},{3,2},{4,5},{5,4},{6,7},{7,6},{8,9},{9,8},{10,11... | collective-permute-start | bytes 786440 | tf_op jit(solution)/shard_map/ppermute | solution.py:318
